TPU v7x, 32 devices: a whole 2x2x4 slice. The times are simulated.
32 devices in a mesh: expert: 8 (over z, y), wshard: 4 (over x, core).
Axes of the slice: x: 2, y: 2, z: 4, core: 2. Of those that a mesh axis runs over, the one named last changes fastest.
Arguments:
- tokens: bfloat16 [16384, 1024], P(('expert', 'wshard')), may hold values from -6 to 6
- norm1_gain: bfloat16 [1024], P('wshard'), may hold values from 0.5 to 1.5
- norm1_shift: bfloat16 [1024], P('wshard'), may hold values from -1 to 1
- w_qkv: bfloat16 [1024, 3072], P('wshard'), may hold values from -0.1875 to 0.1875
- w_out: bfloat16 [1024, 1024], P('wshard'), may hold values from -3 to 3
- norm2_gain: bfloat16 [1024], P('wshard'), may hold values from 0.5 to 1.5
- norm2_shift: bfloat16 [1024], P('wshard'), may hold values from -1 to 1
- w_router: bfloat16 [1024, 16], P('wshard'), may hold values from -0.09375 to 0.09375
- w_up: bfloat16 [16, 1024, 4096], P('expert', None, 'wshard'), may hold values from -0.1875 to 0.1875
- w_down: bfloat16 [16, 4096, 1024], P('expert', 'wshard'), may hold values from -3 to 3
- routes: int32 [16384, 1], P(('expert', 'wshard')), may hold values from 0 to 15
- priority: int32 [32, 512], P(('expert', 'wshard')), may hold values from 0 to 511, each once within a row
- prefix: int32 [32], P(('expert', 'wshard')), may hold values from 51 to 256
- cotangent: bfloat16 [16384, 1024], P(('expert', 'wshard')), may hold values from -6 to 6
Outputs:
- output: bfloat16 [16384, 1024], P(('expert', 'wshard'))
- grad_tokens: float32 [16384, 1024], P(('expert', 'wshard'))
- grad_norm1_gain: float32 [1024], P('wshard')
- grad_norm1_shift: float32 [1024], P('wshard')
- grad_w_qkv: float32 [1024, 3072], P('wshard')
- grad_w_out: float32 [1024, 1024], P('wshard')
- grad_norm2_gain: float32 [1024], P('wshard')
- grad_norm2_shift: float32 [1024], P('wshard')
- grad_router: float32 [1024, 16], P('wshard')
- grad_up: float32 [16, 1024, 4096], P('expert', None, 'wshard')
- grad_down: float32 [16, 4096, 1024], P('expert', 'wshard')
Inputs may be any that keep to these rules, and one draw needn't show every extreme that they name: `routes`: each token names one expert; every expert is named by some token. `priority`: each row orders the 512 tokens of one sequence, each number once.
All inputs are finite; a program needn't handle non-finite values.
Results may differ from a plain program's by a relative error of at most 0.02.
Values may be sent and summed in bfloat16 or wider, within the bound.
A program may use at most 256 MiB of HBM per device.

v0:
```python
import functools
import math

import jax
import jax.numpy as jnp
from jax import lax
from jax.experimental import pallas as pl
from jax.experimental.pallas import tpu as pltpu
from jax.sharding import PartitionSpec as P

HEADS = 16
HEAD_DIM = 64


epsilon = 1e-05
VMEM_LIMIT = 66_000_000


def normalize(values, gain_vec, shift_vec):
    row_mean = jnp.mean(values, axis=-1, keepdims=True)
    centered = values - row_mean
    inverse = lax.rsqrt(jnp.mean(centered * centered, axis=-1, keepdims=True) + epsilon)
    scaled = centered * inverse
    return (scaled * gain_vec + shift_vec, scaled, inverse)


def norm_back(grad_rows, scaled, inverse, gain_vec):
    weighted = grad_rows * gain_vec
    mean_one = jnp.mean(weighted, axis=-1, keepdims=True)
    mean_two = jnp.mean(weighted * scaled, axis=-1, keepdims=True)
    grad_inputs = inverse * (weighted - mean_one - scaled * mean_two)
    return (grad_inputs, jnp.sum(grad_rows * scaled, axis=0), jnp.sum(grad_rows, axis=0))


def contract_rows(left, right):
    return lax.dot_general(
        left, right, (((0,), (0,)), ((), ())), preferred_element_type=jnp.float32
    )


def times_transpose(left, right):
    return lax.dot_general(
        left, right, (((1,), (1,)), ((), ())), preferred_element_type=jnp.float32
    )


def gelu_tanh(values):
    return jax.nn.gelu(values, approximate=True)


def assign_slots(route_ids, order_ids, expert_count, capacity):
    token_count = route_ids.shape[0]
    same_expert = route_ids[:, None] == route_ids[None, :]
    earlier = order_ids[None, :] < order_ids[:, None]
    rank_ids = jnp.sum((same_expert & earlier).astype(jnp.int32), axis=1)
    is_kept = rank_ids < capacity
    slot_index = jnp.where(is_kept, route_ids * capacity + rank_ids, expert_count * capacity)
    slot_ids = jnp.arange(expert_count * capacity, dtype=jnp.int32)
    match_table = slot_index[None, :] == slot_ids[:, None]
    token_ids = jnp.arange(token_count, dtype=jnp.int32)
    filled = jnp.any(match_table, axis=1)
    picked = jnp.sum(jnp.where(match_table, token_ids[None, :], 0), axis=1)
    slot_source = jnp.where(filled, picked, token_count)
    return (slot_index, slot_source)


def group_heads(values, groups):
    token_count = values.shape[0]
    return jnp.transpose(values.reshape(token_count, groups, -1, HEAD_DIM), (1, 0, 2, 3))


def block_scores(query_block, key_group, block_start, prefix_len):
    block_rows = query_block.shape[0]
    key_count = key_group.shape[0]
    scores = jnp.einsum(
        "qgd,kgd->gqk", query_block, key_group, preferred_element_type=jnp.float32
    ) * (1.0 / math.sqrt(HEAD_DIM))
    query_pos = block_start + jnp.arange(block_rows, dtype=jnp.int32)
    key_pos = jnp.arange(key_count, dtype=jnp.int32)
    allowed = (key_pos[None, :] <= query_pos[:, None]) | (key_pos[None, :] < prefix_len)
    return jnp.where(allowed[None], scores, -1e30)


def attend_forward(query_heads, key_heads, value_heads, prefix_len):
    token_count = query_heads.shape[0]
    group_size = min(4, HEADS)
    groups = HEADS // group_size
    block_rows = min(512, token_count)
    blocks = token_count // block_rows
    starts = jnp.arange(blocks, dtype=jnp.int32) * block_rows

    def one_group(group_item):
        query_group, key_group, value_group = group_item
        query_blocks = query_group.reshape(blocks, block_rows, group_size, HEAD_DIM)

        def one_block(block_item):
            query_block, block_start = block_item
            scores = block_scores(query_block, key_group, block_start, prefix_len)
            row_max = jnp.max(scores, axis=-1, keepdims=True)
            exponent = jnp.exp(scores - row_max)
            row_total = jnp.sum(exponent, axis=-1, keepdims=True)
            attn_probs = (exponent / row_total).astype(jnp.bfloat16)
            result = jnp.einsum(
                "gqk,kgd->qgd", attn_probs, value_group, preferred_element_type=jnp.float32
            )
            return (result, (row_max + jnp.log(row_total))[..., 0])

        return lax.map(one_block, (query_blocks, starts))

    attended, log_totals = lax.map(
        one_group,
        (
            group_heads(query_heads, groups),
            group_heads(key_heads, groups),
            group_heads(value_heads, groups),
        ),
    )
    merged = (
        jnp.transpose(attended, (1, 2, 0, 3, 4))
        .reshape(token_count, HEADS * HEAD_DIM)
        .astype(jnp.bfloat16)
    )
    return (merged, log_totals)


def attend_backward(query_heads, key_heads, value_heads, grad_merged, log_totals, prefix_len):
    token_count = query_heads.shape[0]
    group_size = min(4, HEADS)
    groups = HEADS // group_size
    block_rows = min(512, token_count)
    blocks = token_count // block_rows
    starts = jnp.arange(blocks, dtype=jnp.int32) * block_rows
    score_scale = 1.0 / math.sqrt(HEAD_DIM)

    def one_group(group_item):
        query_group, key_group, value_group, grad_group, total_group = group_item
        query_blocks = query_group.reshape(blocks, block_rows, group_size, HEAD_DIM)
        grad_blocks = grad_group.reshape(blocks, block_rows, group_size, HEAD_DIM)

        def one_block(carry, block_item):
            grad_keys, grad_vals = carry
            query_block, grad_block, total_block, block_start = block_item
            scores = block_scores(query_block, key_group, block_start, prefix_len)
            attn_probs = jnp.exp(scores - total_block[..., None])
            grad_probs = jnp.einsum(
                "qgd,kgd->gqk", grad_block, value_group, preferred_element_type=jnp.float32
            )
            row_delta = jnp.sum(attn_probs * grad_probs, axis=-1, keepdims=True)
            grad_scores = (attn_probs * (grad_probs - row_delta)).astype(jnp.bfloat16)
            grad_vals = grad_vals + jnp.einsum(
                "gqk,qgd->kgd",
                attn_probs.astype(jnp.bfloat16),
                grad_block,
                preferred_element_type=jnp.float32,
            )
            grad_keys = (
                grad_keys
                + jnp.einsum(
                    "gqk,qgd->kgd", grad_scores, query_block, preferred_element_type=jnp.float32
                )
                * score_scale
            )
            grad_query = (
                jnp.einsum(
                    "gqk,kgd->qgd", grad_scores, key_group, preferred_element_type=jnp.float32
                )
                * score_scale
            )
            return ((grad_keys, grad_vals), grad_query)

        zero_keys = jnp.zeros(key_group.shape, jnp.float32)
        carried, grad_queries = lax.scan(
            one_block, (zero_keys, zero_keys), (query_blocks, grad_blocks, total_group, starts)
        )
        return (grad_queries, carried[0], carried[1])

    grad_queries, grad_keys, grad_vals = lax.map(
        one_group,
        (
            group_heads(query_heads, groups),
            group_heads(key_heads, groups),
            group_heads(value_heads, groups),
            group_heads(grad_merged, groups),
            log_totals,
        ),
    )
    query_part = jnp.transpose(grad_queries, (1, 2, 0, 3, 4)).reshape(token_count, HEADS * HEAD_DIM)
    key_part = jnp.transpose(grad_keys, (1, 0, 2, 3)).reshape(token_count, HEADS * HEAD_DIM)
    value_part = jnp.transpose(grad_vals, (1, 0, 2, 3)).reshape(token_count, HEADS * HEAD_DIM)
    return jnp.concatenate([query_part, key_part, value_part], axis=1).astype(jnp.bfloat16)


MESH = pl.DeviceIdType.MESH
LANES = 128


def dot_nn(left, right):
    return lax.dot_general(
        left, right, (((1,), (0,)), ((), ())), preferred_element_type=jnp.float32
    )


def dot_nt(left, right):
    return lax.dot_general(
        left, right, (((1,), (1,)), ((), ())), preferred_element_type=jnp.float32
    )


def dot_tn(left, right):
    return lax.dot_general(
        left, right, (((0,), (0,)), ((), ())), preferred_element_type=jnp.float32
    )


def span(start, size):
    return pl.ds(pl.multiple_of(start, size), size)


def every(start, stop, step):
    def body(i, carry):
        step(i)
        return carry

    lax.fori_loop(start, stop, body, 0)


class Place:
    def __init__(self, owners):
        self.owners = owners
        self.e = lax.axis_index("expert")
        self.w = lax.axis_index("wshard")
        self.c = lax.rem(self.w, 2)
        self.x = lax.div(self.w, 2)
        self.sib = self.w + 1 - 2 * self.c
        self.far = lax.rem(self.w + 2, 4)
        self.diag = 3 - self.w
        self.pair = self.e + 1 - 2 * lax.rem(self.e, 2)

    def ahead(self, k):
        return lax.rem(self.e + k, self.owners)

    def behind(self, k):
        return lax.rem(self.e + self.owners - k, self.owners)


def remote(src, dst, send, recv, device):
    return pltpu.make_async_remote_copy(
        src_ref=src,
        dst_ref=dst,
        send_sem=send,
        recv_sem=recv,
        device_id=device,
        device_id_type=MESH,
    )


def greet(peers):
    barrier = pltpu.get_barrier_semaphore()
    for peer in peers:
        pl.semaphore_signal(barrier, inc=1, device_id=peer, device_id_type=MESH)
    pl.semaphore_wait(barrier, len(peers))


class Dispatch:
    def __init__(self, place, capacity, send_ref, rows_ref, sems):
        self.p, self.cap, self.src, self.rows = place, capacity, send_ref, rows_ref
        self.own_sem, self.send, self.recv = sems

    def slice(self, k, core, side):
        start = (((lax.div(k, 2) * 2 + core) * 2 + side) * 2 + lax.rem(k, 2)) * self.cap
        return self.rows.at[:, span(start, self.cap)]

    def own(self):
        return pltpu.make_async_copy(
            self.src.at[self.p.e], self.slice(0, self.p.c, self.p.x), self.own_sem
        )

    def direct(self, k):
        return remote(
            self.src.at[self.p.ahead(k)],
            self.slice(k, self.p.c, self.p.x),
            self.send.at[0, k],
            self.recv.at[0, k],
            (self.p.ahead(k), self.p.w),
        )

    def hop(self, k, side, which, peer):
        part = self.slice(k, self.p.c, side)
        return remote(
            part, part, self.send.at[which, k], self.recv.at[which, k], (self.p.e, peer)
        )

    def to_sib(self, k):
        return self.hop(k, self.p.x, 1, self.p.sib)

    def to_far(self, k):
        return self.hop(k, self.p.x, 2, self.p.far)

    def relayed(self, k):
        return self.hop(k, 1 - self.p.x, 3, self.p.sib)

    def start(self):
        self.own().start()
        every(1, self.p.owners, lambda k: self.direct(k).start())

    def forward(self, k):
        k = jnp.int32(k)

        @pl.when(k == 0)
        def _():
            self.own().wait()

        @pl.when(k > 0)
        def _():
            self.direct(k).wait_recv()

        self.to_far(k).start()
        self.to_sib(k).start()

    def relay(self, k):
        self.to_far(k).wait_recv()
        self.relayed(k).start()

    def ready(self, k):
        self.to_sib(k).wait_recv()
        self.relayed(k).wait_recv()

    def drain(self):
        every(1, self.p.owners, lambda k: self.direct(k).wait_send())

        def rest(k):
            self.to_sib(k).wait_send()
            self.to_far(k).wait_send()
            self.relayed(k).wait_send()

        every(0, self.p.owners, rest)


class Return:
    def __init__(self, place, capacity, experts, part, got, mid, far, done, home, sems):
        self.p, self.cap, self.experts = place, capacity, experts
        self.part, self.got, self.mid, self.far, self.done, self.home = (
            part, got, mid, far, done, home,
        )
        self.own_sem, self.send, self.recv, self.home_send, self.home_recv = sems
        self.swapped, self.crossed, self.homed = {}, {}, {}

    def swap(self, j):
        size = 4 * self.cap
        self.swapped[j] = remote(
            self.part.at[:, span((j * 2 + 1 - self.p.c) * size, size)],
            self.got.at[:, span(j * size, size)],
            self.send.at[0, j],
            self.recv.at[0, j],
            (self.p.e, self.p.sib),
        )
        self.swapped[j].start()

    def pair_sum(self, expert, j, side):
        size = 2 * self.cap
        mine = self.part[expert, span(((j * 2 + self.p.c) * 2 + side) * size, size), :]
        theirs = self.got[expert, span((j * 2 + side) * size, size), :]
        return mine.astype(jnp.float32) + theirs.astype(jnp.float32)

    def cross(self, j):
        self.swapped[j].wait_recv()
        size = 2 * self.cap
        for expert in range(self.experts):
            self.mid[expert, pl.ds(j * size, size), :] = self.pair_sum(
                expert, j, 1 - self.p.x
            ).astype(jnp.bfloat16)
        part = pl.ds(j * size, size)
        self.crossed[j] = remote(
            self.mid.at[:, part],
            self.far.at[:, part],
            self.send.at[1, j],
            self.recv.at[1, j],
            (self.p.e, self.p.far),
        )
        self.crossed[j].start()

    def finish(self, j):
        self.crossed[j].wait_recv()
        size = 2 * self.cap
        for expert in range(self.experts):
            total = self.pair_sum(expert, j, self.p.x) + self.far[
                expert, pl.ds(j * size, size), :
            ].astype(jnp.float32)
            total = total.astype(jnp.bfloat16)
            self.done[2 * j, expert] = total[: self.cap]
            self.done[2 * j + 1, expert] = total[self.cap :]
        for k in (2 * j, 2 * j + 1):
            if k == 0:
                copy = pltpu.make_async_copy(
                    self.done.at[0], self.home.at[self.p.e], self.own_sem
                )
            else:
                copy = remote(
                    self.done.at[k],
                    self.home.at[self.p.e],
                    self.home_send.at[k],
                    self.home_recv.at[k],
                    (self.p.behind(k), self.p.w),
                )
            copy.start()
            self.homed[k] = copy

    def drain(self):
        for group in (self.swapped, self.crossed):
            for copy in group.values():
                copy.wait_send()
        for k, copy in self.homed.items():
            copy.wait()


def gelu_pair(v):
    root = math.sqrt(2.0 / math.pi)
    square = v * v
    t = jnp.tanh(v * (root + (root * 0.044715) * square))
    half = 0.5 + 0.5 * t
    slope = half + (half * (1.0 - t)) * (v * (root + (3.0 * root * 0.044715) * square))
    return v * half, slope


def expert_kernel(
    dims,
    send_ref, grads_hbm, up_hbm, down_hbm, router_ref,
    home_out, home_grad, rows_out, scaled_out, hidden_out, pre_out, router_grad,
    rows, grads, scaled, hidden, pre, up, down,
    part_out, part_grad, got_out, got_grad, mid_out, mid_grad,
    far_out, far_grad, done_out, done_grad,
    load_sem, own_sem, disp_send, disp_recv, red_send, red_recv, home_send, home_recv,
):
    owners, experts, capacity, width, units, expert_count = dims
    place = Place(owners)
    loads = [
        pltpu.make_async_copy(src, dst, load_sem.at[i])
        for i, (src, dst) in enumerate(
            [(up_hbm, up), (grads_hbm, grads), (down_hbm, down)]
        )
    ]
    for load in loads:
        load.start()
    greet(
        [(place.ahead(k), place.w) for k in range(1, owners)]
        + [(place.e, place.sib), (place.e, place.far)]
    )
    dispatch = Dispatch(
        place, capacity, send_ref, rows, (own_sem.at[0], disp_send, disp_recv)
    )
    ret = [
        Return(
            place, capacity, experts, part, got, mid, far, done, home,
            (own_sem.at[1 + i], red_send.at[i], red_recv.at[i], home_send.at[i], home_recv.at[i]),
        )
        for i, (part, got, mid, far, done, home) in enumerate(
            [
                (part_grad, got_grad, mid_grad, far_grad, done_grad, home_grad),
                (part_out, got_out, mid_out, far_out, done_out, home_out),
            ]
        )
    ]
    dispatch.start()
    router_grad[...] = jnp.zeros_like(router_grad)
    tile = min(256, units)
    wide = min(256, width)
    chunks = owners // 2
    size = 8 * capacity
    lane = lax.broadcasted_iota(jnp.int32, (size, LANES), 1)

    def compute(j):
        here = pl.ds(j * size, size)

        def one_expert(expert, carry):
            logits = dot_nn(rows[expert, here, :], router_ref[...])
            logits = jnp.where(lane < expert_count, logits, -1e30)
            exponent = jnp.exp(logits - jnp.max(logits, axis=1, keepdims=True))
            prob = exponent / jnp.sum(exponent, axis=1, keepdims=True)
            mine = lane == place.e * experts + expert
            gate = jnp.sum(jnp.where(mine, prob, 0.0), axis=1, keepdims=True)
            scaled[expert, here, :] = (
                gate * grads[expert, here, :].astype(jnp.float32)
            ).astype(jnp.bfloat16)

            def one_tile(n, carry):
                cols = pl.ds(pl.multiple_of(n * tile, tile), tile)
                value, slope = gelu_pair(dot_nn(rows[expert, here, :], up[expert, :, cols]))
                hidden[expert, here, cols] = value.astype(jnp.bfloat16)
                back = dot_nt(scaled[expert, here, :], down[expert, cols, :])
                pre[expert, here, cols] = (back * slope).astype(jnp.bfloat16)
                return carry

            lax.fori_loop(0, units // tile, one_tile, 0)

            def one_out(n, total):
                cols = pl.ds(pl.multiple_of(n * wide, wide), wide)
                value = dot_nn(hidden[expert, here, :], down[expert, :, cols])
                part_out[expert, here, cols] = (gate * value).astype(jnp.bfloat16)
                weighted = value * grads[expert, here, cols].astype(jnp.float32)
                for start in range(0, wide, LANES):
                    total = total + weighted[:, start : start + LANES]
                return total

            total = lax.fori_loop(
                0, width // wide, one_out, jnp.zeros((size, LANES), jnp.float32)
            )
            grad_gate = jnp.sum(total, axis=1, keepdims=True)
            grad_logits = (
                prob * ((jnp.where(mine, 1.0, 0.0) - gate) * grad_gate)
            ).astype(jnp.bfloat16)

            def one_in(n, carry):
                cols = pl.ds(pl.multiple_of(n * wide, wide), wide)
                value = dot_nt(pre[expert, here, :], up[expert, cols, :]) + dot_nt(
                    grad_logits, router_ref[cols, :]
                )
                part_grad[expert, here, cols] = value.astype(jnp.bfloat16)
                router_grad[:, cols] += dot_tn(grad_logits, rows[expert, here, cols])
                return carry

            lax.fori_loop(0, width // wide, one_in, 0)
            return carry

        lax.fori_loop(0, experts, one_expert, 0)

    for k in (0, 1):
        dispatch.forward(k)
    for j in range(chunks):
        if j + 1 < chunks:
            for k in (2 * j + 2, 2 * j + 3):
                dispatch.forward(k)
        for k in (2 * j, 2 * j + 1):
            dispatch.relay(k)
        for k in (2 * j, 2 * j + 1):
            dispatch.ready(k)
        if j == 0:
            for load in loads:
                load.wait()
        compute(j)
        ret[0].swap(j)
        ret[1].swap(j)
        if j >= 1:
            ret[0].cross(j - 1)
        if j >= 2:
            ret[0].finish(j - 2)
    ret[0].cross(chunks - 1)
    stores = [
        pltpu.make_async_copy(src, dst, load_sem.at[i])
        for i, (src, dst) in enumerate(
            [(rows, rows_out), (scaled, scaled_out), (hidden, hidden_out), (pre, pre_out)]
        )
    ]
    for store in stores:
        store.start()
    if chunks >= 2:
        ret[0].finish(chunks - 2)
    for j in range(chunks):
        ret[1].cross(j)
    ret[0].finish(chunks - 1)
    for j in range(chunks):
        ret[1].finish(j)
    for store in stores:
        store.wait()
    dispatch.drain()
    for each in ret:
        each.drain()


def run_experts(owners, capacity, expert_count, send_rows, grads, w_up, w_down, router):
    experts, width, units = w_up.shape
    slots = owners * 4 * capacity
    chunks = owners // 2
    dims = (owners, experts, capacity, width, units, expert_count)
    any_spec = pl.BlockSpec(memory_space=pl.ANY)
    vmem_spec = pl.BlockSpec(memory_space=pltpu.VMEM)
    bf16 = jnp.bfloat16
    home = jax.ShapeDtypeStruct((owners, experts, capacity, width), bf16)
    slab = jax.ShapeDtypeStruct((experts, slots, width), bf16)
    thin = jax.ShapeDtypeStruct((experts, slots, units), bf16)
    dma = pltpu.SemaphoreType.DMA

    def vm(*shape):
        return pltpu.VMEM(shape, bf16)

    return pl.pallas_call(
        functools.partial(expert_kernel, dims),
        out_shape=(
            home, home, slab, slab, thin, thin,
            jax.ShapeDtypeStruct((LANES, width), jnp.float32),
        ),
        in_specs=[any_spec] * 4 + [vmem_spec],
        out_specs=(any_spec,) * 6 + (vmem_spec,),
        scratch_shapes=[
            vm(experts, slots, width),
            vm(experts, slots, width),
            vm(experts, slots, width),
            vm(experts, slots, units),
            vm(experts, slots, units),
            vm(experts, width, units),
            vm(experts, units, width),
            vm(experts, slots, width),
            vm(experts, slots, width),
            vm(experts, slots // 2, width),
            vm(experts, slots // 2, width),
            vm(experts, slots // 4, width),
            vm(experts, slots // 4, width),
            vm(experts, slots // 4, width),
            vm(experts, slots // 4, width),
            vm(owners, experts, capacity, width),
            vm(owners, experts, capacity, width),
            dma((4,)),
            dma((3,)),
            dma((4, owners)),
            dma((4, owners)),
            dma((2, 2, chunks)),
            dma((2, 2, chunks)),
            dma((2, owners)),
            dma((2, owners)),
        ],
        compiler_params=pltpu.CompilerParams(
            collective_id=1, has_side_effects=True, vmem_limit_bytes=VMEM_LIMIT
        ),
        name="experts",
    )(send_rows, grads, w_up, w_down, router)


def masked_softmax(scores):
    exponent = jnp.exp(scores - jnp.max(scores, axis=1, keepdims=True))
    return exponent * (1.0 / jnp.sum(exponent, axis=1, keepdims=True))


def attend_head(query, key, value, prefix_len):
    half = query.shape[0] // 2
    query = query * (1.0 / math.sqrt(HEAD_DIM))
    row = lax.broadcasted_iota(jnp.int32, (half, half), 0)
    col = lax.broadcasted_iota(jnp.int32, (half, half), 1)
    low = dot_nt(query[:half], key[:half])
    low = jnp.where((col <= row) | (col < prefix_len), low, -1e30)
    low = masked_softmax(low).astype(jnp.bfloat16)
    high = dot_nt(query[half:], key)
    high = jnp.concatenate(
        [high[:, :half], jnp.where(col <= row, high[:, half:], -1e30)], axis=1
    )
    high = masked_softmax(high).astype(jnp.bfloat16)
    return low, high, dot_nn(low, value[:half]), dot_nn(high, value)


def score_grads(probs, grad_probs):
    probs = probs.astype(jnp.float32)
    weighted = probs * grad_probs
    total = jnp.sum(weighted, axis=1, keepdims=True)
    return (weighted - probs * total).astype(jnp.bfloat16)


def attend_back_head(query, key, value, low, high, grad):
    half = query.shape[0] // 2
    scale = 1.0 / math.sqrt(HEAD_DIM)
    query = query * scale
    grad_low = score_grads(low, dot_nt(grad[:half], value[:half]))
    grad_high = score_grads(high, dot_nt(grad[half:], value))
    grad_query = jnp.concatenate(
        [dot_nn(grad_low, key[:half]), dot_nn(grad_high, key)], axis=0
    )
    value_all = dot_tn(high, grad[half:])
    key_all = dot_tn(grad_high, query[half:])
    grad_value = jnp.concatenate(
        [value_all[:half] + dot_tn(low, grad[:half]), value_all[half:]], axis=0
    )
    grad_key = jnp.concatenate(
        [key_all[:half] + dot_tn(grad_low, query[:half]), key_all[half:]], axis=0
    )
    return (
        (grad_query * scale).astype(jnp.bfloat16),
        grad_key.astype(jnp.bfloat16),
        grad_value.astype(jnp.bfloat16),
    )


class Gather:
    def __init__(self, place, pieces, src, dst, sems):
        self.p, self.src, self.dst = place, src, dst
        self.send, self.recv, self.near_send, self.near_recv, self.own_sem = sems
        self.shard = src.shape[0]
        self.half = self.shard // 2
        self.step = self.half // pieces
        self.pieces = pieces
        self.first = lax.rem(place.e, 2) * self.half
        self.second = self.half - self.first

    def block(self, owner, start, size):
        return self.dst.at[pl.ds(pl.multiple_of(owner * self.shard + start, self.step), size)]

    def own(self):
        return pltpu.make_async_copy(self.src, self.block(self.p.w, 0, self.shard), self.own_sem)

    def near(self):
        return remote(
            self.src, self.block(self.p.w, 0, self.shard), self.near_send, self.near_recv,
            (self.p.e, self.p.sib),
        )

    def hop(self, n):
        return remote(
            self.src.at[span(self.first + n * self.step, self.step)],
            self.block(self.p.w, self.first + n * self.step, self.step),
            self.send.at[0, n], self.recv.at[0, n], (self.p.e, self.p.far),
        )

    def pass_from(self, start, n, which, device):
        part = self.block(self.p.far, start + n * self.step, self.step)
        return remote(part, part, self.send.at[which, n], self.recv.at[which, n], device)

    def pairs(self, n):
        return self.pass_from(self.first, n, 1, (self.p.pair, self.p.w))

    def relay(self, n):
        return self.pass_from(self.first, n, 2, (self.p.e, self.p.sib))

    def pair_relay(self, n):
        return self.pass_from(self.second, n, 3, (self.p.e, self.p.sib))

    def start(self):
        every(0, self.pieces, lambda n: self.hop(n).start())
        self.near().start()

    def pass_on(self, n):
        self.hop(n).wait_recv()
        self.pairs(n).start()
        self.relay(n).start()

    def pass_pair(self, n):
        self.pairs(n).wait_recv()
        self.pair_relay(n).start()

    def near_ready(self):
        self.own().wait()
        self.near().wait_recv()

    def far_ready(self):
        def one(n):
            self.relay(n).wait_recv()
            self.pair_relay(n).wait_recv()

        every(0, self.pieces, one)

    def drain(self):
        self.near().wait_send()

        def one(n):
            for copy in (self.hop(n), self.pairs(n), self.relay(n), self.pair_relay(n)):
                copy.wait_send()

        every(0, self.pieces, one)


def slot_tables(routes_ref, priority_ref, capacity, pick_ref, back_ref):
    count = routes_ref.shape[0]
    row = lax.broadcasted_iota(jnp.int32, (count, count), 0).astype(jnp.float32)
    col = lax.broadcasted_iota(jnp.int32, (count, count), 1).astype(jnp.float32)
    eye = row == col
    route_col = routes_ref[...].astype(jnp.float32)
    order_row = priority_ref[...].astype(jnp.float32)
    route_row = jnp.sum(jnp.where(eye, route_col, 0.0), axis=0, keepdims=True)
    order_col = jnp.sum(jnp.where(eye, order_row, 0.0), axis=1, keepdims=True)
    same = route_col == route_row
    rank_row = jnp.sum(
        jnp.where(same & (order_col < order_row), 1.0, 0.0), axis=0, keepdims=True
    )
    rank_col = jnp.sum(
        jnp.where(same & (order_row < order_col), 1.0, 0.0), axis=1, keepdims=True
    )
    slots = float(count)
    slot_row = jnp.where(rank_row < capacity, route_row * capacity + rank_row, slots)
    slot_col = jnp.where(rank_col < capacity, route_col * capacity + rank_col, slots)
    pick_ref[...] = jnp.where(slot_row == row, 1.0, 0.0).astype(jnp.bfloat16)
    back_ref[...] = jnp.where(slot_col == col, 1.0, 0.0).astype(jnp.bfloat16)


def norm_stats(value):
    centered = value - jnp.mean(value, axis=1, keepdims=True)
    inverse = lax.rsqrt(jnp.mean(centered * centered, axis=1, keepdims=True) + epsilon)
    return centered * inverse, inverse


def front_kernel(
    dims,
    prefix_ref, routes_ref, priority_ref, tokens_ref, cot_ref, small_hbm, qkv_hbm, out_hbm,
    qkv_out, act_out, merged_out, back_out, weight_out, out_full, low_out, high_out, grads_rows,
    hidden_ref, send_ref, small_out,
    small, weight, out_w, total, qkv, act, merged, act_two, turned, pick, back, grads_send, low_buf, high_buf,
    own_sem, disp_send, disp_recv, small_send, small_recv, near_send, near_recv,
    gat_send, gat_recv, store_sem, prob_sem,
):
    owners, capacity, pieces = dims
    place = Place(owners)
    rows, width = tokens_ref.shape
    shard = qkv_hbm.shape[0]
    gathers = [
        Gather(
            place, pieces, src, dst,
            (gat_send.at[i], gat_recv.at[i], near_send.at[i], near_recv.at[i], own_sem.at[1 + i]),
        )
        for i, (src, dst) in enumerate(((qkv_hbm, weight), (out_hbm, out_w)))
    ]
    for gather in gathers:
        gather.own().start()
    own_small = pltpu.make_async_copy(small_hbm, small.at[place.w], own_sem.at[3])
    own_small.start()
    greet(
        [(place.ahead(k), place.w) for k in range(1, owners)]
        + [(place.e, place.sib), (place.e, place.far), (place.e, place.diag)]
    )
    smalls = [
        remote(small_hbm, small.at[place.w], small_send.at[i], small_recv.at[i], (place.e, peer))
        for i, peer in enumerate((place.sib, place.far, place.diag))
    ]
    for copy in smalls:
        copy.start()
    for gather in gathers:
        gather.start()
    slot_tables(routes_ref, priority_ref, capacity, pick, back)
    tile = min(256, width)
    shape = grads_send.shape[:3]

    def to_slots(values_ref, slots_ref):
        def one(n):
            cols = span(n * tile, tile)
            value = dot_nn(pick[...], values_ref[:, cols]).astype(jnp.bfloat16)
            slots_ref[:, :, :, cols] = value.reshape(shape + (tile,))

        every(0, width // tile, one)

    to_slots(cot_ref, grads_send)
    dispatch = Dispatch(
        place, capacity, grads_send, grads_rows, (own_sem.at[0], disp_send, disp_recv)
    )
    dispatch.start()
    own_small.wait()
    for copy in smalls:
        copy.wait_recv()
    small_out[...] = small[...]

    def vector(which):
        parts = [small[i, which : which + 1, :] for i in range(4)]
        return jnp.concatenate(parts, axis=1).astype(jnp.float32)

    band = min(64, rows)
    gain, shift = vector(0), vector(1)

    def norm_band(i):
        part = span(i * band, band)
        scaled, _ = norm_stats(tokens_ref[part, :].astype(jnp.float32))
        act[part, :] = (scaled * gain + shift).astype(jnp.bfloat16)

    every(0, rows // band, norm_band)
    turned[0] = act[...].T
    columns = weight.shape[1]
    wide = min(512, columns)

    def multiply(owner, cols):
        depth = span(owner * shard, shard)
        return dot_nn(act[:, depth], weight[depth, cols])

    def first_tile(n):
        cols = span(n * wide, wide)
        total[:, cols] = multiply(place.w, cols) + multiply(place.sib, cols)

    def last_tile(n):
        cols = span(n * wide, wide)
        value = total[:, cols] + multiply(place.far, cols) + multiply(place.diag, cols)
        qkv[:, cols] = value.astype(jnp.bfloat16)

    gathers[0].near_ready()
    every(0, columns // wide, first_tile)

    def pass_piece(gather, n):
        @pl.when(n < pieces)
        def _():
            gather.pass_on(n)

        @pl.when(n >= 1)
        def _():
            gather.pass_pair(n - 1)

    every(0, pieces + 1, lambda n: pass_piece(gathers[0], n))
    gathers[0].far_ready()
    every(0, columns // wide, last_tile)
    stores = [
        pltpu.make_async_copy(src, dst, store_sem.at[i])
        for i, (src, dst) in enumerate(
            [(qkv, qkv_out), (turned.at[0], act_out), (back, back_out), (weight, weight_out),
             (turned.at[1], merged_out), (out_w, out_full)]
        )
    ]
    for store in stores[:4]:
        store.start()
    half = rows // 2
    pairs = width // LANES

    def keep_probs(i):
        slot = lax.rem(i, 2)
        return (
            pltpu.make_async_copy(
                low_buf.at[slot], low_out.at[pl.ds(2 * i, 2)], prob_sem.at[0, slot]
            ),
            pltpu.make_async_copy(
                high_buf.at[slot], high_out.at[pl.ds(2 * i, 2)], prob_sem.at[1, slot]
            ),
        )

    def attend_pair(i):
        slot = lax.rem(i, 2)

        @pl.when(i >= 2)
        def _():
            for copy in keep_probs(i - 2):
                copy.wait()

        query, key, value = (
            qkv[:, span(part * width + i * LANES, LANES)] for part in range(3)
        )
        tops, bottoms = [], []
        for head in range(2):
            part = slice(head * HEAD_DIM, (head + 1) * HEAD_DIM)
            low, high, top, bottom = attend_head(
                query[:, part], key[:, part], value[:, part], prefix_ref[0]
            )
            low_buf[slot, head] = low
            high_buf[slot, head] = high
            tops.append(top)
            bottoms.append(bottom)
        cols = span(i * LANES, LANES)
        merged[:half, cols] = jnp.concatenate(tops, axis=1).astype(jnp.bfloat16)
        merged[half:, cols] = jnp.concatenate(bottoms, axis=1).astype(jnp.bfloat16)
        for copy in keep_probs(i):
            copy.start()

    def attend_step(i):
        @pl.when(i < pairs)
        def _():
            attend_pair(i)

        @pl.when(i < owners)
        def _():
            dispatch.forward(i)

        @pl.when((i >= 1) & (i < pieces + 2))
        def _():
            pass_piece(gathers[1], i - 1)

        @pl.when((i >= 2) & (i < owners + 2))
        def _():
            dispatch.relay(i - 2)

    every(0, max(pairs, owners + 2), attend_step)
    turned[1] = merged[...].T
    stores[4].start()
    gathers[1].near_ready()
    gathers[1].far_ready()
    stores[5].start()
    gain_two, shift_two = vector(2), vector(3)
    band_two = min(128, rows)

    def middle(i):
        part = span(i * band_two, band_two)
        value = tokens_ref[part, :].astype(jnp.float32) + dot_nn(merged[part, :], out_w[...])
        hidden_ref[part, :] = value
        scaled, _ = norm_stats(value)
        act_two[part, :] = (scaled * gain_two + shift_two).astype(jnp.bfloat16)

    every(0, rows // band_two, middle)
    to_slots(act_two, send_ref)
    for i in (pairs - 2, pairs - 1):
        for copy in keep_probs(i):
            copy.wait()
    every(0, owners, dispatch.ready)
    for store in stores:
        store.wait()
    for copy in smalls:
        copy.wait_send()
    for gather in gathers:
        gather.drain()
    dispatch.drain()


def run_front(owners, experts, capacity, prefix, routes, priority, tokens, cotangent, small, w_qkv, w_out):
    rows, width = tokens.shape
    shard, columns = w_qkv.shape
    half = rows // 2
    heads = width // HEAD_DIM
    pieces = 4
    any_spec = pl.BlockSpec(memory_space=pl.ANY)
    vmem_spec = pl.BlockSpec(memory_space=pltpu.VMEM)
    bf16, f32 = jnp.bfloat16, jnp.float32
    dma = pltpu.SemaphoreType.DMA

    def out(*shape):
        return jax.ShapeDtypeStruct(shape, bf16)

    def vm(*shape):
        return pltpu.VMEM(shape, bf16)

    return pl.pallas_call(
        functools.partial(front_kernel, (owners, capacity, pieces)),
        out_shape=(
            out(rows, columns),
            out(width, rows),
            out(width, rows),
            out(rows, rows),
            out(4 * shard, columns),
            out(4 * shard, width),
            out(heads, half, half),
            out(heads, half, rows),
            out(experts, owners * 4 * capacity, width),
            jax.ShapeDtypeStruct((rows, width), f32),
            out(owners, experts, capacity, width),
            out(4, *small.shape),
        ),
        in_specs=[pl.BlockSpec(memory_space=pltpu.SMEM)] + [vmem_spec] * 4 + [any_spec] * 3,
        out_specs=(any_spec,) * 9 + (vmem_spec,) * 3,
        scratch_shapes=[
            vm(4, *small.shape),
            vm(4 * shard, columns),
            vm(4 * shard, width),
            pltpu.VMEM((rows, columns), f32),
            vm(rows, columns),
            vm(rows, width),
            vm(rows, width),
            vm(rows, width),
            vm(2, width, rows),
            vm(rows, rows),
            vm(rows, rows),
            vm(owners, experts, capacity, width),
            vm(2, 2, half, half),
            vm(2, 2, half, rows),
            dma((4,)),
            dma((4, owners)),
            dma((4, owners)),
            dma((3,)),
            dma((3,)),
            dma((2,)),
            dma((2,)),
            dma((2, 4, pieces)),
            dma((2, 4, pieces)),
            dma((6,)),
            dma((2, 2)),
        ],
        compiler_params=pltpu.CompilerParams(
            collective_id=0, has_side_effects=True, vmem_limit_bytes=VMEM_LIMIT
        ),
        name="front",
    )(prefix, routes, priority, tokens, cotangent, small, w_qkv, w_out)


class Reduce:
    def __init__(self, place, part, got, far, pair, lines, done, sems):
        self.p = place
        self.part, self.got, self.far = part, got, far
        self.pair, self.lines, self.done = pair, lines, done
        self.send, self.recv, self.line_send, self.line_recv = sems
        self.chunks = part.shape[0]
        self.halves = done.shape[1] // 2
        self.count = place.owners // 2
        self.slice = self.halves // self.count
        self.bit = lax.rem(place.e, 2)
        self.level = lax.div(place.e, 2)

    def step(self, which, n, src, dst, device):
        return remote(src, dst, self.send.at[which, n], self.recv.at[which, n], device)

    def swapped(self, n):
        return self.step(
            0, n, self.part.at[n, :, 1 - self.p.c], self.got.at[n], (self.p.e, self.p.sib)
        )

    def crossed(self, n):
        return self.step(
            1, n, self.part.at[n, 1 - self.p.x, self.p.c], self.far.at[n], (self.p.e, self.p.far)
        )

    def folded(self, n):
        other = span((1 - self.bit) * self.halves, self.halves)
        return self.step(
            2, n, self.part.at[n, self.p.x, self.p.c, other], self.pair.at[n],
            (self.p.pair, self.p.w),
        )

    def shared(self, n):
        part = self.done.at[n, span(self.bit * self.halves, self.halves)]
        return self.step(3, n, part, part, (self.p.pair, self.p.w))

    def line(self, which, n, k, src, dst):
        return remote(
            src, dst, self.line_send.at[which, n, k], self.line_recv.at[which, n, k],
            (self.p.ahead(2 * k), self.p.w),
        )

    def row(self, level):
        return span(self.bit * self.halves + level * self.slice, self.slice)

    def spreads(self, n, k):
        target = lax.rem(self.level + k, self.count)
        return self.line(
            0, n, k, self.part.at[n, self.p.x, self.p.c, self.row(target)], self.lines.at[n, k]
        )

    def collects(self, n, k):
        part = self.done.at[n, self.row(self.level)]
        return self.line(1, n, k, part, part)

    def pair_sum(self, n, side):
        return self.part[n, side, self.p.c].astype(jnp.float32) + self.got[n, side].astype(
            jnp.float32
        )

    def swap(self, n):
        self.swapped(n).start()

    def cross(self, n):
        self.swapped(n).wait_recv()
        side = 1 - self.p.x
        self.part[n, side, self.p.c] = self.pair_sum(n, side).astype(jnp.bfloat16)
        self.crossed(n).start()

    def fold(self, n):
        self.crossed(n).wait_recv()
        total = self.pair_sum(n, self.p.x) + self.far[n].astype(jnp.float32)
        self.part[n, self.p.x, self.p.c] = total.astype(jnp.bfloat16)
        self.folded(n).start()

    def spread(self, n):
        self.folded(n).wait_recv()
        own = span(self.bit * self.halves, self.halves)
        total = self.part[n, self.p.x, self.p.c, own, :].astype(jnp.float32) + self.pair[
            n
        ].astype(jnp.float32)
        self.part[n, self.p.x, self.p.c, own, :] = total.astype(jnp.bfloat16)
        for k in range(1, self.count):
            self.spreads(n, k).start()

    def collect(self, n):
        total = self.part[n, self.p.x, self.p.c, self.row(self.level), :].astype(jnp.float32)
        for k in range(1, self.count):
            self.spreads(n, k).wait_recv()
            total = total + self.lines[n, k].astype(jnp.float32)
        self.done[n, self.row(self.level), :] = total.astype(jnp.bfloat16)
        for k in range(1, self.count):
            self.collects(n, k).start()

    def share(self, n):
        for k in range(1, self.count):
            self.collects(n, k).wait_recv()
        self.shared(n).start()

    def finish(self, n):
        self.shared(n).wait_recv()

    def stages(self):
        return (self.cross, self.fold, self.spread, self.collect, self.share, self.finish)

    def drain(self):
        def one(n):
            for copy in (self.swapped(n), self.crossed(n), self.folded(n), self.shared(n)):
                copy.wait_send()
            for k in range(1, self.count):
                self.spreads(n, k).wait_send()
                self.collects(n, k).wait_send()

        every(0, self.chunks, one)


class Small:
    def __init__(self, place, value, part, got, mid, far, total, others, out, sems):
        self.p, self.value, self.part, self.got, self.mid = place, value, part, got, mid
        self.far, self.total, self.others, self.out = far, total, others, out
        self.send, self.recv, self.all_send, self.all_recv = sems

    def swapped(self):
        return remote(
            self.part.at[:, 1 - self.p.c], self.got, self.send.at[0], self.recv.at[0],
            (self.p.e, self.p.sib),
        )

    def crossed(self):
        return remote(
            self.mid, self.far, self.send.at[1], self.recv.at[1], (self.p.e, self.p.far)
        )

    def spreads(self, k):
        return remote(
            self.total, self.others.at[k], self.all_send.at[k], self.all_recv.at[k],
            (self.p.ahead(k), self.p.w),
        )

    def swap(self):
        size = self.part.shape[-1]
        for owner in range(4):
            self.part[owner // 2, owner % 2] = self.value[:, owner * size : (owner + 1) * size]
        self.swapped().start()

    def cross(self):
        self.swapped().wait_recv()
        self.mid[...] = self.part[1 - self.p.x, self.p.c] + self.got[1 - self.p.x]
        self.crossed().start()

    def spread(self):
        self.crossed().wait_recv()
        self.total[...] = self.part[self.p.x, self.p.c] + self.got[self.p.x] + self.far[...]
        for k in range(1, self.p.owners):
            self.spreads(k).start()

    def finish(self):
        total = self.total[...]
        for k in range(1, self.p.owners):
            self.spreads(k).wait_recv()
            total = total + self.others[k]
        self.out[...] = total

    def drain(self):
        self.swapped().wait_send()
        self.crossed().wait_send()
        for k in range(1, self.p.owners):
            self.spreads(k).wait_send()


def norm_back_rows(grad, scaled, inverse, gain):
    weighted = grad * gain
    mean_one = jnp.mean(weighted, axis=1, keepdims=True)
    mean_two = jnp.mean(weighted * scaled, axis=1, keepdims=True)
    return inverse * (weighted - mean_one - scaled * mean_two)


def back_kernel(
    dims,
    home_grad_ref, home_out_ref, back_ref, hidden_ref, cot_ref, tokens_ref, vectors_ref, router_ref,
    act_hbm, merged_hbm, qkv_hbm, weight_hbm, out_hbm, low_hbm, high_hbm,
    output_ref, tokens_out, small_out, qkv_out, out_out,
    act_t, merged_t, qkv, weight, out_w, low_buf, high_buf, attn, grad_merged, grad_qkv,
    part_q, got_q, far_q, pair_q, lines_q, done_q,
    part_o, got_o, far_o, pair_o, lines_o, done_o,
    small, small_part, small_got, small_mid, small_far, small_sum, small_all,
    load_sem, prob_sem, send_q, recv_q, lsend_q, lrecv_q, send_o, recv_o, lsend_o, lrecv_o,
    small_send, small_recv, all_send, all_recv, out_sem,
):
    (owners,) = dims
    place = Place(owners)
    loads = [
        pltpu.make_async_copy(src, dst, load_sem.at[i])
        for i, (src, dst) in enumerate(
            [(merged_hbm, merged_t), (out_hbm, out_w), (qkv_hbm, qkv), (act_hbm, act_t),
             (weight_hbm, weight)]
        )
    ]

    def load_probs(i):
        slot = lax.rem(i, 2)
        return (
            pltpu.make_async_copy(
                low_hbm.at[pl.ds(2 * i, 2)], low_buf.at[slot], prob_sem.at[0, slot]
            ),
            pltpu.make_async_copy(
                high_hbm.at[pl.ds(2 * i, 2)], high_buf.at[slot], prob_sem.at[1, slot]
            ),
        )

    for load in loads:
        load.start()
    for load in load_probs(0):
        load.start()
    greet(
        [(place.ahead(k), place.w) for k in range(1, owners)]
        + [(place.e, place.sib), (place.e, place.far)]
    )
    reduce_o = Reduce(
        place, part_o, got_o, far_o, pair_o, lines_o, done_o, (send_o, recv_o, lsend_o, lrecv_o)
    )
    reduce_q = Reduce(
        place, part_q, got_q, far_q, pair_q, lines_q, done_q, (send_q, recv_q, lsend_q, lrecv_q)
    )
    smalls = Small(
        place, small, small_part, small_got, small_mid, small_far, small_sum, small_all, small_out,
        (small_send, small_recv, all_send, all_recv),
    )
    rows, width = tokens_ref.shape
    shard = width // 4
    band = min(128, rows)
    lead = small.shape[0]

    def vector(which):
        parts = [vectors_ref[i, which : which + 1, :] for i in range(4)]
        return jnp.concatenate(parts, axis=1).astype(jnp.float32)

    gain_one, gain_two = vector(0), vector(2)
    small[0:4, :] = jnp.zeros((4, width), jnp.float32)
    small[4:lead, :] = router_ref[0 : lead - 4, :]

    def post(i):
        part = span(i * band, band)
        grad = dot_nn(back_ref[part, :], home_grad_ref[...])
        scaled, inverse = norm_stats(hidden_ref[part, :])
        value = cot_ref[part, :].astype(jnp.float32) + norm_back_rows(
            grad, scaled, inverse, gain_two
        )
        tokens_out[part, :] = value
        attn[part, :] = value.astype(jnp.bfloat16)
        small[2:3, :] += jnp.sum(grad * scaled, axis=0, keepdims=True)
        small[3:4, :] += jnp.sum(grad, axis=0, keepdims=True)

    every(0, rows // band, post)
    loads[0].wait()

    def weight_grad(part, n, left, right):
        def one(owner):
            value = dot_nn(left[span(owner * shard, shard), :], right)
            part[n, lax.div(owner, 2), lax.rem(owner, 2)] = value.astype(jnp.bfloat16)

        every(0, 4, one)

    tile_o = part_o.shape[-1]
    out_chunks = part_o.shape[0]
    for n in range(out_chunks):
        weight_grad(part_o, n, merged_t, attn[:, n * tile_o : (n + 1) * tile_o])
        reduce_o.swap(n)
    loads[1].wait()

    def merged_band(i):
        part = span(i * band, band)
        grad_merged[part, :] = dot_nt(attn[part, :], out_w[...]).astype(jnp.bfloat16)

    every(0, rows // band, merged_band)
    for load in loads[2:4]:
        load.wait()
    pairs = part_q.shape[0]

    def attend_pair(i):
        slot = lax.rem(i, 2)
        for load in load_probs(i):
            load.wait()

        @pl.when(i + 1 < pairs)
        def _():
            for load in load_probs(i + 1):
                load.start()

        cols = span(i * LANES, LANES)
        query, key, value = (
            qkv[:, span(part * width + i * LANES, LANES)] for part in range(3)
        )
        grad = grad_merged[:, cols]
        results = []
        for head in range(2):
            part = slice(head * HEAD_DIM, (head + 1) * HEAD_DIM)
            results.append(
                attend_back_head(
                    query[:, part], key[:, part], value[:, part],
                    low_buf[slot, head], high_buf[slot, head], grad[:, part],
                )
            )
        for which in range(3):
            grad_qkv[:, span(which * width + i * LANES, LANES)] = jnp.concatenate(
                [results[0][which], results[1][which]], axis=1
            )
        right = jnp.concatenate(
            [grad_qkv[:, span(which * width + i * LANES, LANES)] for which in range(3)], axis=1
        )
        weight_grad(part_q, i, act_t, right)
        reduce_q.swap(i)

    def input_band(i):
        part = span(i * band, band)
        grad = dot_nt(grad_qkv[part, :], weight[...])
        scaled, inverse = norm_stats(tokens_ref[part, :].astype(jnp.float32))
        tokens_out[part, :] += norm_back_rows(grad, scaled, inverse, gain_one)
        small[0:1, :] += jnp.sum(grad * scaled, axis=0, keepdims=True)
        small[1:2, :] += jnp.sum(grad, axis=0, keepdims=True)

    def output_band(i):
        part = span(i * band, band)
        value = hidden_ref[part, :] + dot_nn(back_ref[part, :], home_out_ref[...])
        output_ref[part, :] = value.astype(jnp.bfloat16)

    def store_q(i):
        return [
            pltpu.make_async_copy(
                done_q.at[i, :, pl.ds(which * LANES, LANES)],
                qkv_out.at[:, span(which * width + i * LANES, LANES)],
                out_sem.at[which, i],
            )
            for which in range(3)
        ]

    def store_o(n):
        return pltpu.make_async_copy(
            done_o.at[n], out_out.at[:, span(n * tile_o, tile_o)], out_sem.at[3, n]
        )

    stages_o, stages_q = reduce_o.stages(), reduce_q.stages()
    depth = len(stages_q)

    def slot_step(slot):
        for s in range(depth - 1, -1, -1):
            n = slot - 1 - s

            @pl.when((n >= 0) & (n < pairs))
            def _(s=s, n=n):
                stages_q[s](n)
                if s == depth - 1:
                    for copy in store_q(n):
                        copy.start()

            @pl.when(slot == s)
            def _(s=s):
                for n in range(out_chunks):
                    stages_o[s](n)
                    if s == depth - 1:
                        store_o(n).start()

        @pl.when(slot < pairs)
        def _():
            attend_pair(slot)

        @pl.when(slot == pairs)
        def _():
            loads[4].wait()
            every(0, rows // band // 2, input_band)

        @pl.when(slot == pairs + 1)
        def _():
            every(rows // band // 2, rows // band, input_band)

        @pl.when(slot == pairs + 2)
        def _():
            smalls.swap()
            every(0, rows // band, output_band)

        @pl.when(slot == pairs + 3)
        def _():
            smalls.cross()

        @pl.when(slot == pairs + 4)
        def _():
            smalls.spread()

        @pl.when(slot == pairs + 5)
        def _():
            smalls.finish()

    every(0, pairs + depth, slot_step)

    def stored(i):
        for copy in store_q(i):
            copy.wait()

    every(0, pairs, stored)
    for n in range(out_chunks):
        store_o(n).wait()
    reduce_o.drain()
    reduce_q.drain()
    smalls.drain()


def run_back(
    owners, lead, home_grad, home_out, back, hidden, cotangent, tokens, vectors, router_grad,
    act_t, merged_t, qkv, weight, w_out, low, high,
):
    rows, width = tokens.shape
    shard = width // 4
    pairs = width // LANES
    tile_o = min(512, width)
    out_chunks = width // tile_o
    count = owners // 2
    half = shard // 2
    mid = rows // 2
    any_spec = pl.BlockSpec(memory_space=pl.ANY)
    vmem_spec = pl.BlockSpec(memory_space=pltpu.VMEM)
    bf16, f32 = jnp.bfloat16, jnp.float32
    dma = pltpu.SemaphoreType.DMA

    def vm(*shape):
        return pltpu.VMEM(shape, bf16)

    def fm(*shape):
        return pltpu.VMEM(shape, f32)

    def reduce_buffers(chunks, tile):
        return [
            vm(chunks, 2, 2, shard, tile),
            vm(chunks, 2, shard, tile),
            vm(chunks, shard, tile),
            vm(chunks, half, tile),
            vm(chunks, count, half // count, tile),
            vm(chunks, shard, tile),
        ]

    def reduce_sems(chunks):
        return [dma((4, chunks)), dma((4, chunks)), dma((2, chunks, count)), dma((2, chunks, count))]

    return pl.pallas_call(
        functools.partial(back_kernel, (owners,)),
        out_shape=(
            jax.ShapeDtypeStruct((rows, width), bf16),
            jax.ShapeDtypeStruct((rows, width), f32),
            jax.ShapeDtypeStruct((lead, shard), f32),
            jax.ShapeDtypeStruct((shard, 3 * width), bf16),
            jax.ShapeDtypeStruct((shard, width), bf16),
        ),
        in_specs=[vmem_spec] * 8 + [any_spec] * 7,
        out_specs=(vmem_spec,) * 3 + (any_spec,) * 2,
        scratch_shapes=[
            vm(width, rows),
            vm(width, rows),
            vm(rows, 3 * width),
            vm(width, 3 * width),
            vm(width, width),
            vm(2, 2, mid, mid),
            vm(2, 2, mid, rows),
            vm(rows, width),
            vm(rows, width),
            vm(rows, 3 * width),
        ]
        + reduce_buffers(pairs, 3 * LANES)
        + reduce_buffers(out_chunks, tile_o)
        + [
            fm(lead, width),
            fm(2, 2, lead, shard),
            fm(2, lead, shard),
            fm(lead, shard),
            fm(lead, shard),
            fm(lead, shard),
            fm(owners, lead, shard),
            dma((5,)),
            dma((2, 2)),
        ]
        + reduce_sems(pairs)
        + reduce_sems(out_chunks)
        + [dma((2,)), dma((2,)), dma((owners,)), dma((owners,)), dma((4, pairs))],
        compiler_params=pltpu.CompilerParams(
            collective_id=2, has_side_effects=True, vmem_limit_bytes=VMEM_LIMIT
        ),
        name="back",
    )(
        home_grad, home_out, back, hidden, cotangent, tokens, vectors, router_grad,
        act_t, merged_t, qkv, weight, w_out, low, high,
    )


def on_device_plain(
    tokens,
    norm1_gain,
    norm1_shift,
    w_qkv,
    w_out,
    norm2_gain,
    norm2_shift,
    w_router,
    w_up,
    w_down,
    routes,
    priority,
    prefix,
    cotangent,
):
    row_count, model_width = tokens.shape
    expert_count = w_router.shape[1]
    capacity = row_count // expert_count
    owners = lax.axis_size("expert")
    local_experts = w_up.shape[0]
    slot_count = expert_count * capacity
    prefix_len = prefix[0]
    small = jnp.concatenate(
        [
            norm1_gain[None],
            norm1_shift[None],
            norm2_gain[None],
            norm2_shift[None],
            w_router.T,
        ],
        axis=0,
    )
    qkv_full = lax.all_gather(w_qkv, "wshard", axis=0, tiled=True)
    small_full = lax.all_gather(small, "wshard", axis=1, tiled=True)
    out_full = lax.all_gather(w_out, "wshard", axis=0, tiled=True)
    gain_one, shift_one, gain_two, shift_two = (small_full[i] for i in range(4))
    router_full = small_full[4:].T
    gain_one = gain_one.astype(jnp.float32)
    gain_two = gain_two.astype(jnp.float32)
    inputs = tokens.astype(jnp.float32)
    normed_one, scaled_one, inverse_one = normalize(inputs, gain_one, shift_one.astype(jnp.float32))
    act_one = normed_one.astype(jnp.bfloat16)
    qkv = jnp.dot(act_one, qkv_full, preferred_element_type=jnp.float32).astype(jnp.bfloat16)
    query_heads = qkv[:, :model_width]
    key_heads = qkv[:, model_width : 2 * model_width]
    value_heads = qkv[:, 2 * model_width :]
    merged, log_totals = attend_forward(query_heads, key_heads, value_heads, prefix_len)
    attn_out = jnp.dot(merged, out_full, preferred_element_type=jnp.float32)
    hidden = inputs + attn_out
    normed_two, scaled_two, inverse_two = normalize(hidden, gain_two, shift_two.astype(jnp.float32))
    act_two = normed_two.astype(jnp.bfloat16)
    logits = jnp.dot(act_two, router_full, preferred_element_type=jnp.float32)
    row_max = jnp.max(logits, axis=-1, keepdims=True)
    exponent = jnp.exp(logits - row_max)
    gate_prob = exponent / jnp.sum(exponent, axis=-1, keepdims=True)
    route_ids = routes[:, 0]
    chosen = route_ids[:, None] == jnp.arange(expert_count, dtype=jnp.int32)[None, :]
    gate_value = jnp.sum(jnp.where(chosen, gate_prob, 0.0), axis=1)
    slot_index, slot_source = assign_slots(route_ids, priority[0], expert_count, capacity)
    zero_row = jnp.zeros((1, model_width), jnp.bfloat16)
    padded = jnp.concatenate([act_two, zero_row], axis=0)
    send_rows = padded[slot_source].reshape(owners, local_experts * capacity, model_width)
    arrived = lax.all_to_all(send_rows, "expert", split_axis=0, concat_axis=0, tiled=True).reshape(
        owners, local_experts, capacity, model_width
    )
    group = lax.axis_size("wshard")
    local_rows = owners * capacity

    def by_expert(chunk):
        rows = jnp.transpose(chunk, (1, 0, 2, 3)).reshape(local_experts, local_rows, model_width)
        return lax.all_gather(rows, "wshard", axis=1, tiled=True)

    def home_rows(rows):
        own = lax.psum_scatter(rows.astype(jnp.bfloat16), "wshard", scatter_dimension=1, tiled=True)
        own = own.reshape(local_experts, owners, capacity, model_width)
        return jnp.transpose(own, (1, 0, 2, 3)).reshape(
            owners, local_experts * capacity, model_width
        )

    grad_output = cotangent.astype(jnp.float32)
    grad_combined = (gate_value[:, None] * grad_output).astype(jnp.bfloat16)
    grad_padded = jnp.concatenate([grad_combined, zero_row], axis=0)
    grad_send = grad_padded[slot_source].reshape(owners, local_experts * capacity, model_width)
    grad_arrived = lax.all_to_all(
        grad_send, "expert", split_axis=0, concat_axis=0, tiled=True
    ).reshape(owners, local_experts, capacity, model_width)
    rows_in = by_expert(arrived)
    grad_rows = by_expert(grad_arrived)
    pre_act = jnp.einsum("erd,edf->erf", rows_in, w_up, preferred_element_type=jnp.float32)
    activated, gelu_pull = jax.vjp(gelu_tanh, pre_act)
    act_hidden = activated.astype(jnp.bfloat16)
    produced = jnp.einsum(
        "erf,efd->erd", act_hidden, w_down, preferred_element_type=jnp.float32
    )
    expert_out = home_rows(produced)
    returned = lax.all_to_all(expert_out, "expert", split_axis=0, concat_axis=0, tiled=True)
    slots_back = jnp.concatenate([returned.reshape(slot_count, model_width), zero_row], axis=0)
    combined = slots_back[slot_index].astype(jnp.float32)
    output = (hidden + gate_value[:, None] * combined).astype(jnp.bfloat16)
    grad_gate = jnp.sum(grad_output * combined, axis=1)
    grad_down = jnp.einsum(
        "erf,erd->efd", act_hidden, grad_rows, preferred_element_type=jnp.float32
    )
    grad_hidden_units = jnp.einsum(
        "erd,efd->erf", grad_rows, w_down, preferred_element_type=jnp.float32
    )
    grad_pre = gelu_pull(grad_hidden_units)[0].astype(jnp.bfloat16)
    grad_up = jnp.einsum("erd,erf->edf", rows_in, grad_pre, preferred_element_type=jnp.float32)
    grad_expert_in = jnp.einsum(
        "erf,edf->erd", grad_pre, w_up, preferred_element_type=jnp.float32
    )
    grad_send_back = home_rows(grad_expert_in)
    grad_back = lax.all_to_all(grad_send_back, "expert", split_axis=0, concat_axis=0, tiled=True)
    grad_slots = jnp.concatenate([grad_back.reshape(slot_count, model_width), zero_row], axis=0)
    grad_act_two = grad_slots[slot_index].astype(jnp.float32)
    grad_logits = (
        gate_prob * (jnp.where(chosen, grad_gate[:, None], 0.0) - (gate_value * grad_gate)[:, None])
    ).astype(jnp.bfloat16)
    grad_router = contract_rows(act_two, grad_logits)
    grad_act_two = grad_act_two + times_transpose(grad_logits, router_full)
    grad_from_two, grad_gain_two, grad_shift_two = norm_back(
        grad_act_two, scaled_two, inverse_two, gain_two
    )
    grad_hidden = grad_output + grad_from_two
    grad_attn = grad_hidden.astype(jnp.bfloat16)
    grad_out_w = contract_rows(merged, grad_attn)
    grad_merged = times_transpose(grad_attn, out_full).astype(jnp.bfloat16)
    grad_qkv = attend_backward(
        query_heads, key_heads, value_heads, grad_merged, log_totals, prefix_len
    )
    grad_qkv_w = contract_rows(act_one, grad_qkv)
    grad_act_one = times_transpose(grad_qkv, qkv_full)
    grad_from_one, grad_gain_one, grad_shift_one = norm_back(
        grad_act_one, scaled_one, inverse_one, gain_one
    )
    grad_tokens = grad_hidden + grad_from_one
    small_grad = jnp.concatenate(
        [
            grad_gain_one[None],
            grad_shift_one[None],
            grad_gain_two[None],
            grad_shift_two[None],
            grad_router.T,
        ],
        axis=0,
    )
    out_share = lax.psum_scatter(
        grad_out_w.astype(jnp.bfloat16), "wshard", scatter_dimension=0, tiled=True
    )
    qkv_share = lax.psum_scatter(
        grad_qkv_w.astype(jnp.bfloat16), "wshard", scatter_dimension=0, tiled=True
    )
    small_share = lax.psum_scatter(small_grad, "wshard", scatter_dimension=1, tiled=True)
    out_total = lax.psum(out_share, "expert").astype(jnp.float32)
    qkv_total = lax.psum(qkv_share, "expert").astype(jnp.float32)
    small_total = lax.psum(small_share, "expert")
    totals = (
        small_total[0],
        small_total[1],
        qkv_total,
        out_total,
        small_total[2],
        small_total[3],
        small_total[4:].T,
    )
    return (
        output,
        grad_tokens,
        totals[0],
        totals[1],
        totals[2],
        totals[3],
        totals[4],
        totals[5],
        totals[6],
        grad_up,
        grad_down,
    )


def on_device(
    tokens,
    norm1_gain,
    norm1_shift,
    w_qkv,
    w_out,
    norm2_gain,
    norm2_shift,
    w_router,
    w_up,
    w_down,
    routes,
    priority,
    prefix,
    cotangent,
):
    row_count, model_width = tokens.shape
    expert_count = w_router.shape[1]
    capacity = row_count // expert_count
    owners = lax.axis_size("expert")
    experts = w_up.shape[0]
    small = jnp.concatenate(
        [norm1_gain[None], norm1_shift[None], norm2_gain[None], norm2_shift[None], w_router.T],
        axis=0,
    )
    lead = small.shape[0]
    small = jnp.pad(small, ((0, -lead % 16), (0, 0)))
    (
        qkv, act_t, merged_t, back, weight, out_full, low, high, grad_rows, hidden, send_rows,
        vectors,
    ) = run_front(
        owners, experts, capacity, prefix, routes, priority, tokens, cotangent, small, w_qkv, w_out
    )
    router = jnp.transpose(vectors[:, 4:lead], (0, 2, 1)).reshape(model_width, expert_count)
    router = jnp.pad(router, ((0, 0), (0, LANES - expert_count)))
    home_out, home_grad, rows, scaled, act_hidden, grad_pre, grad_router = run_experts(
        owners, capacity, expert_count, send_rows, grad_rows, w_up, w_down, router
    )
    grad_down = jnp.einsum("erf,erd->efd", act_hidden, scaled, preferred_element_type=jnp.float32)
    grad_up = jnp.einsum("erd,erf->edf", rows, grad_pre, preferred_element_type=jnp.float32)
    output, grad_tokens, small_total, qkv_total, out_total = run_back(
        owners, lead + -lead % 8, home_grad.reshape(-1, model_width),
        home_out.reshape(-1, model_width), back, hidden, cotangent, tokens, vectors, grad_router,
        act_t, merged_t, qkv, weight, out_full, low, high,
    )
    return (
        output,
        grad_tokens,
        small_total[0],
        small_total[1],
        qkv_total.astype(jnp.float32),
        out_total.astype(jnp.float32),
        small_total[2],
        small_total[3],
        small_total[4:lead].T,
        grad_up,
        grad_down,
    )


def solution(mesh):
    placed = (
        P(("expert", "wshard"), None),
        P("wshard"),
        P("wshard"),
        P("wshard", None),
        P("wshard", None),
        P("wshard"),
        P("wshard"),
        P("wshard", None),
        P("expert", None, "wshard"),
        P("expert", "wshard", None),
        P(("expert", "wshard"), None),
        P(("expert", "wshard"), None),
        P(("expert", "wshard")),
        P(("expert", "wshard"), None),
    )
    owners, group = mesh.shape["expert"], mesh.shape["wshard"]

    def body(*args):
        capacity = args[0].shape[0] // args[7].shape[1]
        fits = group == 4 and owners % 2 == 0 and capacity % 16 == 0
        return (on_device if fits else on_device_plain)(*args)

    return jax.shard_map(
        body,
        mesh=mesh,
        in_specs=placed,
        out_specs=(
            P(("expert", "wshard"), None),
            P(("expert", "wshard"), None),
            P("wshard"),
            P("wshard"),
            P("wshard", None),
            P("wshard", None),
            P("wshard"),
            P("wshard"),
            P("wshard", None),
            P("expert", None, "wshard"),
            P("expert", "wshard", None),
        ),
        check_vma=False,
    )
```

profile of v0, /device:TPU:0, one launch (start us, length us, event | category | flops | bytes accessed | tf_op | source)
XLA Modules:
  0.0 338.4 jit_solution(12429422454792101270)
XLA Ops:
  1.3 0.7 broadcast_in_dim.12
  1.9 0.7 broadcast_in_dim.13
  2.6 0.7 broadcast_in_dim.14
  3.3 0.7 broadcast_in_dim.15
  3.9 0.8 concatenate.3
  4.8 0.6 pad.8.small_hbm
  5.4 1.5 copy.25.routes_ref
  6.9 76.9 %front.1 = (bf16[512,3072]{1,0:T(8,128)(2,1)}, bf16[1024,512]{1,0:T(8,128)(2,1)}, bf16[1024,512]{1,0:T(8,128)(2,1)}, bf16[512,512]{1,0:T(8,128)(2,1)}, bf16[1024...) custom-call(s32[1]{0:T(128)S(6)} %copy.33.prefix_ref, ...), custom_call_target="tpu_custom_call" | custom-call | tf_op jit(solution)/shard_map/front/pallas_call | solution.py:1003
  83.8 0.8 slice_bitcast_fusion
  84.6 0.2 copy.26
  84.8 0.8 pad.9.router_ref
  85.6 126.5 %experts.1 = (bf16[8,2,32,1024]{3,2,1,0:T(8,128)(2,1)}, bf16[8,2,32,1024]{3,2,1,0:T(8,128)(2,1)}, bf16[2,1024,1024]{2,1,0:T(8,128)(2,1)}, bf16[2,1024,1024]{2,1,...) custom-call(bf16[8,2,32,1024]{3,2,1,0:T(8,128)(2,1)} %get-tuple-element.35.send, ...), custom_call_target="tpu_custom_call" | custom-call | tf_op jit(solution)/shard_map/experts/pallas_call | solution.py:585
  212.1 99.4 %back.1 = (bf16[512,1024]{1,0:T(8,128)(2,1)}, f32[512,1024]{1,0:T(8,128)}, f32[24,256]{1,0:T(8,128)}, bf16[256,3072]{1,0:T(8,128)(2,1)}, bf16[256,1024]{1,0:T(8,128)(2,1)}) custom-call(bf16[512,1024]{1,0:T(8,128)(2,1)} %bitcast.18, bf16[512,1024]{1,0:T(8,128)(2,1)} %bitcast.17, bf16[512,512]{1,0:T(8,128)(2,1)} %get-tuple-element.40.back_ref, ...), custom_call_target="tpu_custom_call" | custom-call | tf_op jit(solution)/shard_map/back/pallas_call | solution.py:1498
  311.5 0.0 copy-start.4
  311.5 1.5 fusion
  313.0 1.3 slice_bitcast_fusion.1
  314.3 2.1 convert_element_type.11
  316.4 3.4 %convert_element_type.10 = f32[256,3072]{1,0:T(8,128)} convert(bf16[256,3072]{1,0:T(8,128)(2,1)} %get-tuple-element.53) | non-fusion elementwise | flops 786432 | bytes 4718592 | tf_op jit(solution)/shard_map/convert_element_type | solution.py:1778
  319.9 0.0 copy-done.4
  319.9 0.0 copy-start.2
  319.9 0.0 copy-start.3
  319.9 9.4 %fusion.1 = f32[2,1024,1024]{2,1,0:T(8,128)} fusion(bf16[2,1024,1024]{2,1,0:T(8,128)(2,1)S(1)} %copy-done.4, bf16[2,1024,1024]{2,1,0:T(8,128)(2,1)} %get-tuple-element.56), kind=kOutput, calls=%fused_computation.3 | convolution fusion | flops 4294967296 | bytes 16777216 | tf_op jit(solution)/shard_map/erd,erf->edf/dot_general | solution.py:1767
  329.3 0.0 copy-done.2
  329.3 0.0 copy-done.3
  329.3 0.0 copy-start.1
  329.3 0.0 copy-start
  329.3 6.8 %fusion.2 = f32[2,1024,1024]{2,1,0:T(8,128)} fusion(bf16[2,1024,1024]{2,1,0:T(8,128)(2,1)S(1)} %copy-done.3, bf16[2,1024,1024]{2,1,0:T(8,128)(2,1)S(1)} %copy-done.2), kind=kOutput, calls=%fused_computation.4 | convolution fusion | flops 4294967296 | bytes 16777216 | tf_op jit(solution)/shard_map/erf,erd->efd/dot_general | solution.py:1766
  336.1 0.0 copy-done.1
  336.1 1.0 copy.34
  337.1 0.0 copy-done
  337.1 1.3 copy.35
Async XLA Ops:
  311.5 8.4 %copy-start.4 = (bf16[2,1024,1024]{2,1,0:T(8,128)(2,1)S(1)}, bf16[2,1024,1024]{2,1,0:T(8,128)(2,1)}, u32[]{:S(2)}) copy-start(bf16[2,1024,1024]{2,1,0:T(8,128)(2,1)} %get-tuple-element.55) | copy-start | bytes 12582916
  319.9 9.4 %copy-start.2 = (bf16[2,1024,1024]{2,1,0:T(8,128)(2,1)S(1)}, bf16[2,1024,1024]{2,1,0:T(8,128)(2,1)}, u32[]{:S(2)}) copy-start(bf16[2,1024,1024]{2,1,0:T(8,128)(2,1)} %get-tuple-element.58) | copy-start | bytes 12582916
  319.9 9.4 %copy-start.3 = (bf16[2,1024,1024]{2,1,0:T(8,128)(2,1)S(1)}, bf16[2,1024,1024]{2,1,0:T(8,128)(2,1)}, u32[]{:S(2)}) copy-start(bf16[2,1024,1024]{2,1,0:T(8,128)(2,1)} %get-tuple-element.57) | copy-start | bytes 12582916
  329.3 6.8 %copy-start.1 = (bf16[512,1024]{1,0:T(8,128)(2,1)S(1)}, bf16[512,1024]{1,0:T(8,128)(2,1)}, u32[]{:S(2)}) copy-start(bf16[512,1024]{1,0:T(8,128)(2,1)} %get-tuple-element.74) | copy-start | bytes 3145732
  329.3 7.8 %copy-start = (f32[512,1024]{1,0:T(8,128)S(1)}, f32[512,1024]{1,0:T(8,128)}, u32[]{:S(2)}) copy-start(f32[512,1024]{1,0:T(8,128)} %get-tuple-element.75) | copy-start | bytes 6291460
where the time goes:
time: 339 us; the launch traced here: 338 us
  Pallas kernels  303 us (89%)
  matrix products  16.2 us (5%)
  local copies, waits for them, and re-layouts  12.5 us (4%)
  other arithmetic  5.56 us (2%)
    pallas_call x1, Pallas kernels, run_experts(): pl.pallas_call(functools.partial(expert_kernel, dims), out_shape=(home, h...  126 us
    pallas_call x1, Pallas kernels, run_back(): pl.pallas_call(functools.partial(back_kernel, (owners,)), out_shape=(jax....  99.4 us
    pallas_call x1, Pallas kernels, run_front(): pl.pallas_call(functools.partial(front_kernel, (owners, capacity, pieces)...  76.9 us
    dot_general x1, matrix products, on_device(): jnp.einsum('erd,erf->edf', rows, grad_pre, preferred_element_type=jnp.flo...  9.38 us
    dot_general x1, matrix products, on_device(): jnp.einsum('erf,erd->efd', act_hidden, scaled, preferred_element_type=jnp...  6.82 us

commit v1 on v0

--- a/solution.py
+++ b/solution.py
@@ -14,6 +14,7 @@
 
 epsilon = 1e-05
 VMEM_LIMIT = 66_000_000
+TILE = 512
 
 
 def normalize(values, gain_vec, shift_vec):
@@ -239,8 +240,13 @@
     def ahead(self, k):
         return lax.rem(self.e + k, self.owners)
 
-    def behind(self, k):
-        return lax.rem(self.e + self.owners - k, self.owners)
+    def peer(self, n):
+        other = lax.div(n, 2) + lax.rem(n, 2) * (self.owners // 2)
+        result, bit = 0, 1
+        while bit < self.owners:
+            result = result + bit * lax.rem(lax.div(self.e, bit) + lax.div(other, bit), 2)
+            bit *= 2
+        return result
 
 
 def remote(src, dst, send, recv, device):
@@ -261,6 +267,11 @@
     pl.semaphore_wait(barrier, len(peers))
 
 
+def either(test, yes, no):
+    pl.when(test)(yes)
+    pl.when(jnp.logical_not(test))(no)
+
+
 class Dispatch:
     def __init__(self, place, capacity, send_ref, rows_ref, sems):
         self.p, self.cap, self.src, self.rows = place, capacity, send_ref, rows_ref
@@ -277,11 +288,11 @@
 
     def direct(self, k):
         return remote(
-            self.src.at[self.p.ahead(k)],
+            self.src.at[self.p.peer(k)],
             self.slice(k, self.p.c, self.p.x),
             self.send.at[0, k],
             self.recv.at[0, k],
-            (self.p.ahead(k), self.p.w),
+            (self.p.peer(k), self.p.w),
         )
 
     def hop(self, k, side, which, peer):
@@ -343,18 +354,38 @@
             part, got, mid, far, done, home,
         )
         self.own_sem, self.send, self.recv, self.home_send, self.home_recv = sems
-        self.swapped, self.crossed, self.homed = {}, {}, {}
-
-    def swap(self, j):
+
+    def swapped(self, j):
         size = 4 * self.cap
-        self.swapped[j] = remote(
+        return remote(
             self.part.at[:, span((j * 2 + 1 - self.p.c) * size, size)],
             self.got.at[:, span(j * size, size)],
             self.send.at[0, j],
             self.recv.at[0, j],
             (self.p.e, self.p.sib),
         )
-        self.swapped[j].start()
+
+    def crossed(self, j):
+        part = span(j * 2 * self.cap, 2 * self.cap)
+        return remote(
+            self.mid.at[:, part],
+            self.far.at[:, part],
+            self.send.at[1, j],
+            self.recv.at[1, j],
+            (self.p.e, self.p.far),
+        )
+
+    def own(self):
+        return pltpu.make_async_copy(self.done.at[0], self.home.at[self.p.e], self.own_sem)
+
+    def homed(self, n):
+        return remote(
+            self.done.at[n],
+            self.home.at[self.p.e],
+            self.home_send.at[n],
+            self.home_recv.at[n],
+            (self.p.peer(n), self.p.w),
+        )
 
     def pair_sum(self, expert, j, side):
         size = 2 * self.cap
@@ -362,55 +393,40 @@
         theirs = self.got[expert, span((j * 2 + side) * size, size), :]
         return mine.astype(jnp.float32) + theirs.astype(jnp.float32)
 
+    def swap(self, j):
+        self.swapped(j).start()
+
     def cross(self, j):
-        self.swapped[j].wait_recv()
+        self.swapped(j).wait_recv()
         size = 2 * self.cap
         for expert in range(self.experts):
-            self.mid[expert, pl.ds(j * size, size), :] = self.pair_sum(
+            self.mid[expert, span(j * size, size), :] = self.pair_sum(
                 expert, j, 1 - self.p.x
             ).astype(jnp.bfloat16)
-        part = pl.ds(j * size, size)
-        self.crossed[j] = remote(
-            self.mid.at[:, part],
-            self.far.at[:, part],
-            self.send.at[1, j],
-            self.recv.at[1, j],
-            (self.p.e, self.p.far),
-        )
-        self.crossed[j].start()
+        self.crossed(j).start()
 
     def finish(self, j):
-        self.crossed[j].wait_recv()
+        self.crossed(j).wait_recv()
         size = 2 * self.cap
         for expert in range(self.experts):
             total = self.pair_sum(expert, j, self.p.x) + self.far[
-                expert, pl.ds(j * size, size), :
+                expert, span(j * size, size), :
             ].astype(jnp.float32)
             total = total.astype(jnp.bfloat16)
             self.done[2 * j, expert] = total[: self.cap]
             self.done[2 * j + 1, expert] = total[self.cap :]
-        for k in (2 * j, 2 * j + 1):
-            if k == 0:
-                copy = pltpu.make_async_copy(
-                    self.done.at[0], self.home.at[self.p.e], self.own_sem
-                )
-            else:
-                copy = remote(
-                    self.done.at[k],
-                    self.home.at[self.p.e],
-                    self.home_send.at[k],
-                    self.home_recv.at[k],
-                    (self.p.behind(k), self.p.w),
-                )
-            copy.start()
-            self.homed[k] = copy
-
-    def drain(self):
-        for group in (self.swapped, self.crossed):
-            for copy in group.values():
-                copy.wait_send()
-        for k, copy in self.homed.items():
-            copy.wait()
+        j = jnp.int32(j)
+        self.homed(2 * j + 1).start()
+        either(j == 0, lambda: self.own().start(), lambda: self.homed(2 * j).start())
+
+    def drain(self, chunks):
+        def one(j):
+            self.swapped(j).wait_send()
+            self.crossed(j).wait_send()
+
+        every(0, chunks, one)
+        self.own().wait()
+        every(1, self.p.owners, lambda n: self.homed(n).wait())
 
 
 def gelu_pair(v):
@@ -425,8 +441,8 @@
 def expert_kernel(
     dims,
     send_ref, grads_hbm, up_hbm, down_hbm, router_ref,
-    home_out, home_grad, rows_out, scaled_out, hidden_out, pre_out, router_grad,
-    rows, grads, scaled, hidden, pre, up, down,
+    home_out, home_grad, up_out, down_out, router_grad,
+    rows, grads, scaled, hidden, pre, up, down, grad_up, grad_down,
     part_out, part_grad, got_out, got_grad, mid_out, mid_grad,
     far_out, far_grad, done_out, done_grad,
     load_sem, own_sem, disp_send, disp_recv, red_send, red_recv, home_send, home_recv,
@@ -448,7 +464,7 @@
     dispatch = Dispatch(
         place, capacity, send_ref, rows, (own_sem.at[0], disp_send, disp_recv)
     )
-    ret = [
+    ret_grad, ret_out = [
         Return(
             place, capacity, experts, part, got, mid, far, done, home,
             (own_sem.at[1 + i], red_send.at[i], red_recv.at[i], home_send.at[i], home_recv.at[i]),
@@ -462,108 +478,137 @@
     ]
     dispatch.start()
     router_grad[...] = jnp.zeros_like(router_grad)
-    tile = min(256, units)
-    wide = min(256, width)
+    tile = min(TILE, units)
+    wide = min(TILE, width)
     chunks = owners // 2
     size = 8 * capacity
     lane = lax.broadcasted_iota(jnp.int32, (size, LANES), 1)
 
-    def compute(j):
-        here = pl.ds(j * size, size)
-
-        def one_expert(expert, carry):
-            logits = dot_nn(rows[expert, here, :], router_ref[...])
-            logits = jnp.where(lane < expert_count, logits, -1e30)
-            exponent = jnp.exp(logits - jnp.max(logits, axis=1, keepdims=True))
-            prob = exponent / jnp.sum(exponent, axis=1, keepdims=True)
-            mine = lane == place.e * experts + expert
-            gate = jnp.sum(jnp.where(mine, prob, 0.0), axis=1, keepdims=True)
-            scaled[expert, here, :] = (
-                gate * grads[expert, here, :].astype(jnp.float32)
+    def compute(j, expert):
+        here = span(j * size, size)
+        logits = dot_nn(rows[expert, here, :], router_ref[...])
+        logits = jnp.where(lane < expert_count, logits, -1e30)
+        exponent = jnp.exp(logits - jnp.max(logits, axis=1, keepdims=True))
+        prob = exponent * (1.0 / jnp.sum(exponent, axis=1, keepdims=True))
+        mine = lane == place.e * experts + expert
+        gate = jnp.sum(jnp.where(mine, prob, 0.0), axis=1, keepdims=True)
+        scaled[expert, here, :] = (
+            gate * grads[expert, here, :].astype(jnp.float32)
+        ).astype(jnp.bfloat16)
+
+        def one_tile(n):
+            cols = span(n * tile, tile)
+            value, slope = gelu_pair(dot_nn(rows[expert, here, :], up[expert, :, cols]))
+            hidden[expert, here, cols] = value.astype(jnp.bfloat16)
+            back = dot_nt(scaled[expert, here, :], down[expert, cols, :])
+            pre[expert, here, cols] = (back * slope).astype(jnp.bfloat16)
+
+        every(0, units // tile, one_tile)
+
+        def one_out(n, total):
+            cols = span(n * wide, wide)
+            value = dot_nn(hidden[expert, here, :], down[expert, :, cols])
+            part_out[expert, here, cols] = (gate * value).astype(jnp.bfloat16)
+            weighted = value * grads[expert, here, cols].astype(jnp.float32)
+            for start in range(0, wide, LANES):
+                total = total + weighted[:, start : start + LANES]
+            return total
+
+        total = lax.fori_loop(
+            0, width // wide, one_out, jnp.zeros((size, LANES), jnp.float32)
+        )
+        grad_gate = jnp.sum(total, axis=1, keepdims=True)
+        grad_logits = (
+            prob * ((jnp.where(mine, 1.0, 0.0) - gate) * grad_gate)
+        ).astype(jnp.bfloat16)
+
+        def one_in(n):
+            cols = span(n * wide, wide)
+            value = dot_nt(pre[expert, here, :], up[expert, cols, :]) + dot_nt(
+                grad_logits, router_ref[cols, :]
+            )
+            part_grad[expert, here, cols] = value.astype(jnp.bfloat16)
+            router_grad[:, cols] += dot_tn(grad_logits, rows[expert, here, cols])
+
+        every(0, width // wide, one_in)
+
+    block = min(256, width)
+
+    def weight_grads(expert, first, last):
+        def one(n):
+            part = span(n * block, block)
+            grad_down[expert, part, :] = dot_tn(
+                hidden[expert, :, part], scaled[expert]
             ).astype(jnp.bfloat16)
-
-            def one_tile(n, carry):
-                cols = pl.ds(pl.multiple_of(n * tile, tile), tile)
-                value, slope = gelu_pair(dot_nn(rows[expert, here, :], up[expert, :, cols]))
-                hidden[expert, here, cols] = value.astype(jnp.bfloat16)
-                back = dot_nt(scaled[expert, here, :], down[expert, cols, :])
-                pre[expert, here, cols] = (back * slope).astype(jnp.bfloat16)
-                return carry
-
-            lax.fori_loop(0, units // tile, one_tile, 0)
-
-            def one_out(n, total):
-                cols = pl.ds(pl.multiple_of(n * wide, wide), wide)
-                value = dot_nn(hidden[expert, here, :], down[expert, :, cols])
-                part_out[expert, here, cols] = (gate * value).astype(jnp.bfloat16)
-                weighted = value * grads[expert, here, cols].astype(jnp.float32)
-                for start in range(0, wide, LANES):
-                    total = total + weighted[:, start : start + LANES]
-                return total
-
-            total = lax.fori_loop(
-                0, width // wide, one_out, jnp.zeros((size, LANES), jnp.float32)
+            grad_up[expert, part, :] = dot_tn(rows[expert, :, part], pre[expert]).astype(
+                jnp.bfloat16
             )
-            grad_gate = jnp.sum(total, axis=1, keepdims=True)
-            grad_logits = (
-                prob * ((jnp.where(mine, 1.0, 0.0) - gate) * grad_gate)
-            ).astype(jnp.bfloat16)
-
-            def one_in(n, carry):
-                cols = pl.ds(pl.multiple_of(n * wide, wide), wide)
-                value = dot_nt(pre[expert, here, :], up[expert, cols, :]) + dot_nt(
-                    grad_logits, router_ref[cols, :]
-                )
-                part_grad[expert, here, cols] = value.astype(jnp.bfloat16)
-                router_grad[:, cols] += dot_tn(grad_logits, rows[expert, here, cols])
-                return carry
-
-            lax.fori_loop(0, width // wide, one_in, 0)
-            return carry
-
-        lax.fori_loop(0, experts, one_expert, 0)
-
-    for k in (0, 1):
-        dispatch.forward(k)
-    for j in range(chunks):
-        if j + 1 < chunks:
-            for k in (2 * j + 2, 2 * j + 3):
-                dispatch.forward(k)
-        for k in (2 * j, 2 * j + 1):
-            dispatch.relay(k)
-        for k in (2 * j, 2 * j + 1):
-            dispatch.ready(k)
-        if j == 0:
-            for load in loads:
-                load.wait()
-        compute(j)
-        ret[0].swap(j)
-        ret[1].swap(j)
-        if j >= 1:
-            ret[0].cross(j - 1)
-        if j >= 2:
-            ret[0].finish(j - 2)
-    ret[0].cross(chunks - 1)
-    stores = [
-        pltpu.make_async_copy(src, dst, load_sem.at[i])
-        for i, (src, dst) in enumerate(
-            [(rows, rows_out), (scaled, scaled_out), (hidden, hidden_out), (pre, pre_out)]
-        )
-    ]
-    for store in stores:
+
+        every(first * width // block // 4, last * width // block // 4, one)
+
+    def keep(expert):
+        return [
+            pltpu.make_async_copy(src.at[expert], dst.at[expert], load_sem.at[2 * expert + i])
+            for i, (src, dst) in enumerate(((grad_up, up_out), (grad_down, down_out)))
+        ]
+
+    def arrive(j):
+        for n in (2 * j, 2 * j + 1):
+            dispatch.relay(n)
+        for n in (2 * j, 2 * j + 1):
+            dispatch.ready(n)
+
+    def forward(j):
+        dispatch.forward(2 * j)
+        dispatch.forward(2 * j + 1)
+
+    forward(0)
+    forward(1)
+    for load in loads:
+        load.wait()
+
+    def step(j):
+        arrive(j)
+        compute(j, 0)
+        pl.when(j + 2 < chunks)(lambda: forward(j + 2))
+        pl.when(j >= 1)(lambda: ret_grad.cross(j - 1))
+
+        @pl.when(j >= 2)
+        def _():
+            ret_grad.finish(j - 2)
+            ret_out.cross(j - 2)
+
+        for expert in range(1, experts):
+            compute(j, expert)
+        ret_grad.swap(j)
+        ret_out.swap(j)
+
+    every(0, chunks, step)
+    weight_grads(0, 0, 1)
+    ret_grad.cross(chunks - 1)
+    ret_out.cross(chunks - 2)
+    ret_grad.finish(chunks - 2)
+    ret_out.cross(chunks - 1)
+    weight_grads(0, 1, 3)
+    every(0, chunks - 2, ret_out.finish)
+    weight_grads(0, 3, 4)
+    for store in keep(0):
         store.start()
-    if chunks >= 2:
-        ret[0].finish(chunks - 2)
-    for j in range(chunks):
-        ret[1].cross(j)
-    ret[0].finish(chunks - 1)
-    for j in range(chunks):
-        ret[1].finish(j)
-    for store in stores:
-        store.wait()
+    ret_grad.finish(chunks - 1)
+    for expert in range(1, experts):
+        weight_grads(expert, 0, 2)
+        if expert == 1:
+            ret_out.finish(chunks - 2)
+        weight_grads(expert, 2, 4)
+        for store in keep(expert):
+            store.start()
+    ret_out.finish(chunks - 1)
+    for expert in range(experts):
+        for store in keep(expert):
+            store.wait()
     dispatch.drain()
-    for each in ret:
-        each.drain()
+    ret_grad.drain(chunks)
+    ret_out.drain(chunks)
 
 
 def run_experts(owners, capacity, expert_count, send_rows, grads, w_up, w_down, router):
@@ -575,8 +620,6 @@
     vmem_spec = pl.BlockSpec(memory_space=pltpu.VMEM)
     bf16 = jnp.bfloat16
     home = jax.ShapeDtypeStruct((owners, experts, capacity, width), bf16)
-    slab = jax.ShapeDtypeStruct((experts, slots, width), bf16)
-    thin = jax.ShapeDtypeStruct((experts, slots, units), bf16)
     dma = pltpu.SemaphoreType.DMA
 
     def vm(*shape):
@@ -585,17 +628,21 @@
     return pl.pallas_call(
         functools.partial(expert_kernel, dims),
         out_shape=(
-            home, home, slab, slab, thin, thin,
+            home, home,
+            jax.ShapeDtypeStruct(w_up.shape, bf16),
+            jax.ShapeDtypeStruct(w_down.shape, bf16),
             jax.ShapeDtypeStruct((LANES, width), jnp.float32),
         ),
         in_specs=[any_spec] * 4 + [vmem_spec],
-        out_specs=(any_spec,) * 6 + (vmem_spec,),
+        out_specs=(any_spec,) * 4 + (vmem_spec,),
         scratch_shapes=[
             vm(experts, slots, width),
             vm(experts, slots, width),
             vm(experts, slots, width),
             vm(experts, slots, units),
             vm(experts, slots, units),
+            vm(experts, width, units),
+            vm(experts, units, width),
             vm(experts, width, units),
             vm(experts, units, width),
             vm(experts, slots, width),
@@ -852,8 +899,6 @@
         scaled, _ = norm_stats(tokens_ref[part, :].astype(jnp.float32))
         act[part, :] = (scaled * gain + shift).astype(jnp.bfloat16)
 
-    every(0, rows // band, norm_band)
-    turned[0] = act[...].T
     columns = weight.shape[1]
     wide = min(512, columns)
 
@@ -870,19 +915,34 @@
         value = total[:, cols] + multiply(place.far, cols) + multiply(place.diag, cols)
         qkv[:, cols] = value.astype(jnp.bfloat16)
 
+    def pass_piece(gather, n):
+        @pl.when(n < pieces)
+        def _():
+            gather.pass_on(n)
+
+        @pl.when(n >= 1)
+        def _():
+            gather.pass_pair(n - 1)
+
+    gathers[0].pass_on(0)
+    every(0, rows // band, norm_band)
+    pass_piece(gathers[0], jnp.int32(1))
+    dispatch.forward(0)
+    turned[0] = act[...].T
     gathers[0].near_ready()
     every(0, columns // wide, first_tile)
-
-    def pass_piece(gather, n):
-        @pl.when(n < pieces)
-        def _():
-            gather.pass_on(n)
-
-        @pl.when(n >= 1)
-        def _():
-            gather.pass_pair(n - 1)
-
-    every(0, pieces + 1, lambda n: pass_piece(gathers[0], n))
+    early = max(pieces - 1, owners // 2)
+
+    def pass_step(n):
+        @pl.when(n <= pieces)
+        def _():
+            pass_piece(gathers[0], n)
+
+        @pl.when(n - 1 < owners)
+        def _():
+            dispatch.forward(n - 1)
+
+    every(2, early + 2, pass_step)
     gathers[0].far_ready()
     every(0, columns // wide, last_tile)
     stores = [
@@ -940,19 +1000,19 @@
         def _():
             attend_pair(i)
 
+        @pl.when(i + early + 1 < owners)
+        def _():
+            dispatch.forward(i + early + 1)
+
+        @pl.when((i >= 1) & (i < pieces + 2))
+        def _():
+            pass_piece(gathers[1], i - 1)
+
         @pl.when(i < owners)
         def _():
-            dispatch.forward(i)
-
-        @pl.when((i >= 1) & (i < pieces + 2))
-        def _():
-            pass_piece(gathers[1], i - 1)
-
-        @pl.when((i >= 2) & (i < owners + 2))
-        def _():
-            dispatch.relay(i - 2)
-
-    every(0, max(pairs, owners + 2), attend_step)
+            dispatch.relay(i)
+
+    every(0, max(pairs, owners, pieces + 2), attend_step)
     turned[1] = merged[...].T
     stores[4].start()
     gathers[1].near_ready()
@@ -1760,11 +1820,9 @@
     )
     router = jnp.transpose(vectors[:, 4:lead], (0, 2, 1)).reshape(model_width, expert_count)
     router = jnp.pad(router, ((0, 0), (0, LANES - expert_count)))
-    home_out, home_grad, rows, scaled, act_hidden, grad_pre, grad_router = run_experts(
+    home_out, home_grad, grad_up, grad_down, grad_router = run_experts(
         owners, capacity, expert_count, send_rows, grad_rows, w_up, w_down, router
     )
-    grad_down = jnp.einsum("erf,erd->efd", act_hidden, scaled, preferred_element_type=jnp.float32)
-    grad_up = jnp.einsum("erd,erf->edf", rows, grad_pre, preferred_element_type=jnp.float32)
     output, grad_tokens, small_total, qkv_total, out_total = run_back(
         owners, lead + -lead % 8, home_grad.reshape(-1, model_width),
         home_out.reshape(-1, model_width), back, hidden, cotangent, tokens, vectors, grad_router,
@@ -1780,8 +1838,8 @@
         small_total[2],
         small_total[3],
         small_total[4:lead].T,
-        grad_up,
-        grad_down,
+        grad_up.astype(jnp.float32),
+        grad_down.astype(jnp.float32),
     )
 
 
@@ -1806,7 +1864,7 @@
 
     def body(*args):
         capacity = args[0].shape[0] // args[7].shape[1]
-        fits = group == 4 and owners % 2 == 0 and capacity % 16 == 0
+        fits = group == 4 and owners in (4, 8, 16) and capacity % 16 == 0
         return (on_device if fits else on_device_plain)(*args)
 
     return jax.shard_map(

time: 339 us -> 301 us (0.89)
  Pallas kernels: 303 us -> 272 us
  matrix products: 16.2 us -> 0 us
  other arithmetic: 5.56 us -> 14.4 us
    pallas_call x1, Pallas kernels: 126 us -> 104 us  [run_experts(): pl.pallas_call(functools.partial(expert_kernel, dims), out_shape=(home, h...]
    dot_general x2 -> x0, matrix products: 16.2 us -> none  [the longest x1 9.38 us: on_device(): jnp.einsum('erd,erf->edf', rows, grad_pre, preferred_element_type=jnp.flo...]
    pallas_call x1, Pallas kernels: 76.9 us -> 67.9 us  [run_front(): pl.pallas_call(functools.partial(front_kernel, (owners, capacity, pieces)...]
    convert_element_type x0 -> x2, other arithmetic: none -> 8.88 us  [the longest x1 4.44 us: on_device(): grad_up.astype(jnp.float32)]
where the time goes in v1:
time: 301 us; the launch traced here: 300 us
  Pallas kernels  272 us (90%)
  other arithmetic  14.4 us (5%)
  local copies, waits for them, and re-layouts  12.5 us (4%)
    pallas_call x1, Pallas kernels, run_experts(): pl.pallas_call(functools.partial(expert_kernel, dims), out_shape=(home, h...  104 us
    pallas_call x1, Pallas kernels, run_back(): pl.pallas_call(functools.partial(back_kernel, (owners,)), out_shape=(jax....  100 us
    pallas_call x1, Pallas kernels, run_front(): pl.pallas_call(functools.partial(front_kernel, (owners, capacity, pieces)...  67.9 us

profile of v1, /device:TPU:0, one launch (start us, length us, event | category | flops | bytes accessed | tf_op | source)
XLA Modules:
  0.0 300.1 jit_solution(18440841076537724538)
XLA Ops:
  1.3 0.7 broadcast_in_dim.12
  1.9 0.7 broadcast_in_dim.13
  2.6 0.7 broadcast_in_dim.14
  3.3 0.7 broadcast_in_dim.15
  3.9 0.8 concatenate.3
  4.8 0.6 pad.8.small_hbm
  5.4 1.5 copy.25.routes_ref
  6.9 67.9 %front.1 = (bf16[512,3072]{1,0:T(8,128)(2,1)}, bf16[1024,512]{1,0:T(8,128)(2,1)}, bf16[1024,512]{1,0:T(8,128)(2,1)}, bf16[512,512]{1,0:T(8,128)(2,1)}, bf16[1024...) custom-call(s32[1]{0:T(128)S(6)} %copy.29.prefix_ref, ...), custom_call_target="tpu_custom_call" | custom-call | tf_op jit(solution)/shard_map/front/pallas_call | solution.py:1063
  74.8 0.8 slice_bitcast_fusion
  75.6 0.2 copy.26
  75.8 0.8 pad.9.router_ref
  76.5 103.7 %experts.1 = (bf16[8,2,32,1024]{3,2,1,0:T(8,128)(2,1)}, bf16[8,2,32,1024]{3,2,1,0:T(8,128)(2,1)}, bf16[2,1024,1024]{2,1,0:T(8,128)(2,1)}, bf16[2,1024,1024]{2,1,0:T(8,128)(2,1)}, f32[128,1024]{1,0:T(8,128)}) custom-call(bf16[8,2,32,1024]{3,2,1,0:T(8,128)(2,1)} %get-tuple-element.33.send_ref, bf16[2,1024,1024]{2,1,0:T(8,128)(2,1)} %get-tuple-element.34.grads_hbm, ...), custom_call_target="tpu_custom_call" | custom-call | tf_op jit(solution)/shard_map/experts/pallas_call | solution.py:628
  180.3 100.2 %back.1 = (bf16[512,1024]{1,0:T(8,128)(2,1)}, f32[512,1024]{1,0:T(8,128)}, f32[24,256]{1,0:T(8,128)}, bf16[256,3072]{1,0:T(8,128)(2,1)}, bf16[256,1024]{1,0:T(8,128)(2,1)}) custom-call(bf16[512,1024]{1,0:T(8,128)(2,1)} %bitcast.14, bf16[512,1024]{1,0:T(8,128)(2,1)} %bitcast.13, bf16[512,512]{1,0:T(8,128)(2,1)} %get-tuple-element.38.back_ref, ...), custom_call_target="tpu_custom_call" | custom-call | tf_op jit(solution)/shard_map/back/pallas_call | solution.py:1558
  280.5 0.0 copy-start.1
  280.5 1.5 fusion
  282.0 1.3 slice_bitcast_fusion.1
  283.3 2.1 convert_element_type.17
  285.5 3.4 %convert_element_type.16 = f32[256,3072]{1,0:T(8,128)} convert(bf16[256,3072]{1,0:T(8,128)(2,1)} %get-tuple-element.51) | non-fusion elementwise | flops 786432 | bytes 4718592 | tf_op jit(solution)/shard_map/convert_element_type | solution.py:1836
  288.9 0.0 copy-done.1
  288.9 0.0 copy-start
  288.9 4.4 %convert_element_type.18 = f32[2,1024,1024]{2,1,0:T(8,128)} convert(bf16[2,1024,1024]{2,1,0:T(8,128)(2,1)S(1)} %copy-done.1) | non-fusion elementwise | flops 2097152 | bytes 12582912 | tf_op jit(solution)/shard_map/convert_element_type | solution.py:1841
  293.3 0.0 copy-done
  293.3 0.0 copy-start.3
  293.3 0.0 copy-start.2
  293.3 4.4 %convert_element_type.19 = f32[2,1024,1024]{2,1,0:T(8,128)} convert(bf16[2,1024,1024]{2,1,0:T(8,128)(2,1)S(1)} %copy-done) | non-fusion elementwise | flops 2097152 | bytes 12582912 | tf_op jit(solution)/shard_map/convert_element_type | solution.py:1842
  297.8 0.0 copy-done.3
  297.8 1.0 copy.30
  298.8 0.0 copy-done.2
  298.8 1.3 copy.31
Async XLA Ops:
  280.5 8.4 %copy-start.1 = (bf16[2,1024,1024]{2,1,0:T(8,128)(2,1)S(1)}, bf16[2,1024,1024]{2,1,0:T(8,128)(2,1)}, u32[]{:S(2)}) copy-start(bf16[2,1024,1024]{2,1,0:T(8,128)(2,1)} %get-tuple-element.53) | copy-start | bytes 12582916
  288.9 4.4 %copy-start = (bf16[2,1024,1024]{2,1,0:T(8,128)(2,1)S(1)}, bf16[2,1024,1024]{2,1,0:T(8,128)(2,1)}, u32[]{:S(2)}) copy-start(bf16[2,1024,1024]{2,1,0:T(8,128)(2,1)} %get-tuple-element.54) | copy-start | bytes 12582916
  293.3 4.4 %copy-start.3 = (bf16[512,1024]{1,0:T(8,128)(2,1)S(1)}, bf16[512,1024]{1,0:T(8,128)(2,1)}, u32[]{:S(2)}) copy-start(bf16[512,1024]{1,0:T(8,128)(2,1)} %get-tuple-element.70) | copy-start | bytes 3145732
  293.3 5.4 %copy-start.2 = (f32[512,1024]{1,0:T(8,128)S(1)}, f32[512,1024]{1,0:T(8,128)}, u32[]{:S(2)}) copy-start(f32[512,1024]{1,0:T(8,128)} %get-tuple-element.71) | copy-start | bytes 6291460

commit v2 on v1

--- a/solution.py
+++ b/solution.py
@@ -396,6 +396,13 @@
     def swap(self, j):
         self.swapped(j).start()
 
+    def split(self, j):
+        self.swapped(j).wait_recv()
+        here = span(j * 2 * self.cap, 2 * self.cap)
+        for expert in range(self.experts):
+            self.mid[expert, here, :] = self.pair_sum(expert, j, 1 - self.p.x).astype(jnp.bfloat16)
+            self.far[expert, here, :] = self.pair_sum(expert, j, self.p.x).astype(jnp.bfloat16)
+
     def cross(self, j):
         self.swapped(j).wait_recv()
         size = 2 * self.cap
@@ -405,11 +412,14 @@
             ).astype(jnp.bfloat16)
         self.crossed(j).start()
 
+    def this_side(self, expert, j):
+        return self.pair_sum(expert, j, self.p.x)
+
     def finish(self, j):
         self.crossed(j).wait_recv()
         size = 2 * self.cap
         for expert in range(self.experts):
-            total = self.pair_sum(expert, j, self.p.x) + self.far[
+            total = self.this_side(expert, j) + self.far[
                 expert, span(j * size, size), :
             ].astype(jnp.float32)
             total = total.astype(jnp.bfloat16)
@@ -419,14 +429,32 @@
         self.homed(2 * j + 1).start()
         either(j == 0, lambda: self.own().start(), lambda: self.homed(2 * j).start())
 
+    def drain_swaps(self, chunks):
+        every(0, chunks, lambda j: self.swapped(j).wait_send())
+
     def drain(self, chunks):
-        def one(j):
-            self.swapped(j).wait_send()
-            self.crossed(j).wait_send()
-
-        every(0, chunks, one)
+        every(0, chunks, lambda j: self.crossed(j).wait_send())
+        every(1, self.p.owners, lambda n: self.homed(n).wait_send())
+
+    def arrived(self):
         self.own().wait()
-        every(1, self.p.owners, lambda n: self.homed(n).wait())
+        every(1, self.p.owners, lambda n: self.homed(n).wait_recv())
+
+
+class LateReturn(Return):
+    def crossed(self, j):
+        part = span(j * 2 * self.cap, 2 * self.cap)
+        return remote(
+            self.mid.at[:, part],
+            self.far.at[:, part],
+            self.send.at[j],
+            self.recv.at[j],
+            (self.p.e, self.p.far),
+        )
+
+    def this_side(self, expert, j):
+        size = 2 * self.cap
+        return self.part[expert, span(j * size, size), :].astype(jnp.float32)
 
 
 def gelu_pair(v):
@@ -441,10 +469,10 @@
 def expert_kernel(
     dims,
     send_ref, grads_hbm, up_hbm, down_hbm, router_ref,
-    home_out, home_grad, up_out, down_out, router_grad,
+    far_sums, near_sums, home_grad, up_out, down_out, router_grad,
     rows, grads, scaled, hidden, pre, up, down, grad_up, grad_down,
     part_out, part_grad, got_out, got_grad, mid_out, mid_grad,
-    far_out, far_grad, done_out, done_grad,
+    keep_out, far_grad, done_grad,
     load_sem, own_sem, disp_send, disp_recv, red_send, red_recv, home_send, home_recv,
 ):
     owners, experts, capacity, width, units, expert_count = dims
@@ -464,18 +492,14 @@
     dispatch = Dispatch(
         place, capacity, send_ref, rows, (own_sem.at[0], disp_send, disp_recv)
     )
-    ret_grad, ret_out = [
-        Return(
-            place, capacity, experts, part, got, mid, far, done, home,
-            (own_sem.at[1 + i], red_send.at[i], red_recv.at[i], home_send.at[i], home_recv.at[i]),
-        )
-        for i, (part, got, mid, far, done, home) in enumerate(
-            [
-                (part_grad, got_grad, mid_grad, far_grad, done_grad, home_grad),
-                (part_out, got_out, mid_out, far_out, done_out, home_out),
-            ]
-        )
-    ]
+    ret_grad = Return(
+        place, capacity, experts, part_grad, got_grad, mid_grad, far_grad, done_grad, home_grad,
+        (own_sem.at[1], red_send.at[0], red_recv.at[0], home_send, home_recv),
+    )
+    ret_out = Return(
+        place, capacity, experts, part_out, got_out, mid_out, keep_out, None, None,
+        (None, red_send.at[1], red_recv.at[1], None, None),
+    )
     dispatch.start()
     router_grad[...] = jnp.zeros_like(router_grad)
     tile = min(TILE, units)
@@ -486,7 +510,7 @@
 
     def compute(j, expert):
         here = span(j * size, size)
-        logits = dot_nn(rows[expert, here, :], router_ref[...])
+        logits = dot_nt(rows[expert, here, :], router_ref[...])
         logits = jnp.where(lane < expert_count, logits, -1e30)
         exponent = jnp.exp(logits - jnp.max(logits, axis=1, keepdims=True))
         prob = exponent * (1.0 / jnp.sum(exponent, axis=1, keepdims=True))
@@ -524,8 +548,8 @@
 
         def one_in(n):
             cols = span(n * wide, wide)
-            value = dot_nt(pre[expert, here, :], up[expert, cols, :]) + dot_nt(
-                grad_logits, router_ref[cols, :]
+            value = dot_nt(pre[expert, here, :], up[expert, cols, :]) + dot_nn(
+                grad_logits, router_ref[:, cols]
             )
             part_grad[expert, here, cols] = value.astype(jnp.bfloat16)
             router_grad[:, cols] += dot_tn(grad_logits, rows[expert, here, cols])
@@ -571,12 +595,13 @@
         arrive(j)
         compute(j, 0)
         pl.when(j + 2 < chunks)(lambda: forward(j + 2))
-        pl.when(j >= 1)(lambda: ret_grad.cross(j - 1))
-
-        @pl.when(j >= 2)
+
+        @pl.when(j >= 1)
         def _():
-            ret_grad.finish(j - 2)
-            ret_out.cross(j - 2)
+            ret_grad.cross(j - 1)
+            ret_out.split(j - 1)
+
+        pl.when(j >= 2)(lambda: ret_grad.finish(j - 2))
 
         for expert in range(1, experts):
             compute(j, expert)
@@ -586,29 +611,33 @@
     every(0, chunks, step)
     weight_grads(0, 0, 1)
     ret_grad.cross(chunks - 1)
-    ret_out.cross(chunks - 2)
+    ret_out.split(chunks - 1)
+    sums = [
+        pltpu.make_async_copy(src, dst, load_sem.at[4 + i])
+        for i, (src, dst) in enumerate(((mid_out, far_sums), (keep_out, near_sums)))
+    ]
+    for store in sums:
+        store.start()
     ret_grad.finish(chunks - 2)
-    ret_out.cross(chunks - 1)
     weight_grads(0, 1, 3)
-    every(0, chunks - 2, ret_out.finish)
+    ret_grad.finish(chunks - 1)
     weight_grads(0, 3, 4)
     for store in keep(0):
         store.start()
-    ret_grad.finish(chunks - 1)
     for expert in range(1, experts):
-        weight_grads(expert, 0, 2)
-        if expert == 1:
-            ret_out.finish(chunks - 2)
-        weight_grads(expert, 2, 4)
+        weight_grads(expert, 0, 4)
         for store in keep(expert):
             store.start()
-    ret_out.finish(chunks - 1)
     for expert in range(experts):
         for store in keep(expert):
             store.wait()
+    for store in sums:
+        store.wait()
     dispatch.drain()
+    ret_grad.drain_swaps(chunks)
     ret_grad.drain(chunks)
-    ret_out.drain(chunks)
+    ret_grad.arrived()
+    ret_out.drain_swaps(chunks)
 
 
 def run_experts(owners, capacity, expert_count, send_rows, grads, w_up, w_down, router):
@@ -628,13 +657,15 @@
     return pl.pallas_call(
         functools.partial(expert_kernel, dims),
         out_shape=(
-            home, home,
+            jax.ShapeDtypeStruct((experts, slots // 4, width), bf16),
+            jax.ShapeDtypeStruct((experts, slots // 4, width), bf16),
+            home,
             jax.ShapeDtypeStruct(w_up.shape, bf16),
             jax.ShapeDtypeStruct(w_down.shape, bf16),
             jax.ShapeDtypeStruct((LANES, width), jnp.float32),
         ),
         in_specs=[any_spec] * 4 + [vmem_spec],
-        out_specs=(any_spec,) * 4 + (vmem_spec,),
+        out_specs=(any_spec,) * 5 + (vmem_spec,),
         scratch_shapes=[
             vm(experts, slots, width),
             vm(experts, slots, width),
@@ -654,15 +685,14 @@
             vm(experts, slots // 4, width),
             vm(experts, slots // 4, width),
             vm(owners, experts, capacity, width),
-            vm(owners, experts, capacity, width),
-            dma((4,)),
-            dma((3,)),
+            dma((6,)),
+            dma((2,)),
             dma((4, owners)),
             dma((4, owners)),
             dma((2, 2, chunks)),
             dma((2, 2, chunks)),
-            dma((2, owners)),
-            dma((2, owners)),
+            dma((owners,)),
+            dma((owners,)),
         ],
         compiler_params=pltpu.CompilerParams(
             collective_id=1, has_side_effects=True, vmem_limit_bytes=VMEM_LIMIT
@@ -801,13 +831,13 @@
 
 
 def slot_tables(routes_ref, priority_ref, capacity, pick_ref, back_ref):
-    count = routes_ref.shape[0]
+    count = routes_ref.shape[1]
     row = lax.broadcasted_iota(jnp.int32, (count, count), 0).astype(jnp.float32)
     col = lax.broadcasted_iota(jnp.int32, (count, count), 1).astype(jnp.float32)
     eye = row == col
-    route_col = routes_ref[...].astype(jnp.float32)
+    route_row = routes_ref[...].astype(jnp.float32)
     order_row = priority_ref[...].astype(jnp.float32)
-    route_row = jnp.sum(jnp.where(eye, route_col, 0.0), axis=0, keepdims=True)
+    route_col = jnp.sum(jnp.where(eye, route_row, 0.0), axis=1, keepdims=True)
     order_col = jnp.sum(jnp.where(eye, order_row, 0.0), axis=1, keepdims=True)
     same = route_col == route_row
     rank_row = jnp.sum(
@@ -831,9 +861,9 @@
 
 def front_kernel(
     dims,
-    prefix_ref, routes_ref, priority_ref, tokens_ref, cot_ref, small_hbm, qkv_hbm, out_hbm,
+    prefix_ref, routes_ref, priority_ref, tokens_ref, cot_ref, small_hbm, router_hbm, qkv_hbm, out_hbm,
     qkv_out, act_out, merged_out, back_out, weight_out, out_full, low_out, high_out, grads_rows,
-    hidden_ref, send_ref, small_out,
+    hidden_ref, send_ref, small_out, router_out,
     small, weight, out_w, total, qkv, act, merged, act_two, turned, pick, back, grads_send, low_buf, high_buf,
     own_sem, disp_send, disp_recv, small_send, small_recv, near_send, near_recv,
     gat_send, gat_recv, store_sem, prob_sem,
@@ -851,15 +881,25 @@
     ]
     for gather in gathers:
         gather.own().start()
-    own_small = pltpu.make_async_copy(small_hbm, small.at[place.w], own_sem.at[3])
-    own_small.start()
+    vectors, gates = small_hbm.shape[0], router_hbm.shape[0]
+    small_parts = [
+        (small_hbm, small.at[place.w, pl.ds(0, vectors)]),
+        (router_hbm, small.at[place.w, pl.ds(vectors, gates)]),
+    ]
+    own_smalls = [
+        pltpu.make_async_copy(src, dst, own_sem.at[3 + i])
+        for i, (src, dst) in enumerate(small_parts)
+    ]
+    for copy in own_smalls:
+        copy.start()
     greet(
         [(place.ahead(k), place.w) for k in range(1, owners)]
         + [(place.e, place.sib), (place.e, place.far), (place.e, place.diag)]
     )
     smalls = [
-        remote(small_hbm, small.at[place.w], small_send.at[i], small_recv.at[i], (place.e, peer))
+        remote(src, dst, small_send.at[n, i], small_recv.at[n, i], (place.e, peer))
         for i, peer in enumerate((place.sib, place.far, place.diag))
+        for n, (src, dst) in enumerate(small_parts)
     ]
     for copy in smalls:
         copy.start()
@@ -882,10 +922,15 @@
         place, capacity, grads_send, grads_rows, (own_sem.at[0], disp_send, disp_recv)
     )
     dispatch.start()
-    own_small.wait()
+    for copy in own_smalls:
+        copy.wait()
     for copy in smalls:
         copy.wait_recv()
-    small_out[...] = small[...]
+    small_out[...] = small[:, :vectors, :]
+    router_out[...] = jnp.zeros_like(router_out)
+    router_out[:gates, :] = jnp.concatenate(
+        [small[i, vectors:, :] for i in range(4)], axis=1
+    )
 
     def vector(which):
         parts = [small[i, which : which + 1, :] for i in range(4)]
@@ -1043,7 +1088,9 @@
     dispatch.drain()
 
 
-def run_front(owners, experts, capacity, prefix, routes, priority, tokens, cotangent, small, w_qkv, w_out):
+def run_front(
+    owners, experts, capacity, prefix, routes, priority, tokens, cotangent, small, router, w_qkv, w_out
+):
     rows, width = tokens.shape
     shard, columns = w_qkv.shape
     half = rows // 2
@@ -1075,11 +1122,12 @@
             jax.ShapeDtypeStruct((rows, width), f32),
             out(owners, experts, capacity, width),
             out(4, *small.shape),
+            out(LANES, width),
         ),
-        in_specs=[pl.BlockSpec(memory_space=pltpu.SMEM)] + [vmem_spec] * 4 + [any_spec] * 3,
-        out_specs=(any_spec,) * 9 + (vmem_spec,) * 3,
+        in_specs=[pl.BlockSpec(memory_space=pltpu.SMEM)] + [vmem_spec] * 4 + [any_spec] * 4,
+        out_specs=(any_spec,) * 9 + (vmem_spec,) * 4,
         scratch_shapes=[
-            vm(4, *small.shape),
+            vm(4, small.shape[0] + router.shape[0], shard),
             vm(4 * shard, columns),
             vm(4 * shard, width),
             pltpu.VMEM((rows, columns), f32),
@@ -1093,11 +1141,11 @@
             vm(owners, experts, capacity, width),
             vm(2, 2, half, half),
             vm(2, 2, half, rows),
-            dma((4,)),
+            dma((5,)),
             dma((4, owners)),
             dma((4, owners)),
-            dma((3,)),
-            dma((3,)),
+            dma((2, 3)),
+            dma((2, 3)),
             dma((2,)),
             dma((2,)),
             dma((2, 4, pieces)),
@@ -1109,7 +1157,7 @@
             collective_id=0, has_side_effects=True, vmem_limit_bytes=VMEM_LIMIT
         ),
         name="front",
-    )(prefix, routes, priority, tokens, cotangent, small, w_qkv, w_out)
+    )(prefix, routes, priority, tokens, cotangent, small, router, w_qkv, w_out)
 
 
 class Reduce:
@@ -1274,7 +1322,9 @@
         for k in range(1, self.p.owners):
             self.spreads(k).wait_recv()
             total = total + self.others[k]
-        self.out[...] = total
+        vectors_out, gates_out = self.out
+        vectors_out[...] = total[: vectors_out.shape[0]]
+        gates_out[...] = total[vectors_out.shape[0] :]
 
     def drain(self):
         self.swapped().wait_send()
@@ -1292,23 +1342,25 @@
 
 def back_kernel(
     dims,
-    home_grad_ref, home_out_ref, back_ref, hidden_ref, cot_ref, tokens_ref, vectors_ref, router_ref,
-    act_hbm, merged_hbm, qkv_hbm, weight_hbm, out_hbm, low_hbm, high_hbm,
-    output_ref, tokens_out, small_out, qkv_out, out_out,
-    act_t, merged_t, qkv, weight, out_w, low_buf, high_buf, attn, grad_merged, grad_qkv,
+    home_grad_ref, back_ref, hidden_ref, cot_ref, tokens_ref, vectors_ref, router_ref,
+    far_hbm, near_hbm, act_hbm, merged_hbm, qkv_hbm, weight_hbm, out_hbm, low_hbm, high_hbm,
+    output_ref, tokens_out, vectors_out, gates_out, qkv_out, out_out,
+    near_sums, far_sums, done_rows, home_out,
+    act_t, merged_t, qkv, weight, out_w, low_buf, high_buf, attn, grad_merged, wide_q, wide_o,
     part_q, got_q, far_q, pair_q, lines_q, done_q,
     part_o, got_o, far_o, pair_o, lines_o, done_o,
     small, small_part, small_got, small_mid, small_far, small_sum, small_all,
-    load_sem, prob_sem, send_q, recv_q, lsend_q, lrecv_q, send_o, recv_o, lsend_o, lrecv_o,
+    load_sem, prob_sem, own_sem, cross_send, cross_recv, home_send, home_recv, send_q, recv_q, lsend_q, lrecv_q, send_o, recv_o, lsend_o, lrecv_o,
     small_send, small_recv, all_send, all_recv, out_sem,
 ):
-    (owners,) = dims
+    owners, capacity, gates = dims
+    grad_qkv = qkv
     place = Place(owners)
     loads = [
         pltpu.make_async_copy(src, dst, load_sem.at[i])
         for i, (src, dst) in enumerate(
             [(merged_hbm, merged_t), (out_hbm, out_w), (qkv_hbm, qkv), (act_hbm, act_t),
-             (weight_hbm, weight)]
+             (weight_hbm, weight), (near_hbm, near_sums)]
         )
     ]
 
@@ -1331,6 +1383,13 @@
         [(place.ahead(k), place.w) for k in range(1, owners)]
         + [(place.e, place.sib), (place.e, place.far)]
     )
+    experts = near_sums.shape[0]
+    groups = owners // 2
+    late = LateReturn(
+        place, capacity, experts, near_sums, None, far_hbm, far_sums, done_rows, home_out,
+        (own_sem, cross_send, cross_recv, home_send, home_recv),
+    )
+    every(0, groups, lambda j: late.crossed(j).start())
     reduce_o = Reduce(
         place, part_o, got_o, far_o, pair_o, lines_o, done_o, (send_o, recv_o, lsend_o, lrecv_o)
     )
@@ -1338,7 +1397,7 @@
         place, part_q, got_q, far_q, pair_q, lines_q, done_q, (send_q, recv_q, lsend_q, lrecv_q)
     )
     smalls = Small(
-        place, small, small_part, small_got, small_mid, small_far, small_sum, small_all, small_out,
+        place, small, small_part, small_got, small_mid, small_far, small_sum, small_all, (vectors_out, gates_out),
         (small_send, small_recv, all_send, all_recv),
     )
     rows, width = tokens_ref.shape
@@ -1351,12 +1410,12 @@
         return jnp.concatenate(parts, axis=1).astype(jnp.float32)
 
     gain_one, gain_two = vector(0), vector(2)
-    small[0:4, :] = jnp.zeros((4, width), jnp.float32)
-    small[4:lead, :] = router_ref[0 : lead - 4, :]
+    small[: lead - gates, :] = jnp.zeros((lead - gates, width), jnp.float32)
+    small[lead - gates :, :] = router_ref[:gates, :]
 
     def post(i):
         part = span(i * band, band)
-        grad = dot_nn(back_ref[part, :], home_grad_ref[...])
+        grad = dot_nn(back_ref[part, :], home_grad_ref.reshape(rows, width)[...])
         scaled, inverse = norm_stats(hidden_ref[part, :])
         value = cot_ref[part, :].astype(jnp.float32) + norm_back_rows(
             grad, scaled, inverse, gain_two
@@ -1388,7 +1447,7 @@
         grad_merged[part, :] = dot_nt(attn[part, :], out_w[...]).astype(jnp.bfloat16)
 
     every(0, rows // band, merged_band)
-    for load in loads[2:4]:
+    for load in loads[2:4] + loads[5:]:
         load.wait()
     pairs = part_q.shape[0]
 
@@ -1436,13 +1495,14 @@
 
     def output_band(i):
         part = span(i * band, band)
-        value = hidden_ref[part, :] + dot_nn(back_ref[part, :], home_out_ref[...])
+        slots = home_out.reshape(rows, width)
+        value = hidden_ref[part, :] + dot_nn(back_ref[part, :], slots[...])
         output_ref[part, :] = value.astype(jnp.bfloat16)
 
     def store_q(i):
         return [
             pltpu.make_async_copy(
-                done_q.at[i, :, pl.ds(which * LANES, LANES)],
+                wide_q.at[i, :, pl.ds(which * LANES, LANES)],
                 qkv_out.at[:, span(which * width + i * LANES, LANES)],
                 out_sem.at[which, i],
             )
@@ -1451,61 +1511,53 @@
 
     def store_o(n):
         return pltpu.make_async_copy(
-            done_o.at[n], out_out.at[:, span(n * tile_o, tile_o)], out_sem.at[3, n]
+            wide_o.at[n], out_out.at[:, span(n * tile_o, tile_o)], out_sem.at[3, n]
         )
 
     stages_o, stages_q = reduce_o.stages(), reduce_q.stages()
-    depth = len(stages_q)
+    delays = (1, 3, 4, 5, 6, 7)
+    last = len(delays) - 1
+    half = rows // band // 2
 
     def slot_step(slot):
-        for s in range(depth - 1, -1, -1):
-            n = slot - 1 - s
+        pl.when(slot < groups)(lambda: late.finish(slot))
+        pl.when(slot < pairs)(lambda: attend_pair(slot))
+        for s in range(last, -1, -1):
+            n = slot - delays[s]
 
             @pl.when((n >= 0) & (n < pairs))
             def _(s=s, n=n):
                 stages_q[s](n)
-                if s == depth - 1:
+                if s == last:
+                    wide_q[n] = done_q[n].astype(jnp.float32)
                     for copy in store_q(n):
                         copy.start()
 
-            @pl.when(slot == s)
+            @pl.when(slot == delays[s] - 1)
             def _(s=s):
                 for n in range(out_chunks):
                     stages_o[s](n)
-                    if s == depth - 1:
+                    if s == last:
+                        wide_o[n] = done_o[n].astype(jnp.float32)
                         store_o(n).start()
-
-        @pl.when(slot < pairs)
-        def _():
-            attend_pair(slot)
 
         @pl.when(slot == pairs)
         def _():
             loads[4].wait()
-            every(0, rows // band // 2, input_band)
-
-        @pl.when(slot == pairs + 1)
-        def _():
-            every(rows // band // 2, rows // band, input_band)
-
-        @pl.when(slot == pairs + 2)
-        def _():
-            smalls.swap()
-            every(0, rows // band, output_band)
+            every(0, half, input_band)
+
+        pl.when(slot == pairs + 1)(lambda: every(half, 2 * half, input_band))
+        pl.when(slot == pairs + 2)(smalls.swap)
+        pl.when(slot == pairs + 3)(smalls.cross)
+        pl.when(slot == pairs + 4)(smalls.spread)
 
         @pl.when(slot == pairs + 3)
         def _():
-            smalls.cross()
-
-        @pl.when(slot == pairs + 4)
-        def _():
-            smalls.spread()
-
-        @pl.when(slot == pairs + 5)
-        def _():
-            smalls.finish()
-
-    every(0, pairs + depth, slot_step)
+            late.arrived()
+            every(0, rows // band, output_band)
+
+    every(0, pairs + delays[-1], slot_step)
+    smalls.finish()
 
     def stored(i):
         for copy in store_q(i):
@@ -1514,17 +1566,20 @@
     every(0, pairs, stored)
     for n in range(out_chunks):
         store_o(n).wait()
+    late.drain(groups)
     reduce_o.drain()
     reduce_q.drain()
     smalls.drain()
 
 
 def run_back(
-    owners, lead, home_grad, home_out, back, hidden, cotangent, tokens, vectors, router_grad,
-    act_t, merged_t, qkv, weight, w_out, low, high,
+    owners, capacity, gates, home_grad, far_sums, near_sums, back, hidden, cotangent, tokens,
+    vectors, router_grad, act_t, merged_t, qkv, weight, w_out, low, high,
 ):
     rows, width = tokens.shape
     shard = width // 4
+    lead = 8 + gates
+    groups = owners // 2
     pairs = width // LANES
     tile_o = min(512, width)
     out_chunks = width // tile_o
@@ -1556,17 +1611,22 @@
         return [dma((4, chunks)), dma((4, chunks)), dma((2, chunks, count)), dma((2, chunks, count))]
 
     return pl.pallas_call(
-        functools.partial(back_kernel, (owners,)),
+        functools.partial(back_kernel, (owners, capacity, gates)),
         out_shape=(
             jax.ShapeDtypeStruct((rows, width), bf16),
             jax.ShapeDtypeStruct((rows, width), f32),
-            jax.ShapeDtypeStruct((lead, shard), f32),
-            jax.ShapeDtypeStruct((shard, 3 * width), bf16),
-            jax.ShapeDtypeStruct((shard, width), bf16),
+            jax.ShapeDtypeStruct((8, shard), f32),
+            jax.ShapeDtypeStruct((gates, shard), f32),
+            jax.ShapeDtypeStruct((shard, 3 * width), f32),
+            jax.ShapeDtypeStruct((shard, width), f32),
         ),
-        in_specs=[vmem_spec] * 8 + [any_spec] * 7,
-        out_specs=(vmem_spec,) * 3 + (any_spec,) * 2,
+        in_specs=[vmem_spec] * 7 + [any_spec] * 9,
+        out_specs=(vmem_spec,) * 4 + (any_spec,) * 2,
         scratch_shapes=[
+            vm(*near_sums.shape),
+            vm(*near_sums.shape),
+            vm(*home_grad.shape),
+            vm(*home_grad.shape),
             vm(width, rows),
             vm(width, rows),
             vm(rows, 3 * width),
@@ -1576,7 +1636,8 @@
             vm(2, 2, mid, rows),
             vm(rows, width),
             vm(rows, width),
-            vm(rows, 3 * width),
+            fm(pairs, shard, 3 * LANES),
+            fm(out_chunks, shard, tile_o),
         ]
         + reduce_buffers(pairs, 3 * LANES)
         + reduce_buffers(out_chunks, tile_o)
@@ -1588,8 +1649,13 @@
             fm(lead, shard),
             fm(lead, shard),
             fm(owners, lead, shard),
-            dma((5,)),
+            dma((6,)),
             dma((2, 2)),
+            dma(()),
+            dma((groups,)),
+            dma((groups,)),
+            dma((owners,)),
+            dma((owners,)),
         ]
         + reduce_sems(pairs)
         + reduce_sems(out_chunks)
@@ -1599,8 +1665,8 @@
         ),
         name="back",
     )(
-        home_grad, home_out, back, hidden, cotangent, tokens, vectors, router_grad,
-        act_t, merged_t, qkv, weight, w_out, low, high,
+        home_grad, back, hidden, cotangent, tokens, vectors, router_grad,
+        far_sums, near_sums, act_t, merged_t, qkv, weight, w_out, low, high,
     )
 
 
@@ -1806,38 +1872,34 @@
     capacity = row_count // expert_count
     owners = lax.axis_size("expert")
     experts = w_up.shape[0]
-    small = jnp.concatenate(
-        [norm1_gain[None], norm1_shift[None], norm2_gain[None], norm2_shift[None], w_router.T],
-        axis=0,
-    )
-    lead = small.shape[0]
-    small = jnp.pad(small, ((0, -lead % 16), (0, 0)))
+    which = lax.broadcasted_iota(jnp.int32, (16, norm1_gain.shape[0]), 0)
+    small = jnp.zeros(which.shape, jnp.bfloat16)
+    for i, vector in enumerate((norm1_gain, norm1_shift, norm2_gain, norm2_shift)):
+        small = jnp.where(which == i, vector[None], small)
     (
         qkv, act_t, merged_t, back, weight, out_full, low, high, grad_rows, hidden, send_rows,
-        vectors,
+        vectors, router,
     ) = run_front(
-        owners, experts, capacity, prefix, routes, priority, tokens, cotangent, small, w_qkv, w_out
-    )
-    router = jnp.transpose(vectors[:, 4:lead], (0, 2, 1)).reshape(model_width, expert_count)
-    router = jnp.pad(router, ((0, 0), (0, LANES - expert_count)))
-    home_out, home_grad, grad_up, grad_down, grad_router = run_experts(
+        owners, experts, capacity, prefix, routes.reshape(1, row_count), priority, tokens,
+        cotangent, small, w_router.T, w_qkv, w_out,
+    )
+    far_sums, near_sums, home_grad, grad_up, grad_down, grad_router = run_experts(
         owners, capacity, expert_count, send_rows, grad_rows, w_up, w_down, router
     )
-    output, grad_tokens, small_total, qkv_total, out_total = run_back(
-        owners, lead + -lead % 8, home_grad.reshape(-1, model_width),
-        home_out.reshape(-1, model_width), back, hidden, cotangent, tokens, vectors, grad_router,
-        act_t, merged_t, qkv, weight, out_full, low, high,
+    output, grad_tokens, grad_vectors, grad_gates, grad_qkv, grad_out = run_back(
+        owners, capacity, expert_count, home_grad, far_sums, near_sums, back, hidden, cotangent,
+        tokens, vectors, grad_router, act_t, merged_t, qkv, weight, out_full, low, high,
     )
     return (
         output,
         grad_tokens,
-        small_total[0],
-        small_total[1],
-        qkv_total.astype(jnp.float32),
-        out_total.astype(jnp.float32),
-        small_total[2],
-        small_total[3],
-        small_total[4:lead].T,
+        grad_vectors[0],
+        grad_vectors[1],
+        grad_qkv,
+        grad_out,
+        grad_vectors[2],
+        grad_vectors[3],
+        grad_gates.T,
         grad_up.astype(jnp.float32),
         grad_down.astype(jnp.float32),
     )
@@ -1864,7 +1926,7 @@
 
     def body(*args):
         capacity = args[0].shape[0] // args[7].shape[1]
-        fits = group == 4 and owners in (4, 8, 16) and capacity % 16 == 0
+        fits = group == 4 and owners in (4, 8, 16) and capacity % 16 == 0 and args[7].shape[1] % 16 == 0
         return (on_device if fits else on_device_plain)(*args)
 
     return jax.shard_map(

time: 301 us -> 295 us (0.980)
  local copies, waits for them, and re-layouts: 12.5 us -> 7.99 us
    convert_element_type x2 -> x0, other arithmetic: 5.56 us -> none  [the longest x1 3.43 us: on_device(): qkv_total.astype(jnp.float32)]
    unnamed x11 -> x17, local copies, waits for them, and re-layouts: 3.84 us -> 6.57 us
where the time goes in v2:
time: 295 us; the launch traced here: 294 us
  Pallas kernels  272 us (92%)
  other arithmetic  12.6 us (4%)
  local copies, waits for them, and re-layouts  7.99 us (3%)
    pallas_call x1, Pallas kernels, run_back(): pl.pallas_call(functools.partial(back_kernel, (owners, capacity, gates)),...  117 us
    pallas_call x1, Pallas kernels, run_experts(): pl.pallas_call(functools.partial(expert_kernel, dims), out_shape=(jax.Sha...  87.5 us
    pallas_call x1, Pallas kernels, run_front(): pl.pallas_call(functools.partial(front_kernel, (owners, capacity, pieces)...  67.9 us
    convert_element_type x1, other arithmetic, on_device(): grad_up.astype(jnp.float32)  6.79 us
    unnamed x17, local copies, waits for them, and re-layouts  6.57 us

profile of v2, /device:TPU:0, one launch (start us, length us, event | category | flops | bytes accessed | tf_op | source)
XLA Modules:
  0.0 294.3 jit_solution(11800984170987651177)
XLA Ops:
  1.3 1.4 select_select_fusion.small_hbm
  2.7 67.9 %front.1 = (bf16[512,3072]{1,0:T(8,128)(2,1)}, bf16[1024,512]{1,0:T(8,128)(2,1)}, bf16[1024,512]{1,0:T(8,128)(2,1)}, bf16[512,512]{1,0:T(8,128)(2,1)}, bf16[1024...) custom-call(s32[1]{0:T(128)S(6)} %copy.30.prefix_ref, ...), custom_call_target="tpu_custom_call" | custom-call | tf_op jit(solution)/shard_map/front/pallas_call | solution.py:1110
  70.6 87.5 %experts.1 = (bf16[2,256,1024]{2,1,0:T(8,128)(2,1)}, bf16[2,256,1024]{2,1,0:T(8,128)(2,1)}, bf16[8,2,32,1024]{3,2,1,0:T(8,128)(2,1)}, bf16[2,1024,1024]{2,1,0:T(...) custom-call(bf16[8,2,32,1024]{3,2,1,0:T(8,128)(2,1)} %get-tuple-element.36.send_ref, ...), custom_call_target="tpu_custom_call" | custom-call | tf_op jit(solution)/shard_map/experts/pallas_call | solution.py:657
  158.1 116.9 %back.1 = (bf16[512,1024]{1,0:T(8,128)(2,1)}, f32[512,1024]{1,0:T(8,128)}, f32[8,256]{1,0:T(8,128)}, f32[16,256]{1,0:T(8,128)}, f32[256,3072]{1,0:T(8,128)}, /*index=5*/f32[256,1024]{1,0:T(8,128)}) custom-call(bf16[8,2,32,1024]{3,2,1,0:T(8,128)(2,1)} %get-tuple-element.39.home_grad_ref, bf16[512,512]{1,0:T(8,128)(2,1)} %get-tuple-element.40.back_ref, ...), custom_call_target="tpu_custom_call" | custom-call | tf_op jit(solution)/shard_map/back/pallas_call | solution.py:1613
  275.1 1.4 fusion
  276.5 0.0 copy-start
  276.5 6.8 %convert_element_type.6 = f32[2,1024,1024]{2,1,0:T(8,128)} convert(bf16[2,1024,1024]{2,1,0:T(8,128)(2,1)} %get-tuple-element.59) | non-fusion elementwise | flops 2097152 | bytes 12582912 | tf_op jit(solution)/shard_map/convert_element_type | solution.py:1903
  283.3 0.0 copy-done
  283.3 0.0 copy-start.4
  283.3 0.0 copy-start.2
  283.3 4.4 %convert_element_type.7 = f32[2,1024,1024]{2,1,0:T(8,128)} convert(bf16[2,1024,1024]{2,1,0:T(8,128)(2,1)S(1)} %copy-done) | non-fusion elementwise | flops 2097152 | bytes 12582912 | tf_op jit(solution)/shard_map/convert_element_type | solution.py:1904
  287.7 0.0 copy-done.4
  287.7 0.0 copy-start.1
  287.7 1.0 copy.31
  288.7 0.0 copy-done.2
  288.7 1.3 copy.32
  290.0 0.7 copy-done.1
  290.8 0.0 copy-start.3
  290.8 0.0 copy-start.5
  290.8 1.7 copy.33
  292.4 0.3 copy-done.3
  292.7 1.0 copy.34
  293.7 0.0 copy-done.5
  293.7 0.6 copy.35
  (2 shorter events, 0.0 us)
Async XLA Ops:
  276.5 6.8 %copy-start = (bf16[2,1024,1024]{2,1,0:T(8,128)(2,1)S(1)}, bf16[2,1024,1024]{2,1,0:T(8,128)(2,1)}, u32[]{:S(2)}) copy-start(bf16[2,1024,1024]{2,1,0:T(8,128)(2,1)} %get-tuple-element.60) | copy-start | bytes 12582916
  283.3 4.4 %copy-start.4 = (bf16[512,1024]{1,0:T(8,128)(2,1)S(1)}, bf16[512,1024]{1,0:T(8,128)(2,1)}, u32[]{:S(2)}) copy-start(bf16[512,1024]{1,0:T(8,128)(2,1)} %get-tuple-element.80) | copy-start | bytes 3145732
  283.3 5.4 %copy-start.2 = (f32[512,1024]{1,0:T(8,128)S(1)}, f32[512,1024]{1,0:T(8,128)}, u32[]{:S(2)}) copy-start(f32[512,1024]{1,0:T(8,128)} %get-tuple-element.81) | copy-start | bytes 6291460
  287.7 3.0 %copy-start.1 = (f32[256,3072]{1,0:T(8,128)S(1)}, f32[256,3072]{1,0:T(8,128)}, u32[]{:S(2)}) copy-start(f32[256,3072]{1,0:T(8,128)} %get-tuple-element.84) | copy-start | bytes 9437188
  290.8 2.0 copy-start.3
  290.8 2.9 copy-start.5

commit v3 on v2

--- a/solution.py
+++ b/solution.py
@@ -14,7 +14,8 @@
 
 epsilon = 1e-05
 VMEM_LIMIT = 66_000_000
-TILE = 512
+TILE = 1024
+EARLY_CHUNKS = 2
 
 
 def normalize(values, gain_vec, shift_vec):
@@ -401,7 +402,7 @@
         here = span(j * 2 * self.cap, 2 * self.cap)
         for expert in range(self.experts):
             self.mid[expert, here, :] = self.pair_sum(expert, j, 1 - self.p.x).astype(jnp.bfloat16)
-            self.far[expert, here, :] = self.pair_sum(expert, j, self.p.x).astype(jnp.bfloat16)
+            self.keep[expert, here, :] = self.pair_sum(expert, j, self.p.x).astype(jnp.bfloat16)
 
     def cross(self, j):
         self.swapped(j).wait_recv()
@@ -432,13 +433,14 @@
     def drain_swaps(self, chunks):
         every(0, chunks, lambda j: self.swapped(j).wait_send())
 
-    def drain(self, chunks):
-        every(0, chunks, lambda j: self.crossed(j).wait_send())
-        every(1, self.p.owners, lambda n: self.homed(n).wait_send())
-
-    def arrived(self):
-        self.own().wait()
-        every(1, self.p.owners, lambda n: self.homed(n).wait_recv())
+    def drain(self, first, last):
+        every(first, last, lambda j: self.crossed(j).wait_send())
+        every(max(1, 2 * first), 2 * last, lambda n: self.homed(n).wait_send())
+
+    def arrived(self, first, last):
+        if first == 0:
+            self.own().wait()
+        every(max(1, 2 * first), 2 * last, lambda n: self.homed(n).wait_recv())
 
 
 class LateReturn(Return):
@@ -469,10 +471,10 @@
 def expert_kernel(
     dims,
     send_ref, grads_hbm, up_hbm, down_hbm, router_ref,
-    far_sums, near_sums, home_grad, up_out, down_out, router_grad,
+    far_sums, near_sums, home_out, home_grad, up_out, down_out, router_grad,
     rows, grads, scaled, hidden, pre, up, down, grad_up, grad_down,
     part_out, part_grad, got_out, got_grad, mid_out, mid_grad,
-    keep_out, far_grad, done_grad,
+    keep_out, far_grad, far_out, done_grad, done_out,
     load_sem, own_sem, disp_send, disp_recv, red_send, red_recv, home_send, home_recv,
 ):
     owners, experts, capacity, width, units, expert_count = dims
@@ -494,17 +496,18 @@
     )
     ret_grad = Return(
         place, capacity, experts, part_grad, got_grad, mid_grad, far_grad, done_grad, home_grad,
-        (own_sem.at[1], red_send.at[0], red_recv.at[0], home_send, home_recv),
+        (own_sem.at[1], red_send.at[0], red_recv.at[0], home_send.at[0], home_recv.at[0]),
     )
     ret_out = Return(
-        place, capacity, experts, part_out, got_out, mid_out, keep_out, None, None,
-        (None, red_send.at[1], red_recv.at[1], None, None),
+        place, capacity, experts, part_out, got_out, mid_out, far_out, done_out, home_out,
+        (own_sem.at[2], red_send.at[1], red_recv.at[1], home_send.at[1], home_recv.at[1]),
     )
     dispatch.start()
     router_grad[...] = jnp.zeros_like(router_grad)
     tile = min(TILE, units)
     wide = min(TILE, width)
     chunks = owners // 2
+    early = EARLY_CHUNKS
     size = 8 * capacity
     lane = lax.broadcasted_iota(jnp.int32, (size, LANES), 1)
 
@@ -599,7 +602,9 @@
         @pl.when(j >= 1)
         def _():
             ret_grad.cross(j - 1)
-            ret_out.split(j - 1)
+            either(
+                j - 1 < early, lambda: ret_out.cross(j - 1), lambda: ret_out.split(j - 1)
+            )
 
         pl.when(j >= 2)(lambda: ret_grad.finish(j - 2))
 
@@ -608,6 +613,7 @@
         ret_grad.swap(j)
         ret_out.swap(j)
 
+    ret_out.keep = keep_out
     every(0, chunks, step)
     weight_grads(0, 0, 1)
     ret_grad.cross(chunks - 1)
@@ -619,6 +625,7 @@
     for store in sums:
         store.start()
     ret_grad.finish(chunks - 2)
+    every(0, early, ret_out.finish)
     weight_grads(0, 1, 3)
     ret_grad.finish(chunks - 1)
     weight_grads(0, 3, 4)
@@ -635,8 +642,10 @@
         store.wait()
     dispatch.drain()
     ret_grad.drain_swaps(chunks)
-    ret_grad.drain(chunks)
-    ret_grad.arrived()
+    ret_grad.drain(0, chunks)
+    ret_grad.arrived(0, chunks)
+    ret_out.drain(0, early)
+    ret_out.arrived(0, early)
     ret_out.drain_swaps(chunks)
 
 
@@ -659,13 +668,13 @@
         out_shape=(
             jax.ShapeDtypeStruct((experts, slots // 4, width), bf16),
             jax.ShapeDtypeStruct((experts, slots // 4, width), bf16),
-            home,
+            home, home,
             jax.ShapeDtypeStruct(w_up.shape, bf16),
             jax.ShapeDtypeStruct(w_down.shape, bf16),
             jax.ShapeDtypeStruct((LANES, width), jnp.float32),
         ),
         in_specs=[any_spec] * 4 + [vmem_spec],
-        out_specs=(any_spec,) * 5 + (vmem_spec,),
+        out_specs=(any_spec,) * 6 + (vmem_spec,),
         scratch_shapes=[
             vm(experts, slots, width),
             vm(experts, slots, width),
@@ -684,15 +693,17 @@
             vm(experts, slots // 4, width),
             vm(experts, slots // 4, width),
             vm(experts, slots // 4, width),
+            vm(experts, slots // 4, width),
+            vm(owners, experts, capacity, width),
             vm(owners, experts, capacity, width),
             dma((6,)),
-            dma((2,)),
+            dma((3,)),
             dma((4, owners)),
             dma((4, owners)),
             dma((2, 2, chunks)),
             dma((2, 2, chunks)),
-            dma((owners,)),
-            dma((owners,)),
+            dma((2, owners)),
+            dma((2, owners)),
         ],
         compiler_params=pltpu.CompilerParams(
             collective_id=1, has_side_effects=True, vmem_limit_bytes=VMEM_LIMIT
@@ -754,80 +765,111 @@
 
 
 class Gather:
-    def __init__(self, place, pieces, src, dst, sems):
-        self.p, self.src, self.dst = place, src, dst
-        self.send, self.recv, self.near_send, self.near_recv, self.own_sem = sems
+    def __init__(self, place, pieces, parts, src, dst, sems):
+        self.p, self.src, self.dst, self.pieces, self.parts = place, src, dst, pieces, parts
+        self.send, self.recv = sems
         self.shard = src.shape[0]
         self.half = self.shard // 2
-        self.step = self.half // pieces
-        self.pieces = pieces
+        self.width = src.shape[1] // parts
+        self.step = self.width // pieces
         self.first = lax.rem(place.e, 2) * self.half
         self.second = self.half - self.first
 
-    def block(self, owner, start, size):
-        return self.dst.at[pl.ds(pl.multiple_of(owner * self.shard + start, self.step), size)]
-
-    def own(self):
-        return pltpu.make_async_copy(self.src, self.block(self.p.w, 0, self.shard), self.own_sem)
-
-    def near(self):
+    def cols(self, n, part):
+        return span(part * self.width + n * self.step, self.step)
+
+    def block(self, owner, start, size, n, part):
+        rows = pl.ds(pl.multiple_of(owner * self.shard + start, self.half), size)
+        return self.dst.at[rows, self.cols(n, part)]
+
+    def move(self, which, n, part, src, dst, device):
         return remote(
-            self.src, self.block(self.p.w, 0, self.shard), self.near_send, self.near_recv,
-            (self.p.e, self.p.sib),
-        )
-
-    def hop(self, n):
-        return remote(
-            self.src.at[span(self.first + n * self.step, self.step)],
-            self.block(self.p.w, self.first + n * self.step, self.step),
-            self.send.at[0, n], self.recv.at[0, n], (self.p.e, self.p.far),
-        )
-
-    def pass_from(self, start, n, which, device):
-        part = self.block(self.p.far, start + n * self.step, self.step)
-        return remote(part, part, self.send.at[which, n], self.recv.at[which, n], device)
-
-    def pairs(self, n):
-        return self.pass_from(self.first, n, 1, (self.p.pair, self.p.w))
-
-    def relay(self, n):
-        return self.pass_from(self.first, n, 2, (self.p.e, self.p.sib))
-
-    def pair_relay(self, n):
-        return self.pass_from(self.second, n, 3, (self.p.e, self.p.sib))
+            src, dst, self.send.at[which, n, part], self.recv.at[which, n, part], device
+        )
+
+    def own(self, n, part):
+        return pltpu.make_async_copy(
+            self.src.at[:, self.cols(n, part)],
+            self.block(self.p.w, 0, self.shard, n, part),
+            self.recv.at[5, n, part],
+        )
+
+    def near(self, n, part):
+        return self.move(
+            4, n, part, self.src.at[:, self.cols(n, part)],
+            self.block(self.p.w, 0, self.shard, n, part), (self.p.e, self.p.sib),
+        )
+
+    def hop(self, n, part):
+        return self.move(
+            0, n, part, self.src.at[span(self.first, self.half), self.cols(n, part)],
+            self.block(self.p.w, self.first, self.half, n, part), (self.p.e, self.p.far),
+        )
+
+    def pass_from(self, which, start, n, part, device):
+        block = self.block(self.p.far, start, self.half, n, part)
+        return self.move(which, n, part, block, block, device)
+
+    def pairs(self, n, part):
+        return self.pass_from(1, self.first, n, part, (self.p.pair, self.p.w))
+
+    def relay(self, n, part):
+        return self.pass_from(2, self.first, n, part, (self.p.e, self.p.sib))
+
+    def pair_relay(self, n, part):
+        return self.pass_from(3, self.second, n, part, (self.p.e, self.p.sib))
+
+    def all_parts(self, n, act):
+        for part in range(self.parts):
+            act(n, part)
+
+    def start_own(self):
+        every(
+            0, self.pieces, lambda n: self.all_parts(n, lambda n, part: self.own(n, part).start())
+        )
 
     def start(self):
-        every(0, self.pieces, lambda n: self.hop(n).start())
-        self.near().start()
+        def hop(n, part):
+            self.hop(n, part).start()
+
+        def near(n, part):
+            self.near(n, part).start()
+
+        every(0, self.pieces, lambda n: self.all_parts(n, hop))
+        every(0, self.pieces, lambda n: self.all_parts(n, near))
 
     def pass_on(self, n):
-        self.hop(n).wait_recv()
-        self.pairs(n).start()
-        self.relay(n).start()
+        def one(n, part):
+            self.hop(n, part).wait_recv()
+            self.pairs(n, part).start()
+            self.relay(n, part).start()
+
+        self.all_parts(n, one)
 
     def pass_pair(self, n):
-        self.pairs(n).wait_recv()
-        self.pair_relay(n).start()
-
-    def near_ready(self):
-        self.own().wait()
-        self.near().wait_recv()
-
-    def far_ready(self):
-        def one(n):
-            self.relay(n).wait_recv()
-            self.pair_relay(n).wait_recv()
-
-        every(0, self.pieces, one)
+        def one(n, part):
+            self.pairs(n, part).wait_recv()
+            self.pair_relay(n, part).start()
+
+        self.all_parts(n, one)
+
+    def ready(self, n):
+        def one(n, part):
+            self.own(n, part).wait()
+            for copy in (self.near(n, part), self.relay(n, part), self.pair_relay(n, part)):
+                copy.wait_recv()
+
+        self.all_parts(n, one)
 
     def drain(self):
-        self.near().wait_send()
-
-        def one(n):
-            for copy in (self.hop(n), self.pairs(n), self.relay(n), self.pair_relay(n)):
+        def one(n, part):
+            for copy in (
+                self.hop(n, part), self.pairs(n, part), self.relay(n, part),
+                self.pair_relay(n, part), self.near(n, part),
+            ):
                 copy.wait_send()
 
-        every(0, self.pieces, one)
+        every(0, self.pieces, lambda n: self.all_parts(n, one))
 
 
 def slot_tables(routes_ref, priority_ref, capacity, pick_ref, back_ref):
@@ -864,23 +906,19 @@
     prefix_ref, routes_ref, priority_ref, tokens_ref, cot_ref, small_hbm, router_hbm, qkv_hbm, out_hbm,
     qkv_out, act_out, merged_out, back_out, weight_out, out_full, low_out, high_out, grads_rows,
     hidden_ref, send_ref, small_out, router_out,
-    small, weight, out_w, total, qkv, act, merged, act_two, turned, pick, back, grads_send, low_buf, high_buf,
-    own_sem, disp_send, disp_recv, small_send, small_recv, near_send, near_recv,
-    gat_send, gat_recv, store_sem, prob_sem,
+    small, weight, out_w, qkv, act, merged, act_two, turned, pick, back, grads_send, low_buf, high_buf,
+    own_sem, disp_send, disp_recv, small_send, small_recv, gat_send, gat_recv, store_sem, prob_sem,
 ):
     owners, capacity, pieces = dims
     place = Place(owners)
     rows, width = tokens_ref.shape
     shard = qkv_hbm.shape[0]
     gathers = [
-        Gather(
-            place, pieces, src, dst,
-            (gat_send.at[i], gat_recv.at[i], near_send.at[i], near_recv.at[i], own_sem.at[1 + i]),
-        )
-        for i, (src, dst) in enumerate(((qkv_hbm, weight), (out_hbm, out_w)))
+        Gather(place, pieces, parts, src, dst, (gat_send.at[i], gat_recv.at[i]))
+        for i, (parts, src, dst) in enumerate(((3, qkv_hbm, weight), (1, out_hbm, out_w)))
     ]
     for gather in gathers:
-        gather.own().start()
+        gather.start_own()
     vectors, gates = small_hbm.shape[0], router_hbm.shape[0]
     small_parts = [
         (small_hbm, small.at[place.w, pl.ds(0, vectors)]),
@@ -944,52 +982,14 @@
         scaled, _ = norm_stats(tokens_ref[part, :].astype(jnp.float32))
         act[part, :] = (scaled * gain + shift).astype(jnp.bfloat16)
 
-    columns = weight.shape[1]
-    wide = min(512, columns)
-
-    def multiply(owner, cols):
-        depth = span(owner * shard, shard)
-        return dot_nn(act[:, depth], weight[depth, cols])
-
-    def first_tile(n):
-        cols = span(n * wide, wide)
-        total[:, cols] = multiply(place.w, cols) + multiply(place.sib, cols)
-
-    def last_tile(n):
-        cols = span(n * wide, wide)
-        value = total[:, cols] + multiply(place.far, cols) + multiply(place.diag, cols)
-        qkv[:, cols] = value.astype(jnp.bfloat16)
-
-    def pass_piece(gather, n):
-        @pl.when(n < pieces)
-        def _():
-            gather.pass_on(n)
-
-        @pl.when(n >= 1)
-        def _():
-            gather.pass_pair(n - 1)
+    def project(n):
+        for part in range(3):
+            cols = gathers[0].cols(n, part)
+            qkv[:, cols] = dot_nn(act[...], weight[:, cols]).astype(jnp.bfloat16)
 
     gathers[0].pass_on(0)
     every(0, rows // band, norm_band)
-    pass_piece(gathers[0], jnp.int32(1))
-    dispatch.forward(0)
     turned[0] = act[...].T
-    gathers[0].near_ready()
-    every(0, columns // wide, first_tile)
-    early = max(pieces - 1, owners // 2)
-
-    def pass_step(n):
-        @pl.when(n <= pieces)
-        def _():
-            pass_piece(gathers[0], n)
-
-        @pl.when(n - 1 < owners)
-        def _():
-            dispatch.forward(n - 1)
-
-    every(2, early + 2, pass_step)
-    gathers[0].far_ready()
-    every(0, columns // wide, last_tile)
     stores = [
         pltpu.make_async_copy(src, dst, store_sem.at[i])
         for i, (src, dst) in enumerate(
@@ -997,7 +997,7 @@
              (turned.at[1], merged_out), (out_w, out_full)]
         )
     ]
-    for store in stores[:4]:
+    for store in stores[1:3]:
         store.start()
     half = rows // 2
     pairs = width // LANES
@@ -1040,28 +1040,30 @@
         for copy in keep_probs(i):
             copy.start()
 
-    def attend_step(i):
-        @pl.when(i < pairs)
+    group = pairs // pieces
+    share = -(-owners // pieces)
+
+    def front_step(n):
+        @pl.when(n + 1 < pieces)
         def _():
-            attend_pair(i)
-
-        @pl.when(i + early + 1 < owners)
-        def _():
-            dispatch.forward(i + early + 1)
-
-        @pl.when((i >= 1) & (i < pieces + 2))
-        def _():
-            pass_piece(gathers[1], i - 1)
-
-        @pl.when(i < owners)
-        def _():
-            dispatch.relay(i)
-
-    every(0, max(pairs, owners, pieces + 2), attend_step)
+            gathers[0].pass_on(n + 1)
+
+        gathers[0].pass_pair(n)
+        for i in range(share):
+            pl.when(n * share + i < owners)(lambda: dispatch.forward(n * share + i))
+        gathers[0].ready(n)
+        project(n)
+        for i in range(group):
+            attend_pair(n * group + i)
+
+    every(0, pieces, front_step)
     turned[1] = merged[...].T
-    stores[4].start()
-    gathers[1].near_ready()
-    gathers[1].far_ready()
+    for i in (0, 3, 4):
+        stores[i].start()
+    every(0, pieces, gathers[1].pass_on)
+    every(0, pieces, gathers[1].pass_pair)
+    dispatch.relay(0)
+    every(0, pieces, gathers[1].ready)
     stores[5].start()
     gain_two, shift_two = vector(2), vector(3)
     band_two = min(128, rows)
@@ -1072,9 +1074,11 @@
         hidden_ref[part, :] = value
         scaled, _ = norm_stats(value)
         act_two[part, :] = (scaled * gain_two + shift_two).astype(jnp.bfloat16)
+        pl.when(i + 1 < owners)(lambda: dispatch.relay(i + 1))
 
     every(0, rows // band_two, middle)
     to_slots(act_two, send_ref)
+    every(1 + min(rows // band_two, owners - 1), owners, dispatch.relay)
     for i in (pairs - 2, pairs - 1):
         for copy in keep_probs(i):
             copy.wait()
@@ -1130,7 +1134,6 @@
             vm(4, small.shape[0] + router.shape[0], shard),
             vm(4 * shard, columns),
             vm(4 * shard, width),
-            pltpu.VMEM((rows, columns), f32),
             vm(rows, columns),
             vm(rows, width),
             vm(rows, width),
@@ -1146,10 +1149,8 @@
             dma((4, owners)),
             dma((2, 3)),
             dma((2, 3)),
-            dma((2,)),
-            dma((2,)),
-            dma((2, 4, pieces)),
-            dma((2, 4, pieces)),
+            dma((2, 6, pieces, 3)),
+            dma((2, 6, pieces, 3)),
             dma((6,)),
             dma((2, 2)),
         ],
@@ -1343,14 +1344,14 @@
 def back_kernel(
     dims,
     home_grad_ref, back_ref, hidden_ref, cot_ref, tokens_ref, vectors_ref, router_ref,
-    far_hbm, near_hbm, act_hbm, merged_hbm, qkv_hbm, weight_hbm, out_hbm, low_hbm, high_hbm,
+    far_hbm, near_hbm, home_hbm, act_hbm, merged_hbm, qkv_hbm, weight_hbm, out_hbm, low_hbm, high_hbm,
     output_ref, tokens_out, vectors_out, gates_out, qkv_out, out_out,
     near_sums, far_sums, done_rows, home_out,
     act_t, merged_t, qkv, weight, out_w, low_buf, high_buf, attn, grad_merged, wide_q, wide_o,
     part_q, got_q, far_q, pair_q, lines_q, done_q,
     part_o, got_o, far_o, pair_o, lines_o, done_o,
     small, small_part, small_got, small_mid, small_far, small_sum, small_all,
-    load_sem, prob_sem, own_sem, cross_send, cross_recv, home_send, home_recv, send_q, recv_q, lsend_q, lrecv_q, send_o, recv_o, lsend_o, lrecv_o,
+    load_sem, prob_sem, own_sem, early_sem, cross_send, cross_recv, home_send, home_recv, send_q, recv_q, lsend_q, lrecv_q, send_o, recv_o, lsend_o, lrecv_o,
     small_send, small_recv, all_send, all_recv, out_sem,
 ):
     owners, capacity, gates = dims
@@ -1389,7 +1390,13 @@
         place, capacity, experts, near_sums, None, far_hbm, far_sums, done_rows, home_out,
         (own_sem, cross_send, cross_recv, home_send, home_recv),
     )
-    every(0, groups, lambda j: late.crossed(j).start())
+    every(EARLY_CHUNKS, groups, lambda j: late.crossed(j).start())
+
+    def early_rows(n):
+        row = place.peer(n)
+        return pltpu.make_async_copy(home_hbm.at[row], home_out.at[row], early_sem.at[n])
+
+    every(0, 2 * EARLY_CHUNKS, lambda n: early_rows(n).start())
     reduce_o = Reduce(
         place, part_o, got_o, far_o, pair_o, lines_o, done_o, (send_o, recv_o, lsend_o, lrecv_o)
     )
@@ -1520,7 +1527,7 @@
     half = rows // band // 2
 
     def slot_step(slot):
-        pl.when(slot < groups)(lambda: late.finish(slot))
+        pl.when(slot + EARLY_CHUNKS < groups)(lambda: late.finish(slot + EARLY_CHUNKS))
         pl.when(slot < pairs)(lambda: attend_pair(slot))
         for s in range(last, -1, -1):
             n = slot - delays[s]
@@ -1553,7 +1560,8 @@
 
         @pl.when(slot == pairs + 3)
         def _():
-            late.arrived()
+            late.arrived(EARLY_CHUNKS, groups)
+            every(0, 2 * EARLY_CHUNKS, lambda n: early_rows(n).wait())
             every(0, rows // band, output_band)
 
     every(0, pairs + delays[-1], slot_step)
@@ -1566,14 +1574,14 @@
     every(0, pairs, stored)
     for n in range(out_chunks):
         store_o(n).wait()
-    late.drain(groups)
+    late.drain(EARLY_CHUNKS, groups)
     reduce_o.drain()
     reduce_q.drain()
     smalls.drain()
 
 
 def run_back(
-    owners, capacity, gates, home_grad, far_sums, near_sums, back, hidden, cotangent, tokens,
+    owners, capacity, gates, home_grad, far_sums, near_sums, home_out, back, hidden, cotangent, tokens,
     vectors, router_grad, act_t, merged_t, qkv, weight, w_out, low, high,
 ):
     rows, width = tokens.shape
@@ -1620,7 +1628,7 @@
             jax.ShapeDtypeStruct((shard, 3 * width), f32),
             jax.ShapeDtypeStruct((shard, width), f32),
         ),
-        in_specs=[vmem_spec] * 7 + [any_spec] * 9,
+        in_specs=[vmem_spec] * 7 + [any_spec] * 10,
         out_specs=(vmem_spec,) * 4 + (any_spec,) * 2,
         scratch_shapes=[
             vm(*near_sums.shape),
@@ -1652,6 +1660,7 @@
             dma((6,)),
             dma((2, 2)),
             dma(()),
+            dma((owners,)),
             dma((groups,)),
             dma((groups,)),
             dma((owners,)),
@@ -1666,7 +1675,7 @@
         name="back",
     )(
         home_grad, back, hidden, cotangent, tokens, vectors, router_grad,
-        far_sums, near_sums, act_t, merged_t, qkv, weight, w_out, low, high,
+        far_sums, near_sums, home_out, act_t, merged_t, qkv, weight, w_out, low, high,
     )
 
 
@@ -1883,11 +1892,11 @@
         owners, experts, capacity, prefix, routes.reshape(1, row_count), priority, tokens,
         cotangent, small, w_router.T, w_qkv, w_out,
     )
-    far_sums, near_sums, home_grad, grad_up, grad_down, grad_router = run_experts(
+    far_sums, near_sums, home_out, home_grad, grad_up, grad_down, grad_router = run_experts(
         owners, capacity, expert_count, send_rows, grad_rows, w_up, w_down, router
     )
     output, grad_tokens, grad_vectors, grad_gates, grad_qkv, grad_out = run_back(
-        owners, capacity, expert_count, home_grad, far_sums, near_sums, back, hidden, cotangent,
+        owners, capacity, expert_count, home_grad, far_sums, near_sums, home_out, back, hidden, cotangent,
         tokens, vectors, grad_router, act_t, merged_t, qkv, weight, out_full, low, high,
     )
     return (

time: 295 us -> 287 us (0.973)
  Pallas kernels: 272 us -> 265 us
    pallas_call x1, Pallas kernels: 117 us -> 102 us  [run_back(): pl.pallas_call(functools.partial(back_kernel, (owners, capacity, gates)),...]
    pallas_call x1, Pallas kernels: 87.5 us -> 95.4 us  [run_experts(): pl.pallas_call(functools.partial(expert_kernel, dims), out_shape=(jax.Sha...]
where the time goes in v3:
time: 287 us
  Pallas kernels  265 us (92%)
  other arithmetic  12.6 us (4%)
  local copies, waits for them, and re-layouts  7.99 us (3%)
    pallas_call x1, Pallas kernels, run_back(): pl.pallas_call(functools.partial(back_kernel, (owners, capacity, gates)),...  102 us
    pallas_call x1, Pallas kernels, run_experts(): pl.pallas_call(functools.partial(expert_kernel, dims), out_shape=(jax.Sha...  95.4 us
    pallas_call x1, Pallas kernels, run_front(): pl.pallas_call(functools.partial(front_kernel, (owners, capacity, pieces)...  67.2 us
    convert_element_type x1, other arithmetic, on_device(): grad_up.astype(jnp.float32)  6.79 us
    unnamed x17, local copies, waits for them, and re-layouts  6.57 us

profile of v3, /device:TPU:0, one launch (start us, length us, event | category | flops | bytes accessed | tf_op | source)
XLA Modules:
  0.0 287.0 jit_solution(12341083521638099079)
XLA Ops:
  1.3 1.4 select_select_fusion.small_hbm
  2.7 67.2 %front.1 = (bf16[512,3072]{1,0:T(8,128)(2,1)}, bf16[1024,512]{1,0:T(8,128)(2,1)}, bf16[1024,512]{1,0:T(8,128)(2,1)}, bf16[512,512]{1,0:T(8,128)(2,1)}, bf16[1024...) custom-call(s32[1]{0:T(128)S(6)} %copy.30.prefix_ref, ...), custom_call_target="tpu_custom_call" | custom-call | tf_op jit(solution)/shard_map/front/pallas_call | solution.py:1114
  69.9 95.4 %experts.1 = (bf16[2,256,1024]{2,1,0:T(8,128)(2,1)}, bf16[2,256,1024]{2,1,0:T(8,128)(2,1)}, bf16[8,2,32,1024]{3,2,1,0:T(8,128)(2,1)}, bf16[8,2,32,1024]{3,2,1,0:...) custom-call(bf16[8,2,32,1024]{3,2,1,0:T(8,128)(2,1)} %get-tuple-element.37.send_r, ...), custom_call_target="tpu_custom_call" | custom-call | tf_op jit(solution)/shard_map/experts/pallas_call | solution.py:666
  165.4 102.3 %back.1 = (bf16[512,1024]{1,0:T(8,128)(2,1)}, f32[512,1024]{1,0:T(8,128)}, f32[8,256]{1,0:T(8,128)}, f32[16,256]{1,0:T(8,128)}, f32[256,3072]{1,0:T(8,128)}, /*index=5*/f32[256,1024]{1,0:T(8,128)}) custom-call(bf16[8,2,32,1024]{3,2,1,0:T(8,128)(2,1)} %get-tuple-element.40.home_grad_ref, bf16[512,512]{1,0:T(8,128)(2,1)} %get-tuple-element.41.back_ref, ...), custom_call_target="tpu_custom_call" | custom-call | tf_op jit(solution)/shard_map/back/pallas_call | solution.py:1621
  267.7 1.4 fusion
  269.1 0.0 copy-start
  269.2 6.8 %convert_element_type.6 = f32[2,1024,1024]{2,1,0:T(8,128)} convert(bf16[2,1024,1024]{2,1,0:T(8,128)(2,1)} %get-tuple-element.61) | non-fusion elementwise | flops 2097152 | bytes 12582912 | tf_op jit(solution)/shard_map/convert_element_type | solution.py:1912
  275.9 0.0 copy-done
  275.9 0.0 copy-start.4
  275.9 0.0 copy-start.2
  276.0 4.4 %convert_element_type.7 = f32[2,1024,1024]{2,1,0:T(8,128)} convert(bf16[2,1024,1024]{2,1,0:T(8,128)(2,1)S(1)} %copy-done) | non-fusion elementwise | flops 2097152 | bytes 12582912 | tf_op jit(solution)/shard_map/convert_element_type | solution.py:1913
  280.4 0.0 copy-done.4
  280.4 0.0 copy-start.1
  280.4 1.0 copy.31
  281.4 0.0 copy-done.2
  281.4 1.3 copy.32
  282.7 0.7 copy-done.1
  283.4 0.0 copy-start.3
  283.4 0.0 copy-start.5
  283.4 1.7 copy.33
  285.1 0.3 copy-done.3
  285.4 1.0 copy.34
  286.3 0.0 copy-done.5
  286.4 0.6 copy.35
  (2 shorter events, 0.0 us)
Async XLA Ops:
  269.1 6.8 %copy-start = (bf16[2,1024,1024]{2,1,0:T(8,128)(2,1)S(1)}, bf16[2,1024,1024]{2,1,0:T(8,128)(2,1)}, u32[]{:S(2)}) copy-start(bf16[2,1024,1024]{2,1,0:T(8,128)(2,1)} %get-tuple-element.62) | copy-start | bytes 12582916
  275.9 4.4 %copy-start.4 = (bf16[512,1024]{1,0:T(8,128)(2,1)S(1)}, bf16[512,1024]{1,0:T(8,128)(2,1)}, u32[]{:S(2)}) copy-start(bf16[512,1024]{1,0:T(8,128)(2,1)} %get-tuple-element.82) | copy-start | bytes 3145732
  275.9 5.4 %copy-start.2 = (f32[512,1024]{1,0:T(8,128)S(1)}, f32[512,1024]{1,0:T(8,128)}, u32[]{:S(2)}) copy-start(f32[512,1024]{1,0:T(8,128)} %get-tuple-element.83) | copy-start | bytes 6291460
  280.4 3.0 %copy-start.1 = (f32[256,3072]{1,0:T(8,128)S(1)}, f32[256,3072]{1,0:T(8,128)}, u32[]{:S(2)}) copy-start(f32[256,3072]{1,0:T(8,128)} %get-tuple-element.86) | copy-start | bytes 9437188
  283.4 2.0 copy-start.3
  283.4 2.9 %copy-start.5 = (f32[16,256]{1,0:T(8,128)S(1)}, f32[16,256]{1,0:T(8,128)}, u32[]{:S(2)}) copy-start(f32[16,256]{1,0:T(8,128)} %get-tuple-element.60) | copy-start | bytes 49156

commit v4 on v3

--- a/solution.py
+++ b/solution.py
@@ -337,6 +337,10 @@
         self.to_sib(k).wait_recv()
         self.relayed(k).wait_recv()
 
+    def order(self):
+        near, far = list(range(0, self.p.owners, 2)), list(range(1, self.p.owners, 2))
+        return near[:3] + far[:1] + near[3:] + far[1:]
+
     def drain(self):
         every(1, self.p.owners, lambda k: self.direct(k).wait_send())
 
@@ -349,114 +353,120 @@
 
 
 class Return:
-    def __init__(self, place, capacity, experts, part, got, mid, far, done, home, sems):
-        self.p, self.cap, self.experts = place, capacity, experts
+    def __init__(self, place, capacity, part, got, mid, far, done, home, sems):
+        self.p, self.cap = place, capacity
         self.part, self.got, self.mid, self.far, self.done, self.home = (
             part, got, mid, far, done, home,
         )
         self.own_sem, self.send, self.recv, self.home_send, self.home_recv = sems
 
-    def swapped(self, j):
+    def swapped(self, j, expert):
         size = 4 * self.cap
         return remote(
-            self.part.at[:, span((j * 2 + 1 - self.p.c) * size, size)],
-            self.got.at[:, span(j * size, size)],
-            self.send.at[0, j],
-            self.recv.at[0, j],
+            self.part.at[expert, span((j * 2 + 1 - self.p.c) * size, size)],
+            self.got.at[expert, span(j * size, size)],
+            self.send.at[0, j, expert],
+            self.recv.at[0, j, expert],
             (self.p.e, self.p.sib),
         )
 
-    def crossed(self, j):
+    def crossed(self, j, expert):
         part = span(j * 2 * self.cap, 2 * self.cap)
         return remote(
-            self.mid.at[:, part],
-            self.far.at[:, part],
-            self.send.at[1, j],
-            self.recv.at[1, j],
+            self.mid.at[expert, part],
+            self.far.at[expert, part],
+            self.send.at[1, j, expert],
+            self.recv.at[1, j, expert],
             (self.p.e, self.p.far),
         )
 
-    def own(self):
-        return pltpu.make_async_copy(self.done.at[0], self.home.at[self.p.e], self.own_sem)
-
-    def homed(self, n):
+    def own(self, expert):
+        return pltpu.make_async_copy(
+            self.done.at[0, expert], self.home.at[self.p.e, expert], self.own_sem.at[expert]
+        )
+
+    def homed(self, n, expert):
         return remote(
-            self.done.at[n],
-            self.home.at[self.p.e],
-            self.home_send.at[n],
-            self.home_recv.at[n],
+            self.done.at[n, expert],
+            self.home.at[self.p.e, expert],
+            self.home_send.at[n, expert],
+            self.home_recv.at[n, expert],
             (self.p.peer(n), self.p.w),
         )
 
-    def pair_sum(self, expert, j, side):
+    def pair_sum(self, j, expert, side):
         size = 2 * self.cap
         mine = self.part[expert, span(((j * 2 + self.p.c) * 2 + side) * size, size), :]
         theirs = self.got[expert, span((j * 2 + side) * size, size), :]
         return mine.astype(jnp.float32) + theirs.astype(jnp.float32)
 
-    def swap(self, j):
-        self.swapped(j).start()
-
-    def split(self, j):
-        self.swapped(j).wait_recv()
+    def swap(self, j, expert):
+        self.swapped(j, expert).start()
+
+    def split(self, j, expert):
+        self.swapped(j, expert).wait_recv()
         here = span(j * 2 * self.cap, 2 * self.cap)
-        for expert in range(self.experts):
-            self.mid[expert, here, :] = self.pair_sum(expert, j, 1 - self.p.x).astype(jnp.bfloat16)
-            self.keep[expert, here, :] = self.pair_sum(expert, j, self.p.x).astype(jnp.bfloat16)
-
-    def cross(self, j):
-        self.swapped(j).wait_recv()
-        size = 2 * self.cap
-        for expert in range(self.experts):
-            self.mid[expert, span(j * size, size), :] = self.pair_sum(
-                expert, j, 1 - self.p.x
-            ).astype(jnp.bfloat16)
-        self.crossed(j).start()
-
-    def this_side(self, expert, j):
-        return self.pair_sum(expert, j, self.p.x)
-
-    def finish(self, j):
-        self.crossed(j).wait_recv()
-        size = 2 * self.cap
-        for expert in range(self.experts):
-            total = self.this_side(expert, j) + self.far[
-                expert, span(j * size, size), :
-            ].astype(jnp.float32)
-            total = total.astype(jnp.bfloat16)
-            self.done[2 * j, expert] = total[: self.cap]
-            self.done[2 * j + 1, expert] = total[self.cap :]
+        self.mid[expert, here, :] = self.pair_sum(j, expert, 1 - self.p.x).astype(jnp.bfloat16)
+        self.keep[expert, here, :] = self.pair_sum(j, expert, self.p.x).astype(jnp.bfloat16)
+
+    def cross(self, j, expert):
+        self.swapped(j, expert).wait_recv()
+        here = span(j * 2 * self.cap, 2 * self.cap)
+        self.mid[expert, here, :] = self.pair_sum(j, expert, 1 - self.p.x).astype(jnp.bfloat16)
+        self.crossed(j, expert).start()
+
+    def this_side(self, j, expert):
+        return self.pair_sum(j, expert, self.p.x)
+
+    def finish(self, j, expert):
+        self.crossed(j, expert).wait_recv()
+        here = span(j * 2 * self.cap, 2 * self.cap)
+        total = self.this_side(j, expert) + self.far[expert, here, :].astype(jnp.float32)
+        total = total.astype(jnp.bfloat16)
+        self.done[2 * j, expert] = total[: self.cap]
+        self.done[2 * j + 1, expert] = total[self.cap :]
         j = jnp.int32(j)
-        self.homed(2 * j + 1).start()
-        either(j == 0, lambda: self.own().start(), lambda: self.homed(2 * j).start())
-
-    def drain_swaps(self, chunks):
-        every(0, chunks, lambda j: self.swapped(j).wait_send())
-
-    def drain(self, first, last):
-        every(first, last, lambda j: self.crossed(j).wait_send())
-        every(max(1, 2 * first), 2 * last, lambda n: self.homed(n).wait_send())
-
-    def arrived(self, first, last):
-        if first == 0:
-            self.own().wait()
-        every(max(1, 2 * first), 2 * last, lambda n: self.homed(n).wait_recv())
+        self.homed(2 * j + 1, expert).start()
+        either(
+            j == 0,
+            lambda: self.own(expert).start(),
+            lambda: self.homed(2 * j, expert).start(),
+        )
+
+    def drain_swaps(self, chunks, experts):
+        for expert in range(experts):
+            every(0, chunks, lambda j: self.swapped(j, expert).wait_send())
+
+    def drain(self, first, last, experts):
+        for expert in range(experts):
+            every(first, last, lambda j: self.crossed(j, expert).wait_send())
+            every(
+                max(1, 2 * first), 2 * last, lambda n: self.homed(n, expert).wait_send()
+            )
+
+    def arrived(self, first, last, experts):
+        for expert in range(experts):
+            if first == 0 and last > 0:
+                self.own(expert).wait()
+            every(
+                max(1, 2 * first), 2 * last, lambda n: self.homed(n, expert).wait_recv()
+            )
 
 
 class LateReturn(Return):
-    def crossed(self, j):
+    def crossed(self, j, expert):
         part = span(j * 2 * self.cap, 2 * self.cap)
         return remote(
-            self.mid.at[:, part],
-            self.far.at[:, part],
-            self.send.at[j],
-            self.recv.at[j],
+            self.mid.at[expert, part],
+            self.far.at[expert, part],
+            self.send.at[j, expert],
+            self.recv.at[j, expert],
             (self.p.e, self.p.far),
         )
 
-    def this_side(self, expert, j):
-        size = 2 * self.cap
-        return self.part[expert, span(j * size, size), :].astype(jnp.float32)
+    def this_side(self, j, expert):
+        here = span(j * 2 * self.cap, 2 * self.cap)
+        return self.part[expert, here, :].astype(jnp.float32)
 
 
 def gelu_pair(v):
@@ -492,14 +502,14 @@
         + [(place.e, place.sib), (place.e, place.far)]
     )
     dispatch = Dispatch(
-        place, capacity, send_ref, rows, (own_sem.at[0], disp_send, disp_recv)
+        place, capacity, send_ref, rows, (own_sem.at[0, 0], disp_send, disp_recv)
     )
     ret_grad = Return(
-        place, capacity, experts, part_grad, got_grad, mid_grad, far_grad, done_grad, home_grad,
+        place, capacity, part_grad, got_grad, mid_grad, far_grad, done_grad, home_grad,
         (own_sem.at[1], red_send.at[0], red_recv.at[0], home_send.at[0], home_recv.at[0]),
     )
     ret_out = Return(
-        place, capacity, experts, part_out, got_out, mid_out, far_out, done_out, home_out,
+        place, capacity, part_out, got_out, mid_out, far_out, done_out, home_out,
         (own_sem.at[2], red_send.at[1], red_recv.at[1], home_send.at[1], home_recv.at[1]),
     )
     dispatch.start()
@@ -527,8 +537,8 @@
             cols = span(n * tile, tile)
             value, slope = gelu_pair(dot_nn(rows[expert, here, :], up[expert, :, cols]))
             hidden[expert, here, cols] = value.astype(jnp.bfloat16)
-            back = dot_nt(scaled[expert, here, :], down[expert, cols, :])
-            pre[expert, here, cols] = (back * slope).astype(jnp.bfloat16)
+            back = pre[expert, here, cols].astype(jnp.float32)
+            pre[expert, here, cols] = (gate * back * slope).astype(jnp.bfloat16)
 
         every(0, units // tile, one_tile)
 
@@ -558,6 +568,10 @@
             router_grad[:, cols] += dot_tn(grad_logits, rows[expert, here, cols])
 
         every(0, width // wide, one_in)
+
+    def unscaled(j, expert):
+        here = span(j * size, size)
+        pre[expert, here, :] = dot_nt(grads[expert, here, :], down[expert]).astype(jnp.bfloat16)
 
     block = min(256, width)
 
@@ -579,55 +593,81 @@
             for i, (src, dst) in enumerate(((grad_up, up_out), (grad_down, down_out)))
         ]
 
-    def arrive(j):
-        for n in (2 * j, 2 * j + 1):
-            dispatch.relay(n)
-        for n in (2 * j, 2 * j + 1):
-            dispatch.ready(n)
-
-    def forward(j):
-        dispatch.forward(2 * j)
-        dispatch.forward(2 * j + 1)
-
-    forward(0)
-    forward(1)
+    turns = [(j, expert) for j in range(chunks) for expert in range(experts)]
+    order = dispatch.order()
+    waiting, moved = order[4:], set(order[:4])
+    plan = [[] for _ in turns]
+
+    def forward_to(acts, count):
+        for _ in range(min(count, len(waiting))):
+            n = waiting.pop(0)
+            moved.add(n)
+            acts.append((dispatch.forward, n))
+
+    for u, (j, expert) in enumerate(turns):
+        acts = plan[u]
+        pair = (2 * j, 2 * j + 1)
+        if expert == 0:
+            if j > 0:
+                while not moved.issuperset(pair):
+                    forward_to(acts, 1)
+                for n in pair:
+                    acts.append((dispatch.relay, n))
+            for n in pair:
+                acts.append((dispatch.ready, n))
+        if u > 0:
+            forward_to(acts, 2)
+        if u >= 2:
+            last = turns[u - 2]
+            acts.append((ret_grad.cross,) + last)
+            acts.append((ret_out.cross if last[0] < early else ret_out.split,) + last)
+        if u >= 4:
+            last = turns[u - 4]
+            acts.append((ret_grad.finish,) + last)
+            if last[0] < early:
+                acts.append((ret_out.finish,) + last)
+    ret_out.keep = keep_out
     for load in loads:
         load.wait()
-
-    def step(j):
-        arrive(j)
-        compute(j, 0)
-        pl.when(j + 2 < chunks)(lambda: forward(j + 2))
-
-        @pl.when(j >= 1)
-        def _():
-            ret_grad.cross(j - 1)
-            either(
-                j - 1 < early, lambda: ret_out.cross(j - 1), lambda: ret_out.split(j - 1)
-            )
-
-        pl.when(j >= 2)(lambda: ret_grad.finish(j - 2))
-
-        for expert in range(1, experts):
-            compute(j, expert)
-        ret_grad.swap(j)
-        ret_out.swap(j)
-
-    ret_out.keep = keep_out
-    every(0, chunks, step)
+    for n in order[:4]:
+        dispatch.forward(n)
+        j = n // 2 if n % 2 == 0 else chunks - 1
+        for expert in range(experts):
+            unscaled(j, expert)
+    dispatch.relay(0)
+    dispatch.relay(1)
+
+    def step(unit):
+        for u, acts in enumerate(plan):
+
+            @pl.when(unit == u)
+            def _(acts=acts):
+                for act, *at in acts:
+                    act(*at)
+
+        j, expert = lax.div(unit, experts), lax.rem(unit, experts)
+        compute(j, expert)
+        ret_grad.swap(j, expert)
+        ret_out.swap(j, expert)
+
+    every(0, len(turns), step)
+    ret_grad.cross(*turns[-2])
+    ret_out.split(*turns[-2])
+    ret_grad.finish(*turns[-4])
     weight_grads(0, 0, 1)
-    ret_grad.cross(chunks - 1)
-    ret_out.split(chunks - 1)
+    ret_grad.cross(*turns[-1])
+    ret_out.split(*turns[-1])
     sums = [
         pltpu.make_async_copy(src, dst, load_sem.at[4 + i])
         for i, (src, dst) in enumerate(((mid_out, far_sums), (keep_out, near_sums)))
     ]
     for store in sums:
         store.start()
-    ret_grad.finish(chunks - 2)
-    every(0, early, ret_out.finish)
-    weight_grads(0, 1, 3)
-    ret_grad.finish(chunks - 1)
+    ret_grad.finish(*turns[-3])
+    weight_grads(0, 1, 2)
+    ret_grad.finish(*turns[-2])
+    weight_grads(0, 2, 3)
+    ret_grad.finish(*turns[-1])
     weight_grads(0, 3, 4)
     for store in keep(0):
         store.start()
@@ -641,12 +681,12 @@
     for store in sums:
         store.wait()
     dispatch.drain()
-    ret_grad.drain_swaps(chunks)
-    ret_grad.drain(0, chunks)
-    ret_grad.arrived(0, chunks)
-    ret_out.drain(0, early)
-    ret_out.arrived(0, early)
-    ret_out.drain_swaps(chunks)
+    ret_grad.drain_swaps(chunks, experts)
+    ret_grad.drain(0, chunks, experts)
+    ret_grad.arrived(0, chunks, experts)
+    ret_out.drain_swaps(chunks, experts)
+    ret_out.drain(0, early, experts)
+    ret_out.arrived(0, early, experts)
 
 
 def run_experts(owners, capacity, expert_count, send_rows, grads, w_up, w_down, router):
@@ -697,13 +737,13 @@
             vm(owners, experts, capacity, width),
             vm(owners, experts, capacity, width),
             dma((6,)),
-            dma((3,)),
+            dma((3, experts)),
             dma((4, owners)),
             dma((4, owners)),
-            dma((2, 2, chunks)),
-            dma((2, 2, chunks)),
-            dma((2, owners)),
-            dma((2, owners)),
+            dma((2, 2, chunks, experts)),
+            dma((2, 2, chunks, experts)),
+            dma((2, owners, experts)),
+            dma((2, owners, experts)),
         ],
         compiler_params=pltpu.CompilerParams(
             collective_id=1, has_side_effects=True, vmem_limit_bytes=VMEM_LIMIT
@@ -1049,8 +1089,8 @@
             gathers[0].pass_on(n + 1)
 
         gathers[0].pass_pair(n)
-        for i in range(share):
-            pl.when(n * share + i < owners)(lambda: dispatch.forward(n * share + i))
+        for i, partner in enumerate(dispatch.order()):
+            pl.when(n == i // share)(functools.partial(dispatch.forward, partner))
         gathers[0].ready(n)
         project(n)
         for i in range(group):
@@ -1062,7 +1102,8 @@
         stores[i].start()
     every(0, pieces, gathers[1].pass_on)
     every(0, pieces, gathers[1].pass_pair)
-    dispatch.relay(0)
+    order = dispatch.order()
+    dispatch.relay(order[0])
     every(0, pieces, gathers[1].ready)
     stores[5].start()
     gain_two, shift_two = vector(2), vector(3)
@@ -1074,11 +1115,14 @@
         hidden_ref[part, :] = value
         scaled, _ = norm_stats(value)
         act_two[part, :] = (scaled * gain_two + shift_two).astype(jnp.bfloat16)
-        pl.when(i + 1 < owners)(lambda: dispatch.relay(i + 1))
-
-    every(0, rows // band_two, middle)
+        for n, partner in enumerate(order[1 : 1 + bands]):
+            pl.when(i == n)(functools.partial(dispatch.relay, partner))
+
+    bands = rows // band_two
+    every(0, bands, middle)
     to_slots(act_two, send_ref)
-    every(1 + min(rows // band_two, owners - 1), owners, dispatch.relay)
+    for partner in order[1 + bands :]:
+        dispatch.relay(partner)
     for i in (pairs - 2, pairs - 1):
         for copy in keep_probs(i):
             copy.wait()
@@ -1347,7 +1391,7 @@
     far_hbm, near_hbm, home_hbm, act_hbm, merged_hbm, qkv_hbm, weight_hbm, out_hbm, low_hbm, high_hbm,
     output_ref, tokens_out, vectors_out, gates_out, qkv_out, out_out,
     near_sums, far_sums, done_rows, home_out,
-    act_t, merged_t, qkv, weight, out_w, low_buf, high_buf, attn, grad_merged, wide_q, wide_o,
+    act_t, merged_t, qkv, weight, out_w, low_buf, high_buf, attn, grad_merged,
     part_q, got_q, far_q, pair_q, lines_q, done_q,
     part_o, got_o, far_o, pair_o, lines_o, done_o,
     small, small_part, small_got, small_mid, small_far, small_sum, small_all,
@@ -1387,10 +1431,11 @@
     experts = near_sums.shape[0]
     groups = owners // 2
     late = LateReturn(
-        place, capacity, experts, near_sums, None, far_hbm, far_sums, done_rows, home_out,
+        place, capacity, near_sums, None, far_hbm, far_sums, done_rows, home_out,
         (own_sem, cross_send, cross_recv, home_send, home_recv),
     )
-    every(EARLY_CHUNKS, groups, lambda j: late.crossed(j).start())
+    for expert in range(experts):
+        every(EARLY_CHUNKS, groups, lambda j: late.crossed(j, expert).start())
 
     def early_rows(n):
         row = place.peer(n)
@@ -1509,7 +1554,7 @@
     def store_q(i):
         return [
             pltpu.make_async_copy(
-                wide_q.at[i, :, pl.ds(which * LANES, LANES)],
+                done_q.at[i, :, pl.ds(which * LANES, LANES)],
                 qkv_out.at[:, span(which * width + i * LANES, LANES)],
                 out_sem.at[which, i],
             )
@@ -1518,7 +1563,7 @@
 
     def store_o(n):
         return pltpu.make_async_copy(
-            wide_o.at[n], out_out.at[:, span(n * tile_o, tile_o)], out_sem.at[3, n]
+            done_o.at[n], out_out.at[:, span(n * tile_o, tile_o)], out_sem.at[3, n]
         )
 
     stages_o, stages_q = reduce_o.stages(), reduce_q.stages()
@@ -1527,7 +1572,11 @@
     half = rows // band // 2
 
     def slot_step(slot):
-        pl.when(slot + EARLY_CHUNKS < groups)(lambda: late.finish(slot + EARLY_CHUNKS))
+        @pl.when(slot + EARLY_CHUNKS < groups)
+        def _():
+            for expert in range(experts):
+                late.finish(slot + EARLY_CHUNKS, expert)
+
         pl.when(slot < pairs)(lambda: attend_pair(slot))
         for s in range(last, -1, -1):
             n = slot - delays[s]
@@ -1536,7 +1585,6 @@
             def _(s=s, n=n):
                 stages_q[s](n)
                 if s == last:
-                    wide_q[n] = done_q[n].astype(jnp.float32)
                     for copy in store_q(n):
                         copy.start()
 
@@ -1545,7 +1593,6 @@
                 for n in range(out_chunks):
                     stages_o[s](n)
                     if s == last:
-                        wide_o[n] = done_o[n].astype(jnp.float32)
                         store_o(n).start()
 
         @pl.when(slot == pairs)
@@ -1560,7 +1607,7 @@
 
         @pl.when(slot == pairs + 3)
         def _():
-            late.arrived(EARLY_CHUNKS, groups)
+            late.arrived(EARLY_CHUNKS, groups, experts)
             every(0, 2 * EARLY_CHUNKS, lambda n: early_rows(n).wait())
             every(0, rows // band, output_band)
 
@@ -1574,7 +1621,7 @@
     every(0, pairs, stored)
     for n in range(out_chunks):
         store_o(n).wait()
-    late.drain(EARLY_CHUNKS, groups)
+    late.drain(EARLY_CHUNKS, groups, experts)
     reduce_o.drain()
     reduce_q.drain()
     smalls.drain()
@@ -1625,8 +1672,8 @@
             jax.ShapeDtypeStruct((rows, width), f32),
             jax.ShapeDtypeStruct((8, shard), f32),
             jax.ShapeDtypeStruct((gates, shard), f32),
-            jax.ShapeDtypeStruct((shard, 3 * width), f32),
-            jax.ShapeDtypeStruct((shard, width), f32),
+            jax.ShapeDtypeStruct((shard, 3 * width), bf16),
+            jax.ShapeDtypeStruct((shard, width), bf16),
         ),
         in_specs=[vmem_spec] * 7 + [any_spec] * 10,
         out_specs=(vmem_spec,) * 4 + (any_spec,) * 2,
@@ -1644,8 +1691,6 @@
             vm(2, 2, mid, rows),
             vm(rows, width),
             vm(rows, width),
-            fm(pairs, shard, 3 * LANES),
-            fm(out_chunks, shard, tile_o),
         ]
         + reduce_buffers(pairs, 3 * LANES)
         + reduce_buffers(out_chunks, tile_o)
@@ -1659,12 +1704,12 @@
             fm(owners, lead, shard),
             dma((6,)),
             dma((2, 2)),
-            dma(()),
+            dma((near_sums.shape[0],)),
             dma((owners,)),
-            dma((groups,)),
-            dma((groups,)),
-            dma((owners,)),
-            dma((owners,)),
+            dma((groups, near_sums.shape[0])),
+            dma((groups, near_sums.shape[0])),
+            dma((owners, near_sums.shape[0])),
+            dma((owners, near_sums.shape[0])),
         ]
         + reduce_sems(pairs)
         + reduce_sems(out_chunks)
@@ -1677,6 +1722,30 @@
         home_grad, back, hidden, cotangent, tokens, vectors, router_grad,
         far_sums, near_sums, home_out, act_t, merged_t, qkv, weight, w_out, low, high,
     )
+
+
+def widen_kernel(*refs):
+    count = len(refs) // 2
+    for src, dst in zip(refs[:count], refs[count:]):
+        dst[...] = src[...].astype(dst.dtype)
+
+
+def widen(steps, values, kinds):
+    def spec(value):
+        if value.shape[0] % (16 * steps):
+            return pl.BlockSpec(value.shape, lambda i: (0, 0))
+        return pl.BlockSpec((value.shape[0] // steps, value.shape[1]), lambda i: (i, 0))
+
+    return pl.pallas_call(
+        widen_kernel,
+        grid=(steps,),
+        in_specs=[spec(value) for value in values],
+        out_specs=[spec(value) for value in values],
+        out_shape=[
+            jax.ShapeDtypeStruct(value.shape, kind) for value, kind in zip(values, kinds)
+        ],
+        name="widen",
+    )(*values)
 
 
 def on_device_plain(
@@ -1899,6 +1968,16 @@
         owners, capacity, expert_count, home_grad, far_sums, near_sums, home_out, back, hidden, cotangent,
         tokens, vectors, grad_router, act_t, merged_t, qkv, weight, out_full, low, high,
     )
+    f32 = jnp.float32
+    units = w_up.shape[2]
+    output, grad_tokens, grad_vectors, grad_gates, grad_qkv, grad_out, grad_up, grad_down = widen(
+        16,
+        (
+            output, grad_tokens, grad_vectors, grad_gates, grad_qkv, grad_out,
+            grad_up.reshape(-1, units), grad_down.reshape(-1, model_width),
+        ),
+        (output.dtype,) + (f32,) * 7,
+    )
     return (
         output,
         grad_tokens,
@@ -1909,8 +1988,8 @@
         grad_vectors[2],
         grad_vectors[3],
         grad_gates.T,
-        grad_up.astype(jnp.float32),
-        grad_down.astype(jnp.float32),
+        grad_up.reshape(w_up.shape),
+        grad_down.reshape(w_down.shape),
     )
 
 
@@ -1935,7 +2014,7 @@
 
     def body(*args):
         capacity = args[0].shape[0] // args[7].shape[1]
-        fits = group == 4 and owners in (4, 8, 16) and capacity % 16 == 0 and args[7].shape[1] % 16 == 0
+        fits = group == 4 and owners == 8 and capacity % 16 == 0 and args[7].shape[1] % 16 == 0
         return (on_device if fits else on_device_plain)(*args)
 
     return jax.shard_map(

time: 287 us -> 277 us (0.965)
  other arithmetic: 12.6 us -> 1.4 us
  Pallas kernels: 265 us -> 272 us
  local copies, waits for them, and re-layouts: 7.99 us -> 1.43 us
    pallas_call x0 -> x1, Pallas kernels: none -> 16.7 us  [widen(): pl.pallas_call(widen_kernel, grid=(steps,), in_specs=[spec(value) for val...]
    convert_element_type x2 -> x0, other arithmetic: 11.2 us -> none  [the longest x1 6.79 us: on_device(): grad_up.astype(jnp.float32)]
    pallas_call x1, Pallas kernels: 95.4 us -> 85.7 us  [run_experts(): pl.pallas_call(functools.partial(expert_kernel, dims), out_shape=(jax.Sha...]
    unnamed x17 -> x0, local copies, waits for them, and re-layouts: 6.57 us -> none
where the time goes in v4:
time: 277 us; the launch traced here: 276 us
  Pallas kernels  272 us (98%)
    pallas_call x1, Pallas kernels, run_back(): pl.pallas_call(functools.partial(back_kernel, (owners, capacity, gates)),...  102 us
    pallas_call x1, Pallas kernels, run_experts(): pl.pallas_call(functools.partial(expert_kernel, dims), out_shape=(jax.Sha...  85.7 us
    pallas_call x1, Pallas kernels, run_front(): pl.pallas_call(functools.partial(front_kernel, (owners, capacity, pieces)...  67.2 us
    pallas_call x1, Pallas kernels, widen(): pl.pallas_call(widen_kernel, grid=(steps,), in_specs=[spec(value) for val...  16.7 us

profile of v4, /device:TPU:0, one launch (start us, length us, event | category | flops | bytes accessed | tf_op | source)
XLA Modules:
  0.0 276.0 jit_solution(4380507159179598886)
XLA Ops:
  1.3 1.4 select_select_fusion.small_hbm
  2.7 67.2 %front.1 = (bf16[512,3072]{1,0:T(8,128)(2,1)}, bf16[1024,512]{1,0:T(8,128)(2,1)}, bf16[1024,512]{1,0:T(8,128)(2,1)}, bf16[512,512]{1,0:T(8,128)(2,1)}, bf16[1024...) custom-call(s32[1]{0:T(128)S(6)} %copy.25.prefix_ref, ...), custom_call_target="tpu_custom_call" | custom-call | tf_op jit(solution)/shard_map/front/pallas_call | solution.py:1158
  69.9 85.7 %experts.1 = (bf16[2,256,1024]{2,1,0:T(8,128)(2,1)}, bf16[2,256,1024]{2,1,0:T(8,128)(2,1)}, bf16[8,2,32,1024]{3,2,1,0:T(8,128)(2,1)}, bf16[8,2,32,1024]{3,2,1,0:...) custom-call(bf16[8,2,32,1024]{3,2,1,0:T(8,128)(2,1)} %get-tuple-element.45.send_r, ...), custom_call_target="tpu_custom_call" | custom-call | tf_op jit(solution)/shard_map/experts/pallas_call | solution.py:706
  155.6 102.2 %back.1 = (bf16[512,1024]{1,0:T(8,128)(2,1)}, f32[512,1024]{1,0:T(8,128)}, f32[8,256]{1,0:T(8,128)}, f32[16,256]{1,0:T(8,128)}, bf16[256,3072]{1,0:T(8,128)(2,1)}, /*index=5*/bf16[256,1024]{1,0:T(8,128)(2,1)}) custom-call(bf16[8,2,32,1024]{3,2,1,0:T(8,128)(2,1)} %get-tuple-element.48.home_grad_ref, bf16[512,512]{1,0:T(8,128)(2,1)} %get-tuple-element.49.back_ref, ...), custom_call_target="tpu_custom_call" | custom-call | tf_op jit(solution)/shard_map/back/pallas_call | solution.py:1668
  257.8 16.7 %widen.1 = (bf16[512,1024]{1,0:T(8,128)(2,1)}, f32[512,1024]{1,0:T(8,128)}, f32[8,256]{1,0:T(8,128)}, f32[16,256]{1,0:T(8,128)}, f32[256,3072]{1,0:T(8,128)}, /*...) custom-call(bf16[512,1024]{1,0:T(8,128)(2,1)} %get-tuple-element.63.refs_0_, ...), custom_call_target="tpu_custom_call" | custom-call | tf_op jit(solution)/shard_map/widen/pallas_call | solution.py:1739
  274.6 1.4 fusion
  (2 shorter events, 0.0 us)

commit v5 on v4

--- a/solution.py
+++ b/solution.py
@@ -15,7 +15,7 @@
 epsilon = 1e-05
 VMEM_LIMIT = 66_000_000
 TILE = 1024
-EARLY_CHUNKS = 2
+EARLY_CHUNKS = 1
 
 
 def normalize(values, gain_vec, shift_vec):
@@ -338,8 +338,7 @@
         self.relayed(k).wait_recv()
 
     def order(self):
-        near, far = list(range(0, self.p.owners, 2)), list(range(1, self.p.owners, 2))
-        return near[:3] + far[:1] + near[3:] + far[1:]
+        return (0, 2, 4, 1, 6, 3, 5, 7)
 
     def drain(self):
         every(1, self.p.owners, lambda k: self.direct(k).wait_send())
@@ -594,48 +593,48 @@
         ]
 
     turns = [(j, expert) for j in range(chunks) for expert in range(experts)]
-    order = dispatch.order()
-    waiting, moved = order[4:], set(order[:4])
+    ahead, through, here = dispatch.forward, dispatch.relay, dispatch.ready
     plan = [[] for _ in turns]
-
-    def forward_to(acts, count):
-        for _ in range(min(count, len(waiting))):
-            n = waiting.pop(0)
-            moved.add(n)
-            acts.append((dispatch.forward, n))
-
-    for u, (j, expert) in enumerate(turns):
-        acts = plan[u]
-        pair = (2 * j, 2 * j + 1)
-        if expert == 0:
-            if j > 0:
-                while not moved.issuperset(pair):
-                    forward_to(acts, 1)
-                for n in pair:
-                    acts.append((dispatch.relay, n))
-            for n in pair:
-                acts.append((dispatch.ready, n))
-        if u > 0:
-            forward_to(acts, 2)
-        if u >= 2:
-            last = turns[u - 2]
-            acts.append((ret_grad.cross,) + last)
-            acts.append((ret_out.cross if last[0] < early else ret_out.split,) + last)
+    for unit, acts in (
+        (0, ((here, 0), (here, 1), (ahead, 5))),
+        (1, ((through, 6), (ahead, 7))),
+        (2, ((through, 3), (here, 2), (here, 3))),
+        (3, ((through, 5),)),
+        (4, ((through, 7), (here, 4), (here, 5))),
+        (6, ((here, 6), (here, 7))),
+    ):
+        plan[unit].extend(acts)
+    for u in range(2, len(turns)):
+        done = turns[u - 2]
+        plan[u].append((ret_grad.cross,) + done)
+        plan[u].append((ret_out.cross if done[0] < early else ret_out.split,) + done)
         if u >= 4:
-            last = turns[u - 4]
-            acts.append((ret_grad.finish,) + last)
-            if last[0] < early:
-                acts.append((ret_out.finish,) + last)
+            done = turns[u - 4]
+            plan[u].append((ret_grad.finish,) + done)
+            if done[0] < early:
+                plan[u].append((ret_out.finish,) + done)
     ret_out.keep = keep_out
     for load in loads:
         load.wait()
-    for n in order[:4]:
-        dispatch.forward(n)
-        j = n // 2 if n % 2 == 0 else chunks - 1
+
+    def unscaled_pair(j):
         for expert in range(experts):
             unscaled(j, expert)
-    dispatch.relay(0)
-    dispatch.relay(1)
+
+    ahead(0)
+    unscaled_pair(0)
+    unscaled_pair(1)
+    ahead(2)
+    ahead(4)
+    ahead(1)
+    unscaled_pair(2)
+    through(0)
+    unscaled_pair(3)
+    through(2)
+    ahead(6)
+    through(4)
+    through(1)
+    ahead(3)
 
     def step(unit):
         for u, acts in enumerate(plan):
@@ -1322,6 +1321,50 @@
         every(0, self.chunks, one)
 
 
+class PairFirst(Reduce):
+    def folded(self, n):
+        other = span((1 - self.bit) * self.halves, self.halves)
+        return self.step(
+            2, n, self.part.at[n, :, self.p.c, other], self.pair.at[n], (self.p.pair, self.p.w)
+        )
+
+    def crossed(self, n):
+        own = span(self.bit * self.halves, self.halves)
+        return self.step(
+            1, n, self.part.at[n, 1 - self.p.x, self.p.c, own], self.far.at[n],
+            (self.p.e, self.p.far),
+        )
+
+    def fold(self, n):
+        self.swapped(n).wait_recv()
+        for side in range(2):
+            self.part[n, side, self.p.c] = self.pair_sum(n, side).astype(jnp.bfloat16)
+        self.folded(n).start()
+
+    def cross(self, n):
+        self.folded(n).wait_recv()
+        own = span(self.bit * self.halves, self.halves)
+        for side in range(2):
+            total = self.part[n, side, self.p.c, own, :].astype(jnp.float32) + self.pair[
+                n, side
+            ].astype(jnp.float32)
+            self.part[n, side, self.p.c, own, :] = total.astype(jnp.bfloat16)
+        self.crossed(n).start()
+
+    def spread(self, n):
+        self.crossed(n).wait_recv()
+        own = span(self.bit * self.halves, self.halves)
+        total = self.part[n, self.p.x, self.p.c, own, :].astype(jnp.float32) + self.far[
+            n
+        ].astype(jnp.float32)
+        self.part[n, self.p.x, self.p.c, own, :] = total.astype(jnp.bfloat16)
+        for k in range(1, self.count):
+            self.spreads(n, k).start()
+
+    def stages(self):
+        return (self.fold, self.cross, self.spread, self.collect, self.share, self.finish)
+
+
 class Small:
     def __init__(self, place, value, part, got, mid, far, total, others, out, sems):
         self.p, self.value, self.part, self.got, self.mid = place, value, part, got, mid
@@ -1391,7 +1434,7 @@
     far_hbm, near_hbm, home_hbm, act_hbm, merged_hbm, qkv_hbm, weight_hbm, out_hbm, low_hbm, high_hbm,
     output_ref, tokens_out, vectors_out, gates_out, qkv_out, out_out,
     near_sums, far_sums, done_rows, home_out,
-    act_t, merged_t, qkv, weight, out_w, low_buf, high_buf, attn, grad_merged,
+    act_t, merged_t, qkv, weight, out_w, low_buf, high_buf, attn, grad_merged, grad_act,
     part_q, got_q, far_q, pair_q, lines_q, done_q,
     part_o, got_o, far_o, pair_o, lines_o, done_o,
     small, small_part, small_got, small_mid, small_far, small_sum, small_all,
@@ -1434,15 +1477,19 @@
         place, capacity, near_sums, None, far_hbm, far_sums, done_rows, home_out,
         (own_sem, cross_send, cross_recv, home_send, home_recv),
     )
-    for expert in range(experts):
-        every(EARLY_CHUNKS, groups, lambda j: late.crossed(j, expert).start())
+
+    def start_late(j):
+        for expert in range(experts):
+            late.crossed(j, expert).start()
+
+    every(EARLY_CHUNKS, groups, start_late)
 
     def early_rows(n):
         row = place.peer(n)
         return pltpu.make_async_copy(home_hbm.at[row], home_out.at[row], early_sem.at[n])
 
     every(0, 2 * EARLY_CHUNKS, lambda n: early_rows(n).start())
-    reduce_o = Reduce(
+    reduce_o = PairFirst(
         place, part_o, got_o, far_o, pair_o, lines_o, done_o, (send_o, recv_o, lsend_o, lrecv_o)
     )
     reduce_q = Reduce(
@@ -1499,8 +1546,12 @@
         grad_merged[part, :] = dot_nt(attn[part, :], out_w[...]).astype(jnp.bfloat16)
 
     every(0, rows // band, merged_band)
-    for load in loads[2:4] + loads[5:]:
+    stages_o, stages_q = reduce_o.stages(), reduce_q.stages()
+    for n in range(out_chunks):
+        stages_o[0](n)
+    for load in loads[2:]:
         load.wait()
+    grad_act[...] = jnp.zeros_like(grad_act)
     pairs = part_q.shape[0]
 
     def attend_pair(i):
@@ -1536,10 +1587,14 @@
         )
         weight_grad(part_q, i, act_t, right)
         reduce_q.swap(i)
+        columns = jnp.concatenate(
+            [weight[:, span(which * width + i * LANES, LANES)] for which in range(3)], axis=1
+        )
+        grad_act[...] += dot_nt(right, columns)
 
     def input_band(i):
         part = span(i * band, band)
-        grad = dot_nt(grad_qkv[part, :], weight[...])
+        grad = grad_act[part, :]
         scaled, inverse = norm_stats(tokens_ref[part, :].astype(jnp.float32))
         tokens_out[part, :] += norm_back_rows(grad, scaled, inverse, gain_one)
         small[0:1, :] += jnp.sum(grad * scaled, axis=0, keepdims=True)
@@ -1566,7 +1621,6 @@
             done_o.at[n], out_out.at[:, span(n * tile_o, tile_o)], out_sem.at[3, n]
         )
 
-    stages_o, stages_q = reduce_o.stages(), reduce_q.stages()
     delays = (1, 3, 4, 5, 6, 7)
     last = len(delays) - 1
     half = rows // band // 2
@@ -1588,7 +1642,7 @@
                     for copy in store_q(n):
                         copy.start()
 
-            @pl.when(slot == delays[s] - 1)
+            @pl.when(slot == (delays[s] - 2 if s else -1))
             def _(s=s):
                 for n in range(out_chunks):
                     stages_o[s](n)
@@ -1597,7 +1651,6 @@
 
         @pl.when(slot == pairs)
         def _():
-            loads[4].wait()
             every(0, half, input_band)
 
         pl.when(slot == pairs + 1)(lambda: every(half, 2 * half, input_band))
@@ -1652,12 +1705,13 @@
     def fm(*shape):
         return pltpu.VMEM(shape, f32)
 
-    def reduce_buffers(chunks, tile):
+    def reduce_buffers(chunks, tile, pair_first):
+        far, pair = ((half,), (2, half)) if pair_first else ((shard,), (half,))
         return [
             vm(chunks, 2, 2, shard, tile),
             vm(chunks, 2, shard, tile),
-            vm(chunks, shard, tile),
-            vm(chunks, half, tile),
+            vm(chunks, *far, tile),
+            vm(chunks, *pair, tile),
             vm(chunks, count, half // count, tile),
             vm(chunks, shard, tile),
         ]
@@ -1691,9 +1745,10 @@
             vm(2, 2, mid, rows),
             vm(rows, width),
             vm(rows, width),
+            fm(rows, width),
         ]
-        + reduce_buffers(pairs, 3 * LANES)
-        + reduce_buffers(out_chunks, tile_o)
+        + reduce_buffers(pairs, 3 * LANES, False)
+        + reduce_buffers(out_chunks, tile_o, True)
         + [
             fm(lead, width),
             fm(2, 2, lead, shard),
@@ -1970,13 +2025,13 @@
     )
     f32 = jnp.float32
     units = w_up.shape[2]
-    output, grad_tokens, grad_vectors, grad_gates, grad_qkv, grad_out, grad_up, grad_down = widen(
-        16,
+    output, grad_tokens, grad_gates, grad_qkv, grad_out, grad_up, grad_down = widen(
+        2,
         (
-            output, grad_tokens, grad_vectors, grad_gates, grad_qkv, grad_out,
+            output, grad_tokens, grad_gates, grad_qkv, grad_out,
             grad_up.reshape(-1, units), grad_down.reshape(-1, model_width),
         ),
-        (output.dtype,) + (f32,) * 7,
+        (output.dtype,) + (f32,) * 6,
     )
     return (
         output,

time: 277 us -> 271 us (0.978)
  Pallas kernels: 272 us -> 266 us
    pallas_call x1, Pallas kernels: 85.7 us -> 75.6 us  [run_experts(): pl.pallas_call(functools.partial(expert_kernel, dims), out_shape=(jax.Sha...]
    pallas_call x1, Pallas kernels: 102 us -> 111 us  [run_back(): pl.pallas_call(functools.partial(back_kernel, (owners, capacity, gates)),...]
    pallas_call x1, Pallas kernels: 16.7 us -> 12.2 us  [widen(): pl.pallas_call(widen_kernel, grid=(steps,), in_specs=[spec(value) for val...]
where the time goes in v5:
time: 271 us; the launch traced here: 270 us
  Pallas kernels  266 us (98%)
    pallas_call x1, Pallas kernels, run_back(): pl.pallas_call(functools.partial(back_kernel, (owners, capacity, gates)),...  111 us
    pallas_call x1, Pallas kernels, run_experts(): pl.pallas_call(functools.partial(expert_kernel, dims), out_shape=(jax.Sha...  75.6 us
    pallas_call x1, Pallas kernels, run_front(): pl.pallas_call(functools.partial(front_kernel, (owners, capacity, pieces)...  67.2 us
    pallas_call x1, Pallas kernels, widen(): pl.pallas_call(widen_kernel, grid=(steps,), in_specs=[spec(value) for val...  12.2 us

profile of v5, /device:TPU:0, one launch (start us, length us, event | category | flops | bytes accessed | tf_op | source)
XLA Modules:
  0.0 270.3 jit_solution(588066310280719553)
XLA Ops:
  1.3 1.4 select_select_fusion.small_hbm
  2.7 67.2 %front.1 = (bf16[512,3072]{1,0:T(8,128)(2,1)}, bf16[1024,512]{1,0:T(8,128)(2,1)}, bf16[1024,512]{1,0:T(8,128)(2,1)}, bf16[512,512]{1,0:T(8,128)(2,1)}, bf16[1024...) custom-call(s32[1]{0:T(128)S(6)} %copy.25.prefix_ref, ...), custom_call_target="tpu_custom_call" | custom-call | tf_op jit(solution)/shard_map/front/pallas_call | solution.py:1157
  69.9 75.6 %experts.1 = (bf16[2,256,1024]{2,1,0:T(8,128)(2,1)}, bf16[2,256,1024]{2,1,0:T(8,128)(2,1)}, bf16[8,2,32,1024]{3,2,1,0:T(8,128)(2,1)}, bf16[8,2,32,1024]{3,2,1,0:...) custom-call(bf16[8,2,32,1024]{3,2,1,0:T(8,128)(2,1)} %get-tuple-element.44.send_r, ...), custom_call_target="tpu_custom_call" | custom-call | tf_op jit(solution)/shard_map/experts/pallas_call | solution.py:705
  145.5 111.1 %back.1 = (bf16[512,1024]{1,0:T(8,128)(2,1)}, f32[512,1024]{1,0:T(8,128)}, f32[8,256]{1,0:T(8,128)}, f32[16,256]{1,0:T(8,128)}, bf16[256,3072]{1,0:T(8,128)(2,1)}, /*index=5*/bf16[256,1024]{1,0:T(8,128)(2,1)}) custom-call(bf16[8,2,32,1024]{3,2,1,0:T(8,128)(2,1)} %get-tuple-element.47.home_grad_ref, bf16[512,512]{1,0:T(8,128)(2,1)} %get-tuple-element.48.back_ref, ...), custom_call_target="tpu_custom_call" | custom-call | tf_op jit(solution)/shard_map/back/pallas_call | solution.py:1722
  256.6 1.4 fusion
  258.0 12.2 %widen.1 = (bf16[512,1024]{1,0:T(8,128)(2,1)}, f32[512,1024]{1,0:T(8,128)}, f32[16,256]{1,0:T(8,128)}, f32[256,3072]{1,0:T(8,128)}, f32[256,1024]{1,0:T(8,128)},...) custom-call(bf16[512,1024]{1,0:T(8,128)(2,1)} %get-tuple-element.62.refs_0_, f32[512,1024]{1,0:T(8,128)} %get-tuple-element.63.refs_1_, ...), custom_call_target="tpu_custom_call" | custom-call | tf_op jit(solution)/shard_map/widen/pallas_call | solution.py:1794
  (2 shorter events, 0.0 us)

commit v6 on v5

--- a/solution.py
+++ b/solution.py
@@ -240,6 +240,9 @@
 
     def ahead(self, k):
         return lax.rem(self.e + k, self.owners)
+
+    def flip(self, bit):
+        return self.e + bit * (1 - 2 * lax.rem(lax.div(self.e, bit), 2))
 
     def peer(self, n):
         other = lax.div(n, 2) + lax.rem(n, 2) * (self.owners // 2)
@@ -1205,17 +1208,16 @@
 
 
 class Reduce:
-    def __init__(self, place, part, got, far, pair, lines, done, sems):
+    def __init__(self, place, part, got, far, pair, near, line, done, sems):
         self.p = place
         self.part, self.got, self.far = part, got, far
-        self.pair, self.lines, self.done = pair, lines, done
-        self.send, self.recv, self.line_send, self.line_recv = sems
+        self.pair, self.near, self.line, self.done = pair, near, line, done
+        self.send, self.recv = sems
         self.chunks = part.shape[0]
         self.halves = done.shape[1] // 2
-        self.count = place.owners // 2
-        self.slice = self.halves // self.count
         self.bit = lax.rem(place.e, 2)
-        self.level = lax.div(place.e, 2)
+        self.low = lax.rem(lax.div(place.e, 2), 2)
+        self.high = lax.div(place.e, 4)
 
     def step(self, which, n, src, dst, device):
         return remote(src, dst, self.send.at[which, n], self.recv.at[which, n], device)
@@ -1241,24 +1243,39 @@
         part = self.done.at[n, span(self.bit * self.halves, self.halves)]
         return self.step(3, n, part, part, (self.p.pair, self.p.w))
 
-    def line(self, which, n, k, src, dst):
-        return remote(
-            src, dst, self.line_send.at[which, n, k], self.line_recv.at[which, n, k],
-            (self.p.ahead(2 * k), self.p.w),
-        )
-
-    def row(self, level):
-        return span(self.bit * self.halves + level * self.slice, self.slice)
-
-    def spreads(self, n, k):
-        target = lax.rem(self.level + k, self.count)
-        return self.line(
-            0, n, k, self.part.at[n, self.p.x, self.p.c, self.row(target)], self.lines.at[n, k]
-        )
-
-    def collects(self, n, k):
-        part = self.done.at[n, self.row(self.level)]
-        return self.line(1, n, k, part, part)
+    def quarter(self, low):
+        size = self.halves // 2
+        return span(self.bit * self.halves + low * size, size)
+
+    def eighth(self, high):
+        size = self.halves // 4
+        return span(self.bit * self.halves + (self.low * 2 + high) * size, size)
+
+    def nears(self, n):
+        return self.step(
+            4, n, self.part.at[n, self.p.x, self.p.c, self.quarter(1 - self.low)],
+            self.near.at[n], (self.p.flip(2), self.p.w),
+        )
+
+    def lines(self, n):
+        return self.step(
+            5, n, self.part.at[n, self.p.x, self.p.c, self.eighth(1 - self.high)],
+            self.line.at[n], (self.p.flip(4), self.p.w),
+        )
+
+    def line_back(self, n):
+        part = self.done.at[n, self.eighth(self.high)]
+        return self.step(6, n, part, part, (self.p.flip(4), self.p.w))
+
+    def near_back(self, n):
+        part = self.done.at[n, self.quarter(self.low)]
+        return self.step(7, n, part, part, (self.p.flip(2), self.p.w))
+
+    def add(self, n, rows, other):
+        total = self.part[n, self.p.x, self.p.c, rows, :].astype(jnp.float32) + other.astype(
+            jnp.float32
+        )
+        return total.astype(jnp.bfloat16)
 
     def pair_sum(self, n, side):
         return self.part[n, side, self.p.c].astype(jnp.float32) + self.got[n, side].astype(
@@ -1283,40 +1300,45 @@
     def spread(self, n):
         self.folded(n).wait_recv()
         own = span(self.bit * self.halves, self.halves)
-        total = self.part[n, self.p.x, self.p.c, own, :].astype(jnp.float32) + self.pair[
-            n
-        ].astype(jnp.float32)
-        self.part[n, self.p.x, self.p.c, own, :] = total.astype(jnp.bfloat16)
-        for k in range(1, self.count):
-            self.spreads(n, k).start()
+        self.part[n, self.p.x, self.p.c, own, :] = self.add(n, own, self.pair[n])
+        self.nears(n).start()
+
+    def reach(self, n):
+        self.nears(n).wait_recv()
+        own = self.quarter(self.low)
+        self.part[n, self.p.x, self.p.c, own, :] = self.add(n, own, self.near[n])
+        self.lines(n).start()
 
     def collect(self, n):
-        total = self.part[n, self.p.x, self.p.c, self.row(self.level), :].astype(jnp.float32)
-        for k in range(1, self.count):
-            self.spreads(n, k).wait_recv()
-            total = total + self.lines[n, k].astype(jnp.float32)
-        self.done[n, self.row(self.level), :] = total.astype(jnp.bfloat16)
-        for k in range(1, self.count):
-            self.collects(n, k).start()
+        self.lines(n).wait_recv()
+        own = self.eighth(self.high)
+        self.done[n, own, :] = self.add(n, own, self.line[n])
+        self.line_back(n).start()
+
+    def widen_back(self, n):
+        self.line_back(n).wait_recv()
+        self.near_back(n).start()
 
     def share(self, n):
-        for k in range(1, self.count):
-            self.collects(n, k).wait_recv()
+        self.near_back(n).wait_recv()
         self.shared(n).start()
 
     def finish(self, n):
         self.shared(n).wait_recv()
 
+    def line_stages(self):
+        return (self.spread, self.reach, self.collect, self.widen_back, self.share, self.finish)
+
     def stages(self):
-        return (self.cross, self.fold, self.spread, self.collect, self.share, self.finish)
+        return (self.cross, self.fold) + self.line_stages()
 
     def drain(self):
         def one(n):
-            for copy in (self.swapped(n), self.crossed(n), self.folded(n), self.shared(n)):
+            for copy in (
+                self.swapped(n), self.crossed(n), self.folded(n), self.shared(n), self.nears(n),
+                self.lines(n), self.line_back(n), self.near_back(n),
+            ):
                 copy.wait_send()
-            for k in range(1, self.count):
-                self.spreads(n, k).wait_send()
-                self.collects(n, k).wait_send()
 
         every(0, self.chunks, one)
 
@@ -1354,15 +1376,11 @@
     def spread(self, n):
         self.crossed(n).wait_recv()
         own = span(self.bit * self.halves, self.halves)
-        total = self.part[n, self.p.x, self.p.c, own, :].astype(jnp.float32) + self.far[
-            n
-        ].astype(jnp.float32)
-        self.part[n, self.p.x, self.p.c, own, :] = total.astype(jnp.bfloat16)
-        for k in range(1, self.count):
-            self.spreads(n, k).start()
+        self.part[n, self.p.x, self.p.c, own, :] = self.add(n, own, self.far[n])
+        self.nears(n).start()
 
     def stages(self):
-        return (self.fold, self.cross, self.spread, self.collect, self.share, self.finish)
+        return (self.fold, self.cross) + self.line_stages()
 
 
 class Small:
@@ -1435,10 +1453,10 @@
     output_ref, tokens_out, vectors_out, gates_out, qkv_out, out_out,
     near_sums, far_sums, done_rows, home_out,
     act_t, merged_t, qkv, weight, out_w, low_buf, high_buf, attn, grad_merged, grad_act,
-    part_q, got_q, far_q, pair_q, lines_q, done_q,
-    part_o, got_o, far_o, pair_o, lines_o, done_o,
+    part_q, got_q, far_q, pair_q, near_q, line_q, done_q,
+    part_o, got_o, far_o, pair_o, near_o, line_o, done_o,
     small, small_part, small_got, small_mid, small_far, small_sum, small_all,
-    load_sem, prob_sem, own_sem, early_sem, cross_send, cross_recv, home_send, home_recv, send_q, recv_q, lsend_q, lrecv_q, send_o, recv_o, lsend_o, lrecv_o,
+    load_sem, prob_sem, own_sem, early_sem, cross_send, cross_recv, home_send, home_recv, send_q, recv_q, send_o, recv_o,
     small_send, small_recv, all_send, all_recv, out_sem,
 ):
     owners, capacity, gates = dims
@@ -1490,10 +1508,10 @@
 
     every(0, 2 * EARLY_CHUNKS, lambda n: early_rows(n).start())
     reduce_o = PairFirst(
-        place, part_o, got_o, far_o, pair_o, lines_o, done_o, (send_o, recv_o, lsend_o, lrecv_o)
+        place, part_o, got_o, far_o, pair_o, near_o, line_o, done_o, (send_o, recv_o)
     )
     reduce_q = Reduce(
-        place, part_q, got_q, far_q, pair_q, lines_q, done_q, (send_q, recv_q, lsend_q, lrecv_q)
+        place, part_q, got_q, far_q, pair_q, near_q, line_q, done_q, (send_q, recv_q)
     )
     smalls = Small(
         place, small, small_part, small_got, small_mid, small_far, small_sum, small_all, (vectors_out, gates_out),
@@ -1528,11 +1546,8 @@
     loads[0].wait()
 
     def weight_grad(part, n, left, right):
-        def one(owner):
-            value = dot_nn(left[span(owner * shard, shard), :], right)
-            part[n, lax.div(owner, 2), lax.rem(owner, 2)] = value.astype(jnp.bfloat16)
-
-        every(0, 4, one)
+        value = dot_nn(left[...], right).astype(jnp.bfloat16)
+        part[n] = value.reshape(part.shape[1:])
 
     tile_o = part_o.shape[-1]
     out_chunks = part_o.shape[0]
@@ -1621,7 +1636,8 @@
             done_o.at[n], out_out.at[:, span(n * tile_o, tile_o)], out_sem.at[3, n]
         )
 
-    delays = (1, 3, 4, 5, 6, 7)
+    delays = (1, 3, 4, 5, 6, 7, 8, 9)
+    turns_o = (-1, 3, 5, 6, 7, 8, 9, 10)
     last = len(delays) - 1
     half = rows // band // 2
 
@@ -1642,7 +1658,7 @@
                     for copy in store_q(n):
                         copy.start()
 
-            @pl.when(slot == (delays[s] - 2 if s else -1))
+            @pl.when(slot == turns_o[s])
             def _(s=s):
                 for n in range(out_chunks):
                     stages_o[s](n)
@@ -1691,7 +1707,6 @@
     pairs = width // LANES
     tile_o = min(512, width)
     out_chunks = width // tile_o
-    count = owners // 2
     half = shard // 2
     mid = rows // 2
     any_spec = pl.BlockSpec(memory_space=pl.ANY)
@@ -1712,12 +1727,13 @@
             vm(chunks, 2, shard, tile),
             vm(chunks, *far, tile),
             vm(chunks, *pair, tile),
-            vm(chunks, count, half // count, tile),
+            vm(chunks, half // 2, tile),
+            vm(chunks, half // 4, tile),
             vm(chunks, shard, tile),
         ]
 
     def reduce_sems(chunks):
-        return [dma((4, chunks)), dma((4, chunks)), dma((2, chunks, count)), dma((2, chunks, count))]
+        return [dma((8, chunks)), dma((8, chunks))]
 
     return pl.pallas_call(
         functools.partial(back_kernel, (owners, capacity, gates)),

time: 271 us -> 264 us (0.974)
  Pallas kernels: 266 us -> 259 us
    pallas_call x1, Pallas kernels: 111 us -> 104 us  [run_back(): pl.pallas_call(functools.partial(back_kernel, (owners, capacity, gates)),...]
where the time goes in v6:
time: 264 us; the launch traced here: 263 us
  Pallas kernels  259 us (98%)
    pallas_call x1, Pallas kernels, run_back(): pl.pallas_call(functools.partial(back_kernel, (owners, capacity, gates)),...  104 us
    pallas_call x1, Pallas kernels, run_experts(): pl.pallas_call(functools.partial(expert_kernel, dims), out_shape=(jax.Sha...  75.6 us
    pallas_call x1, Pallas kernels, run_front(): pl.pallas_call(functools.partial(front_kernel, (owners, capacity, pieces)...  67.2 us
    pallas_call x1, Pallas kernels, widen(): pl.pallas_call(widen_kernel, grid=(steps,), in_specs=[spec(value) for val...  12.2 us

profile of v6, /device:TPU:0, one launch (start us, length us, event | category | flops | bytes accessed | tf_op | source)
XLA Modules:
  0.0 263.4 jit_solution(7280347292126823438)
XLA Ops:
  1.3 1.4 select_select_fusion.small_hbm
  2.7 67.2 %front.1 = (bf16[512,3072]{1,0:T(8,128)(2,1)}, bf16[1024,512]{1,0:T(8,128)(2,1)}, bf16[1024,512]{1,0:T(8,128)(2,1)}, bf16[512,512]{1,0:T(8,128)(2,1)}, bf16[1024...) custom-call(s32[1]{0:T(128)S(6)} %copy.25.prefix_ref, ...), custom_call_target="tpu_custom_call" | custom-call | tf_op jit(solution)/shard_map/front/pallas_call | solution.py:1160
  69.9 75.6 %experts.1 = (bf16[2,256,1024]{2,1,0:T(8,128)(2,1)}, bf16[2,256,1024]{2,1,0:T(8,128)(2,1)}, bf16[8,2,32,1024]{3,2,1,0:T(8,128)(2,1)}, bf16[8,2,32,1024]{3,2,1,0:...) custom-call(bf16[8,2,32,1024]{3,2,1,0:T(8,128)(2,1)} %get-tuple-element.44.send_r, ...), custom_call_target="tpu_custom_call" | custom-call | tf_op jit(solution)/shard_map/experts/pallas_call | solution.py:708
  145.5 104.1 %back.1 = (bf16[512,1024]{1,0:T(8,128)(2,1)}, f32[512,1024]{1,0:T(8,128)}, f32[8,256]{1,0:T(8,128)}, f32[16,256]{1,0:T(8,128)}, bf16[256,3072]{1,0:T(8,128)(2,1)}, /*index=5*/bf16[256,1024]{1,0:T(8,128)(2,1)}) custom-call(bf16[8,2,32,1024]{3,2,1,0:T(8,128)(2,1)} %get-tuple-element.47.home_grad_ref, bf16[512,512]{1,0:T(8,128)(2,1)} %get-tuple-element.48.back_ref, ...), custom_call_target="tpu_custom_call" | custom-call | tf_op jit(solution)/shard_map/back/pallas_call | solution.py:1738
  249.6 1.4 fusion
  251.1 12.2 %widen.1 = (bf16[512,1024]{1,0:T(8,128)(2,1)}, f32[512,1024]{1,0:T(8,128)}, f32[16,256]{1,0:T(8,128)}, f32[256,3072]{1,0:T(8,128)}, f32[256,1024]{1,0:T(8,128)},...) custom-call(bf16[512,1024]{1,0:T(8,128)(2,1)} %get-tuple-element.62.refs_0_, f32[512,1024]{1,0:T(8,128)} %get-tuple-element.63.refs_1_, ...), custom_call_target="tpu_custom_call" | custom-call | tf_op jit(solution)/shard_map/widen/pallas_call | solution.py:1810
  (2 shorter events, 0.0 us)

commit v7 on v6

--- a/solution.py
+++ b/solution.py
@@ -1095,15 +1095,22 @@
             pl.when(n == i // share)(functools.partial(dispatch.forward, partner))
         gathers[0].ready(n)
         project(n)
+        pl.when(n >= 2)(lambda: gathers[1].pass_on(n - 2))
+
+        @pl.when(n == pieces - 1)
+        def _():
+            gathers[1].pass_on(pieces - 2)
+            gathers[1].pass_pair(0)
+
         for i in range(group):
             attend_pair(n * group + i)
 
     every(0, pieces, front_step)
+    gathers[1].pass_on(pieces - 1)
+    every(1, pieces, gathers[1].pass_pair)
     turned[1] = merged[...].T
     for i in (0, 3, 4):
         stores[i].start()
-    every(0, pieces, gathers[1].pass_on)
-    every(0, pieces, gathers[1].pass_pair)
     order = dispatch.order()
     dispatch.relay(order[0])
     every(0, pieces, gathers[1].ready)
@@ -1795,13 +1802,15 @@
     )
 
 
-def widen_kernel(*refs):
-    count = len(refs) // 2
+def widen_kernel(vectors_ref, *refs):
+    count = (len(refs) - 4) // 2
     for src, dst in zip(refs[:count], refs[count:]):
         dst[...] = src[...].astype(dst.dtype)
-
-
-def widen(steps, values, kinds):
+    for i, dst in enumerate(refs[2 * count :]):
+        dst[...] = vectors_ref[i, :]
+
+
+def widen(steps, vectors, values, kinds):
     def spec(value):
         if value.shape[0] % (16 * steps):
             return pl.BlockSpec(value.shape, lambda i: (0, 0))
@@ -1810,13 +1819,16 @@
     return pl.pallas_call(
         widen_kernel,
         grid=(steps,),
-        in_specs=[spec(value) for value in values],
-        out_specs=[spec(value) for value in values],
+        in_specs=[pl.BlockSpec(vectors.shape, lambda i: (0, 0))]
+        + [spec(value) for value in values],
+        out_specs=[spec(value) for value in values]
+        + [pl.BlockSpec((vectors.shape[1],), lambda i: (0,))] * 4,
         out_shape=[
             jax.ShapeDtypeStruct(value.shape, kind) for value, kind in zip(values, kinds)
-        ],
+        ]
+        + [jax.ShapeDtypeStruct((vectors.shape[1],), jnp.float32)] * 4,
         name="widen",
-    )(*values)
+    )(vectors, *values)
 
 
 def on_device_plain(
@@ -2041,8 +2053,11 @@
     )
     f32 = jnp.float32
     units = w_up.shape[2]
-    output, grad_tokens, grad_gates, grad_qkv, grad_out, grad_up, grad_down = widen(
+    (
+        output, grad_tokens, grad_gates, grad_qkv, grad_out, grad_up, grad_down, *grad_vectors,
+    ) = widen(
         2,
+        grad_vectors,
         (
             output, grad_tokens, grad_gates, grad_qkv, grad_out,
             grad_up.reshape(-1, units), grad_down.reshape(-1, model_width),

time: 264 us -> 257 us (0.973)
  Pallas kernels: 259 us -> 254 us
    pallas_call x1, Pallas kernels: 67.2 us -> 63.1 us  [run_front(): pl.pallas_call(functools.partial(front_kernel, (owners, capacity, pieces)...]
where the time goes in v7:
time: 257 us
  Pallas kernels  254 us (99%)
    pallas_call x1, Pallas kernels, run_back(): pl.pallas_call(functools.partial(back_kernel, (owners, capacity, gates)),...  103 us
    pallas_call x1, Pallas kernels, run_experts(): pl.pallas_call(functools.partial(expert_kernel, dims), out_shape=(jax.Sha...  75.9 us
    pallas_call x1, Pallas kernels, run_front(): pl.pallas_call(functools.partial(front_kernel, (owners, capacity, pieces)...  63.1 us
    pallas_call x1, Pallas kernels, widen(): pl.pallas_call(widen_kernel, grid=(steps,), in_specs=[pl.BlockSpec(vector...  11.7 us

profile of v7, /device:TPU:0, one launch (start us, length us, event | category | flops | bytes accessed | tf_op | source)
XLA Modules:
  0.0 256.8 jit_solution(9310310428904774587)
XLA Ops:
  1.3 1.4 select_select_fusion.small_hbm
  2.7 63.1 %front.1 = (bf16[512,3072]{1,0:T(8,128)(2,1)}, bf16[1024,512]{1,0:T(8,128)(2,1)}, bf16[1024,512]{1,0:T(8,128)(2,1)}, bf16[512,512]{1,0:T(8,128)(2,1)}, bf16[1024...) custom-call(s32[1]{0:T(128)S(6)} %copy.25.prefix_ref, ...), custom_call_target="tpu_custom_call" | custom-call | tf_op jit(solution)/shard_map/front/pallas_call | solution.py:1167
  65.8 75.9 %experts.1 = (bf16[2,256,1024]{2,1,0:T(8,128)(2,1)}, bf16[2,256,1024]{2,1,0:T(8,128)(2,1)}, bf16[8,2,32,1024]{3,2,1,0:T(8,128)(2,1)}, bf16[8,2,32,1024]{3,2,1,0:...) custom-call(bf16[8,2,32,1024]{3,2,1,0:T(8,128)(2,1)} %get-tuple-element.48.send_r, ...), custom_call_target="tpu_custom_call" | custom-call | tf_op jit(solution)/shard_map/experts/pallas_call | solution.py:708
  141.7 103.2 %back.1 = (bf16[512,1024]{1,0:T(8,128)(2,1)}, f32[512,1024]{1,0:T(8,128)}, f32[8,256]{1,0:T(8,128)}, f32[16,256]{1,0:T(8,128)}, bf16[256,3072]{1,0:T(8,128)(2,1)}, /*index=5*/bf16[256,1024]{1,0:T(8,128)(2,1)}) custom-call(bf16[8,2,32,1024]{3,2,1,0:T(8,128)(2,1)} %get-tuple-element.51.home_grad_ref, bf16[512,512]{1,0:T(8,128)(2,1)} %get-tuple-element.52.back_ref, ...), custom_call_target="tpu_custom_call" | custom-call | tf_op jit(solution)/shard_map/back/pallas_call | solution.py:1745
  244.9 11.7 %widen.1 = (bf16[512,1024]{1,0:T(8,128)(2,1)}, f32[512,1024]{1,0:T(8,128)}, f32[16,256]{1,0:T(8,128)}, f32[256,3072]{1,0:T(8,128)}, f32[256,1024]{1,0:T(8,128)},...) custom-call(f32[8,256]{1,0:T(8,128)} %get-tuple-element.66.vectors_r, ...), custom_call_target="tpu_custom_call" | custom-call | tf_op jit(solution)/shard_map/widen/pallas_call | solution.py:1819
  (2 shorter events, 0.0 us)

commit v8 on v7

--- a/solution.py
+++ b/solution.py
@@ -945,14 +945,21 @@
 
 def front_kernel(
     dims,
-    prefix_ref, routes_ref, priority_ref, tokens_ref, cot_ref, small_hbm, router_hbm, qkv_hbm, out_hbm,
+    prefix_ref, routes_ref, priority_ref, tokens_hbm, cot_hbm, small_hbm, router_hbm, qkv_hbm, out_hbm,
     qkv_out, act_out, merged_out, back_out, weight_out, out_full, low_out, high_out, grads_rows,
-    hidden_ref, send_ref, small_out, router_out,
+    hidden_hbm, send_hbm, small_out, router_out,
+    tokens_ref, cot_ref, hidden_ref, send_ref,
     small, weight, out_w, qkv, act, merged, act_two, turned, pick, back, grads_send, low_buf, high_buf,
-    own_sem, disp_send, disp_recv, small_send, small_recv, gat_send, gat_recv, store_sem, prob_sem,
+    own_sem, disp_send, disp_recv, small_send, small_recv, gat_send, gat_recv, store_sem, prob_sem, first_sem,
 ):
     owners, capacity, pieces = dims
     place = Place(owners)
+    firsts = [
+        pltpu.make_async_copy(src, dst, first_sem.at[i])
+        for i, (src, dst) in enumerate(((cot_hbm, cot_ref), (tokens_hbm, tokens_ref)))
+    ]
+    for load in firsts:
+        load.start()
     rows, width = tokens_ref.shape
     shard = qkv_hbm.shape[0]
     gathers = [
@@ -997,6 +1004,7 @@
 
         every(0, width // tile, one)
 
+    firsts[0].wait()
     to_slots(cot_ref, grads_send)
     dispatch = Dispatch(
         place, capacity, grads_send, grads_rows, (own_sem.at[0], disp_send, disp_recv)
@@ -1030,6 +1038,7 @@
             qkv[:, cols] = dot_nn(act[...], weight[:, cols]).astype(jnp.bfloat16)
 
     gathers[0].pass_on(0)
+    firsts[1].wait()
     every(0, rows // band, norm_band)
     turned[0] = act[...].T
     stores = [
@@ -1129,14 +1138,20 @@
 
     bands = rows // band_two
     every(0, bands, middle)
+    results = [
+        pltpu.make_async_copy(src, dst, first_sem.at[2 + i])
+        for i, (src, dst) in enumerate(((hidden_ref, hidden_hbm), (send_ref, send_hbm)))
+    ]
+    results[0].start()
     to_slots(act_two, send_ref)
+    results[1].start()
     for partner in order[1 + bands :]:
         dispatch.relay(partner)
     for i in (pairs - 2, pairs - 1):
         for copy in keep_probs(i):
             copy.wait()
     every(0, owners, dispatch.ready)
-    for store in stores:
+    for store in stores + results:
         store.wait()
     for copy in smalls:
         copy.wait_send()
@@ -1181,9 +1196,13 @@
             out(4, *small.shape),
             out(LANES, width),
         ),
-        in_specs=[pl.BlockSpec(memory_space=pltpu.SMEM)] + [vmem_spec] * 4 + [any_spec] * 4,
-        out_specs=(any_spec,) * 9 + (vmem_spec,) * 4,
+        in_specs=[pl.BlockSpec(memory_space=pltpu.SMEM)] + [vmem_spec] * 2 + [any_spec] * 6,
+        out_specs=(any_spec,) * 11 + (vmem_spec,) * 2,
         scratch_shapes=[
+            vm(rows, width),
+            vm(rows, width),
+            pltpu.VMEM((rows, width), f32),
+            vm(owners, experts, capacity, width),
             vm(4, small.shape[0] + router.shape[0], shard),
             vm(4 * shard, columns),
             vm(4 * shard, width),
@@ -1206,6 +1225,7 @@
             dma((2, 6, pieces, 3)),
             dma((6,)),
             dma((2, 2)),
+            dma((4,)),
         ],
         compiler_params=pltpu.CompilerParams(
             collective_id=0, has_side_effects=True, vmem_limit_bytes=VMEM_LIMIT
@@ -1455,15 +1475,16 @@
 
 def back_kernel(
     dims,
-    home_grad_ref, back_ref, hidden_ref, cot_ref, tokens_ref, vectors_ref, router_ref,
+    home_grad_hbm, back_hbm, hidden_hbm, cot_hbm, tokens_hbm, vectors_ref, router_ref,
     far_hbm, near_hbm, home_hbm, act_hbm, merged_hbm, qkv_hbm, weight_hbm, out_hbm, low_hbm, high_hbm,
-    output_ref, tokens_out, vectors_out, gates_out, qkv_out, out_out,
+    output_hbm, grad_tokens_hbm, vectors_out, gates_out, qkv_out, out_out,
+    home_grad_ref, back_ref, hidden_ref, cot_ref, tokens_ref, output_ref, tokens_out,
     near_sums, far_sums, done_rows, home_out,
     act_t, merged_t, qkv, weight, out_w, low_buf, high_buf, attn, grad_merged, grad_act,
     part_q, got_q, far_q, pair_q, near_q, line_q, done_q,
     part_o, got_o, far_o, pair_o, near_o, line_o, done_o,
     small, small_part, small_got, small_mid, small_far, small_sum, small_all,
-    load_sem, prob_sem, own_sem, early_sem, cross_send, cross_recv, home_send, home_recv, send_q, recv_q, send_o, recv_o,
+    first_sem, load_sem, prob_sem, own_sem, early_sem, cross_send, cross_recv, home_send, home_recv, send_q, recv_q, send_o, recv_o,
     small_send, small_recv, all_send, all_recv, out_sem,
 ):
     owners, capacity, gates = dims
@@ -1488,7 +1509,18 @@
             ),
         )
 
-    for load in loads:
+    firsts = [
+        pltpu.make_async_copy(src, dst, first_sem.at[i])
+        for i, (src, dst) in enumerate(
+            [(home_grad_hbm, home_grad_ref), (back_hbm, back_ref), (hidden_hbm, hidden_ref),
+             (cot_hbm, cot_ref), (tokens_hbm, tokens_ref)]
+        )
+    ]
+    results = [
+        pltpu.make_async_copy(src, dst, first_sem.at[5 + i])
+        for i, (src, dst) in enumerate([(tokens_out, grad_tokens_hbm), (output_ref, output_hbm)])
+    ]
+    for load in firsts[:4] + loads + firsts[4:]:
         load.start()
     for load in load_probs(0):
         load.start()
@@ -1549,6 +1581,8 @@
         small[2:3, :] += jnp.sum(grad * scaled, axis=0, keepdims=True)
         small[3:4, :] += jnp.sum(grad, axis=0, keepdims=True)
 
+    for load in firsts[:4]:
+        load.wait()
     every(0, rows // band, post)
     loads[0].wait()
 
@@ -1571,7 +1605,7 @@
     stages_o, stages_q = reduce_o.stages(), reduce_q.stages()
     for n in range(out_chunks):
         stages_o[0](n)
-    for load in loads[2:]:
+    for load in loads[2:] + firsts[4:]:
         load.wait()
     grad_act[...] = jnp.zeros_like(grad_act)
     pairs = part_q.shape[0]
@@ -1676,7 +1710,11 @@
         def _():
             every(0, half, input_band)
 
-        pl.when(slot == pairs + 1)(lambda: every(half, 2 * half, input_band))
+        @pl.when(slot == pairs + 1)
+        def _():
+            every(half, 2 * half, input_band)
+            results[0].start()
+
         pl.when(slot == pairs + 2)(smalls.swap)
         pl.when(slot == pairs + 3)(smalls.cross)
         pl.when(slot == pairs + 4)(smalls.spread)
@@ -1686,6 +1724,7 @@
             late.arrived(EARLY_CHUNKS, groups, experts)
             every(0, 2 * EARLY_CHUNKS, lambda n: early_rows(n).wait())
             every(0, rows // band, output_band)
+            results[1].start()
 
     every(0, pairs + delays[-1], slot_step)
     smalls.finish()
@@ -1695,6 +1734,8 @@
             copy.wait()
 
     every(0, pairs, stored)
+    for result in results:
+        result.wait()
     for n in range(out_chunks):
         store_o(n).wait()
     late.drain(EARLY_CHUNKS, groups, experts)
@@ -1752,9 +1793,16 @@
             jax.ShapeDtypeStruct((shard, 3 * width), bf16),
             jax.ShapeDtypeStruct((shard, width), bf16),
         ),
-        in_specs=[vmem_spec] * 7 + [any_spec] * 10,
-        out_specs=(vmem_spec,) * 4 + (any_spec,) * 2,
+        in_specs=[any_spec] * 5 + [vmem_spec] * 2 + [any_spec] * 10,
+        out_specs=(any_spec,) * 2 + (vmem_spec,) * 2 + (any_spec,) * 2,
         scratch_shapes=[
+            vm(*home_grad.shape),
+            vm(rows, rows),
+            fm(rows, width),
+            vm(rows, width),
+            vm(rows, width),
+            vm(rows, width),
+            fm(rows, width),
             vm(*near_sums.shape),
             vm(*near_sums.shape),
             vm(*home_grad.shape),
@@ -1780,6 +1828,7 @@
             fm(lead, shard),
             fm(lead, shard),
             fm(owners, lead, shard),
+            dma((7,)),
             dma((6,)),
             dma((2, 2)),
             dma((near_sums.shape[0],)),

time: 257 us -> 255 us (level)
  no operation moved by 1% of the time
where the time goes in v8:
time: 255 us
  Pallas kernels  252 us (99%)
    pallas_call x1, Pallas kernels, run_back(): pl.pallas_call(functools.partial(back_kernel, (owners, capacity, gates)),...  103 us
    pallas_call x1, Pallas kernels, run_experts(): pl.pallas_call(functools.partial(expert_kernel, dims), out_shape=(jax.Sha...  76 us
    pallas_call x1, Pallas kernels, run_front(): pl.pallas_call(functools.partial(front_kernel, (owners, capacity, pieces)...  61.2 us
    pallas_call x1, Pallas kernels, widen(): pl.pallas_call(widen_kernel, grid=(steps,), in_specs=[pl.BlockSpec(vector...  11.7 us

profile of v8, /device:TPU:0, one launch (start us, length us, event | category | flops | bytes accessed | tf_op | source)
XLA Modules:
  0.0 255.1 jit_solution(12732251748372080183)
XLA Ops:
  1.3 1.4 select_select_fusion.small_hbm
  2.7 61.2 %front.1 = (bf16[512,3072]{1,0:T(8,128)(2,1)}, bf16[1024,512]{1,0:T(8,128)(2,1)}, bf16[1024,512]{1,0:T(8,128)(2,1)}, bf16[512,512]{1,0:T(8,128)(2,1)}, bf16[1024...) custom-call(s32[1]{0:T(128)S(6)} %copy.25.prefix_ref, ...), custom_call_target="tpu_custom_call" | custom-call | tf_op jit(solution)/shard_map/front/pallas_call | solution.py:1182
  63.9 76.0 %experts.1 = (bf16[2,256,1024]{2,1,0:T(8,128)(2,1)}, bf16[2,256,1024]{2,1,0:T(8,128)(2,1)}, bf16[8,2,32,1024]{3,2,1,0:T(8,128)(2,1)}, bf16[8,2,32,1024]{3,2,1,0:...) custom-call(bf16[8,2,32,1024]{3,2,1,0:T(8,128)(2,1)} %get-tuple-element.48.send_r, ...), custom_call_target="tpu_custom_call" | custom-call | tf_op jit(solution)/shard_map/experts/pallas_call | solution.py:708
  139.9 103.4 %back.1 = (bf16[512,1024]{1,0:T(8,128)(2,1)}, f32[512,1024]{1,0:T(8,128)}, f32[8,256]{1,0:T(8,128)}, f32[16,256]{1,0:T(8,128)}, bf16[256,3072]{1,0:T(8,128)(2,1)}, /*index=5*/bf16[256,1024]{1,0:T(8,128)(2,1)}) custom-call(bf16[8,2,32,1024]{3,2,1,0:T(8,128)(2,1)} %get-tuple-element.51.home_grad_hbm, bf16[512,512]{1,0:T(8,128)(2,1)} %get-tuple-element.52.back_hbm, ...), custom_call_target="tpu_custom_call" | custom-call | tf_op jit(solution)/shard_map/back/pallas_call | solution.py:1786
  243.2 11.7 %widen.1 = (bf16[512,1024]{1,0:T(8,128)(2,1)}, f32[512,1024]{1,0:T(8,128)}, f32[16,256]{1,0:T(8,128)}, f32[256,3072]{1,0:T(8,128)}, f32[256,1024]{1,0:T(8,128)},...) custom-call(f32[8,256]{1,0:T(8,128)} %get-tuple-element.66.vectors_r, ...), custom_call_target="tpu_custom_call" | custom-call | tf_op jit(solution)/shard_map/widen/pallas_call | solution.py:1868
  (2 shorter events, 0.0 us)

commit v9 on v8

--- a/solution.py
+++ b/solution.py
@@ -945,10 +945,11 @@
 
 def front_kernel(
     dims,
-    prefix_ref, routes_ref, priority_ref, tokens_hbm, cot_hbm, small_hbm, router_hbm, qkv_hbm, out_hbm,
+    prefix_ref, routes_ref, priority_ref, gain_one_ref, shift_one_ref, gain_two_ref, shift_two_ref,
+    tokens_hbm, cot_hbm, router_hbm, qkv_hbm, out_hbm,
     qkv_out, act_out, merged_out, back_out, weight_out, out_full, low_out, high_out, grads_rows,
     hidden_hbm, send_hbm, small_out, router_out,
-    tokens_ref, cot_ref, hidden_ref, send_ref,
+    small_own, tokens_ref, cot_ref, hidden_ref, send_ref,
     small, weight, out_w, qkv, act, merged, act_two, turned, pick, back, grads_send, low_buf, high_buf,
     own_sem, disp_send, disp_recv, small_send, small_recv, gat_send, gat_recv, store_sem, prob_sem, first_sem,
 ):
@@ -960,6 +961,9 @@
     ]
     for load in firsts:
         load.start()
+    small_own[...] = jnp.zeros_like(small_own)
+    for i, vector_ref in enumerate((gain_one_ref, shift_one_ref, gain_two_ref, shift_two_ref)):
+        small_own[i, :] = vector_ref[...]
     rows, width = tokens_ref.shape
     shard = qkv_hbm.shape[0]
     gathers = [
@@ -968,9 +972,9 @@
     ]
     for gather in gathers:
         gather.start_own()
-    vectors, gates = small_hbm.shape[0], router_hbm.shape[0]
+    vectors, gates = small_own.shape[0], router_hbm.shape[0]
     small_parts = [
-        (small_hbm, small.at[place.w, pl.ds(0, vectors)]),
+        (small_own, small.at[place.w, pl.ds(0, vectors)]),
         (router_hbm, small.at[place.w, pl.ds(vectors, gates)]),
     ]
     own_smalls = [
@@ -1161,7 +1165,7 @@
 
 
 def run_front(
-    owners, experts, capacity, prefix, routes, priority, tokens, cotangent, small, router, w_qkv, w_out
+    owners, experts, capacity, prefix, routes, priority, vectors, tokens, cotangent, router, w_qkv, w_out
 ):
     rows, width = tokens.shape
     shard, columns = w_qkv.shape
@@ -1193,17 +1197,18 @@
             out(experts, owners * 4 * capacity, width),
             jax.ShapeDtypeStruct((rows, width), f32),
             out(owners, experts, capacity, width),
-            out(4, *small.shape),
+            out(4, 16, shard),
             out(LANES, width),
         ),
-        in_specs=[pl.BlockSpec(memory_space=pltpu.SMEM)] + [vmem_spec] * 2 + [any_spec] * 6,
+        in_specs=[pl.BlockSpec(memory_space=pltpu.SMEM)] + [vmem_spec] * 6 + [any_spec] * 5,
         out_specs=(any_spec,) * 11 + (vmem_spec,) * 2,
         scratch_shapes=[
+            vm(16, shard),
             vm(rows, width),
             vm(rows, width),
             pltpu.VMEM((rows, width), f32),
             vm(owners, experts, capacity, width),
-            vm(4, small.shape[0] + router.shape[0], shard),
+            vm(4, 16 + router.shape[0], shard),
             vm(4 * shard, columns),
             vm(4 * shard, width),
             vm(rows, columns),
@@ -1231,7 +1236,7 @@
             collective_id=0, has_side_effects=True, vmem_limit_bytes=VMEM_LIMIT
         ),
         name="front",
-    )(prefix, routes, priority, tokens, cotangent, small, router, w_qkv, w_out)
+    )(prefix, routes, priority, *vectors, tokens, cotangent, router, w_qkv, w_out)
 
 
 class Reduce:
@@ -2082,16 +2087,13 @@
     capacity = row_count // expert_count
     owners = lax.axis_size("expert")
     experts = w_up.shape[0]
-    which = lax.broadcasted_iota(jnp.int32, (16, norm1_gain.shape[0]), 0)
-    small = jnp.zeros(which.shape, jnp.bfloat16)
-    for i, vector in enumerate((norm1_gain, norm1_shift, norm2_gain, norm2_shift)):
-        small = jnp.where(which == i, vector[None], small)
     (
         qkv, act_t, merged_t, back, weight, out_full, low, high, grad_rows, hidden, send_rows,
         vectors, router,
     ) = run_front(
-        owners, experts, capacity, prefix, routes.reshape(1, row_count), priority, tokens,
-        cotangent, small, w_router.T, w_qkv, w_out,
+        owners, experts, capacity, prefix, routes.reshape(1, row_count), priority,
+        (norm1_gain, norm1_shift, norm2_gain, norm2_shift), tokens, cotangent, w_router.T, w_qkv,
+        w_out,
     )
     far_sums, near_sums, home_out, home_grad, grad_up, grad_down, grad_router = run_experts(
         owners, capacity, expert_count, send_rows, grad_rows, w_up, w_down, router

time: 255 us -> 254 us (level)
  no operation moved by 1% of the time
where the time goes in v9:
time: 254 us; the launch traced here: 253 us
  Pallas kernels  252 us (99%)
    pallas_call x1, Pallas kernels, run_back(): pl.pallas_call(functools.partial(back_kernel, (owners, capacity, gates)),...  103 us
    pallas_call x1, Pallas kernels, run_experts(): pl.pallas_call(functools.partial(expert_kernel, dims), out_shape=(jax.Sha...  76.5 us
    pallas_call x1, Pallas kernels, run_front(): pl.pallas_call(functools.partial(front_kernel, (owners, capacity, pieces)...  60.7 us
    pallas_call x1, Pallas kernels, widen(): pl.pallas_call(widen_kernel, grid=(steps,), in_specs=[pl.BlockSpec(vector...  11.7 us

profile of v9, /device:TPU:0, one launch (start us, length us, event | category | flops | bytes accessed | tf_op | source)
XLA Modules:
  0.0 253.5 jit_solution(2308927682974967767)
XLA Ops:
  1.3 60.7 %front.1 = (bf16[512,3072]{1,0:T(8,128)(2,1)}, bf16[1024,512]{1,0:T(8,128)(2,1)}, bf16[1024,512]{1,0:T(8,128)(2,1)}, bf16[512,512]{1,0:T(8,128)(2,1)}, bf16[1024...) custom-call(s32[1]{0:T(128)S(6)} %copy.25.prefix_ref, ...), custom_call_target="tpu_custom_call" | custom-call | tf_op jit(solution)/shard_map/front/pallas_call | solution.py:1186
  62.0 76.5 %experts.1 = (bf16[2,256,1024]{2,1,0:T(8,128)(2,1)}, bf16[2,256,1024]{2,1,0:T(8,128)(2,1)}, bf16[8,2,32,1024]{3,2,1,0:T(8,128)(2,1)}, bf16[8,2,32,1024]{3,2,1,0:...) custom-call(bf16[8,2,32,1024]{3,2,1,0:T(8,128)(2,1)} %get-tuple-element.48.send_r, ...), custom_call_target="tpu_custom_call" | custom-call | tf_op jit(solution)/shard_map/experts/pallas_call | solution.py:708
  138.5 103.1 %back.1 = (bf16[512,1024]{1,0:T(8,128)(2,1)}, f32[512,1024]{1,0:T(8,128)}, f32[8,256]{1,0:T(8,128)}, f32[16,256]{1,0:T(8,128)}, bf16[256,3072]{1,0:T(8,128)(2,1)}, /*index=5*/bf16[256,1024]{1,0:T(8,128)(2,1)}) custom-call(bf16[8,2,32,1024]{3,2,1,0:T(8,128)(2,1)} %get-tuple-element.51.home_grad_hbm, bf16[512,512]{1,0:T(8,128)(2,1)} %get-tuple-element.52.back_hbm, ...), custom_call_target="tpu_custom_call" | custom-call | tf_op jit(solution)/shard_map/back/pallas_call | solution.py:1791
  241.6 11.7 %widen.1 = (bf16[512,1024]{1,0:T(8,128)(2,1)}, f32[512,1024]{1,0:T(8,128)}, f32[16,256]{1,0:T(8,128)}, f32[256,3072]{1,0:T(8,128)}, f32[256,1024]{1,0:T(8,128)},...) custom-call(f32[8,256]{1,0:T(8,128)} %get-tuple-element.66.vectors_r, ...), custom_call_target="tpu_custom_call" | custom-call | tf_op jit(solution)/shard_map/widen/pallas_call | solution.py:1873

commit v10 on v9

--- a/solution.py
+++ b/solution.py
@@ -654,11 +654,11 @@
 
     every(0, len(turns), step)
     ret_grad.cross(*turns[-2])
+    ret_grad.cross(*turns[-1])
+    ret_grad.finish(*turns[-4])
     ret_out.split(*turns[-2])
-    ret_grad.finish(*turns[-4])
+    ret_out.split(*turns[-1])
     weight_grads(0, 0, 1)
-    ret_grad.cross(*turns[-1])
-    ret_out.split(*turns[-1])
     sums = [
         pltpu.make_async_copy(src, dst, load_sem.at[4 + i])
         for i, (src, dst) in enumerate(((mid_out, far_sums), (keep_out, near_sums)))
@@ -1683,7 +1683,7 @@
         )
 
     delays = (1, 3, 4, 5, 6, 7, 8, 9)
-    turns_o = (-1, 3, 5, 6, 7, 8, 9, 10)
+    turns_o = (-1, 3, 6, 7, 8, 9, 10, 11)
     last = len(delays) - 1
     half = rows // band // 2
 

time: 254 us -> 255 us (level)
  no operation moved by 1% of the time
where the time goes in v10:
time: 255 us
  Pallas kernels  254 us (100%)
    pallas_call x1, Pallas kernels, run_back(): pl.pallas_call(functools.partial(back_kernel, (owners, capacity, gates)),...  105 us
    pallas_call x1, Pallas kernels, run_experts(): pl.pallas_call(functools.partial(expert_kernel, dims), out_shape=(jax.Sha...  76.5 us
    pallas_call x1, Pallas kernels, run_front(): pl.pallas_call(functools.partial(front_kernel, (owners, capacity, pieces)...  60.7 us
    pallas_call x1, Pallas kernels, widen(): pl.pallas_call(widen_kernel, grid=(steps,), in_specs=[pl.BlockSpec(vector...  11.7 us

profile of v10, /device:TPU:0, one launch (start us, length us, event | category | flops | bytes accessed | tf_op | source)
XLA Modules:
  0.0 255.1 jit_solution(3720877739196880139)
XLA Ops:
  1.3 60.7 %front.1 = (bf16[512,3072]{1,0:T(8,128)(2,1)}, bf16[1024,512]{1,0:T(8,128)(2,1)}, bf16[1024,512]{1,0:T(8,128)(2,1)}, bf16[512,512]{1,0:T(8,128)(2,1)}, bf16[1024...) custom-call(s32[1]{0:T(128)S(6)} %copy.25.prefix_ref, ...), custom_call_target="tpu_custom_call" | custom-call | tf_op jit(solution)/shard_map/front/pallas_call | solution.py:1186
  62.0 76.5 %experts.1 = (bf16[2,256,1024]{2,1,0:T(8,128)(2,1)}, bf16[2,256,1024]{2,1,0:T(8,128)(2,1)}, bf16[8,2,32,1024]{3,2,1,0:T(8,128)(2,1)}, bf16[8,2,32,1024]{3,2,1,0:...) custom-call(bf16[8,2,32,1024]{3,2,1,0:T(8,128)(2,1)} %get-tuple-element.48.send_r, ...), custom_call_target="tpu_custom_call" | custom-call | tf_op jit(solution)/shard_map/experts/pallas_call | solution.py:708
  138.5 104.7 %back.1 = (bf16[512,1024]{1,0:T(8,128)(2,1)}, f32[512,1024]{1,0:T(8,128)}, f32[8,256]{1,0:T(8,128)}, f32[16,256]{1,0:T(8,128)}, bf16[256,3072]{1,0:T(8,128)(2,1)}, /*index=5*/bf16[256,1024]{1,0:T(8,128)(2,1)}) custom-call(bf16[8,2,32,1024]{3,2,1,0:T(8,128)(2,1)} %get-tuple-element.51.home_grad_hbm, bf16[512,512]{1,0:T(8,128)(2,1)} %get-tuple-element.52.back_hbm, ...), custom_call_target="tpu_custom_call" | custom-call | tf_op jit(solution)/shard_map/back/pallas_call | solution.py:1791
  243.2 11.7 %widen.1 = (bf16[512,1024]{1,0:T(8,128)(2,1)}, f32[512,1024]{1,0:T(8,128)}, f32[16,256]{1,0:T(8,128)}, f32[256,3072]{1,0:T(8,128)}, f32[256,1024]{1,0:T(8,128)},...) custom-call(f32[8,256]{1,0:T(8,128)} %get-tuple-element.66.vectors_r, ...), custom_call_target="tpu_custom_call" | custom-call | tf_op jit(solution)/shard_map/widen/pallas_call | solution.py:1873

commit v11 on v9

--- a/solution.py
+++ b/solution.py
@@ -15,7 +15,7 @@
 epsilon = 1e-05
 VMEM_LIMIT = 66_000_000
 TILE = 1024
-EARLY_CHUNKS = 1
+EARLY_CHUNKS = 2
 
 
 def normalize(values, gain_vec, shift_vec):
@@ -1683,7 +1683,7 @@
         )
 
     delays = (1, 3, 4, 5, 6, 7, 8, 9)
-    turns_o = (-1, 3, 5, 6, 7, 8, 9, 10)
+    turns_o = (-1, 3, 6, 7, 8, 9, 10, 11)
     last = len(delays) - 1
     half = rows // band // 2
 

time: 254 us -> 257 us (1.012)
  Pallas kernels: 252 us -> 256 us
    pallas_call x1, Pallas kernels: 76.5 us -> 79.8 us  [run_experts(): pl.pallas_call(functools.partial(expert_kernel, dims), out_shape=(jax.Sha...]
where the time goes in v11:
time: 257 us
  Pallas kernels  256 us (100%)
    pallas_call x1, Pallas kernels, run_back(): pl.pallas_call(functools.partial(back_kernel, (owners, capacity, gates)),...  103 us
    pallas_call x1, Pallas kernels, run_experts(): pl.pallas_call(functools.partial(expert_kernel, dims), out_shape=(jax.Sha...  79.8 us
    pallas_call x1, Pallas kernels, run_front(): pl.pallas_call(functools.partial(front_kernel, (owners, capacity, pieces)...  60.7 us
    pallas_call x1, Pallas kernels, widen(): pl.pallas_call(widen_kernel, grid=(steps,), in_specs=[pl.BlockSpec(vector...  11.7 us

profile of v11, /device:TPU:0, one launch (start us, length us, event | category | flops | bytes accessed | tf_op | source)
XLA Modules:
  0.0 257.0 jit_solution(7779805359098315140)
XLA Ops:
  1.3 60.7 %front.1 = (bf16[512,3072]{1,0:T(8,128)(2,1)}, bf16[1024,512]{1,0:T(8,128)(2,1)}, bf16[1024,512]{1,0:T(8,128)(2,1)}, bf16[512,512]{1,0:T(8,128)(2,1)}, bf16[1024...) custom-call(s32[1]{0:T(128)S(6)} %copy.25.prefix_ref, ...), custom_call_target="tpu_custom_call" | custom-call | tf_op jit(solution)/shard_map/front/pallas_call | solution.py:1186
  62.0 79.8 %experts.1 = (bf16[2,256,1024]{2,1,0:T(8,128)(2,1)}, bf16[2,256,1024]{2,1,0:T(8,128)(2,1)}, bf16[8,2,32,1024]{3,2,1,0:T(8,128)(2,1)}, bf16[8,2,32,1024]{3,2,1,0:...) custom-call(bf16[8,2,32,1024]{3,2,1,0:T(8,128)(2,1)} %get-tuple-element.48.send_r, ...), custom_call_target="tpu_custom_call" | custom-call | tf_op jit(solution)/shard_map/experts/pallas_call | solution.py:708
  141.8 103.3 %back.1 = (bf16[512,1024]{1,0:T(8,128)(2,1)}, f32[512,1024]{1,0:T(8,128)}, f32[8,256]{1,0:T(8,128)}, f32[16,256]{1,0:T(8,128)}, bf16[256,3072]{1,0:T(8,128)(2,1)}, /*index=5*/bf16[256,1024]{1,0:T(8,128)(2,1)}) custom-call(bf16[8,2,32,1024]{3,2,1,0:T(8,128)(2,1)} %get-tuple-element.51.home_grad_hbm, bf16[512,512]{1,0:T(8,128)(2,1)} %get-tuple-element.52.back_hbm, ...), custom_call_target="tpu_custom_call" | custom-call | tf_op jit(solution)/shard_map/back/pallas_call | solution.py:1791
  245.2 11.7 %widen.1 = (bf16[512,1024]{1,0:T(8,128)(2,1)}, f32[512,1024]{1,0:T(8,128)}, f32[16,256]{1,0:T(8,128)}, f32[256,3072]{1,0:T(8,128)}, f32[256,1024]{1,0:T(8,128)},...) custom-call(f32[8,256]{1,0:T(8,128)} %get-tuple-element.66.vectors_r, ...), custom_call_target="tpu_custom_call" | custom-call | tf_op jit(solution)/shard_map/widen/pallas_call | solution.py:1873
